TPU v7x, 32 devices: a whole 2x2x4 slice. The times are simulated.
32 devices in a mesh: grp: 2 (over x), slab: 16 (over z, y, core).
Axes of the slice: x: 2, y: 2, z: 4, core: 2. Of those that a mesh axis runs over, the one named last changes fastest.
Arguments:
- image: float32 [2, 384, 192, 256], P(None, ('grp', 'slab')), parts along dimension 1, may hold values from -6 to 6
- adjoint_data: bfloat16 [2, 384, 192, 256], P(None, ('grp', 'slab')), parts along dimension 1, may hold values from -6 to 6
- coil_maps: bfloat16 [8, 2, 384, 192, 256], P(None, None, ('grp', 'slab')), parts along dimension 2, may hold values from -2.5 to 2.5
- masks: int32 [1, 384, 192], P(None, 'grp'), parts along dimension 1, may hold values 0 or 1
- sources: int32 [1, 1152, 2], P(None, ('grp', 'slab')), parts along dimension 1, may hold values from 0 to 575, as said below
- weights: bfloat16 [1, 1152, 8192], P(None, ('grp', 'slab')), parts along dimension 1, may hold values from -0.5 to 0.5
Outputs:
- updated: float32 [2, 384, 192, 256], P(None, ('grp', 'slab')), parts along dimension 1
There are 2 independent parts, one for each index of `grp`. A program takes and returns all parts, laid end to end along the dimension named above; each array names one. Nothing has to cross between parts.
Inputs may be any that keep to these rules, and one draw needn't show every extreme that they name: sources[s, t, j] is a block number (plane * 3 + y block); its plane lies within 24 planes of target block t's plane, and its y block within one of t's y block.
All inputs are finite; a program needn't handle non-finite values.
Results may differ from a plain program's by a relative error of at most 0.005.
Values may be sent and summed in bfloat16 or wider, within the bound.
No kernel may reach another device: no remote copies, remote signals or barrier semaphores. Data moves between devices by JAX's collectives and lax.ppermute only.
A program may use at most 256 MiB of HBM per device.

v0:
```python
import math

import jax
import jax.numpy as jnp
from jax import lax
from jax.sharding import PartitionSpec as P

NX = 192
NY = 192
NZ = 256
BLK = 64
REACH = 2


def shifted(shard, axis, by):
    count = lax.axis_size(axis)
    pairs = [(i, i + by) for i in range(count) if 0 <= i + by < count]
    return lax.ppermute(shard, axis, pairs)


def dft_table(length, direction):
    positions = jnp.arange(length, dtype=jnp.int32)
    product = positions[:, None] * positions[None, :] % length
    phases = product.astype(jnp.float32) * (2.0 * math.pi / length)
    factor = 1.0 / math.sqrt(length)
    cosine = jnp.cos(phases) * factor
    sine_part = jnp.sin(phases) * (direction * factor)
    upper_rows = jnp.stack([cosine, -sine_part], axis=1)
    lower_rows = jnp.stack([sine_part, cosine], axis=1)
    return jnp.stack([upper_rows, lower_rows], axis=0).astype(jnp.bfloat16)


def column_y(volume, matrix):
    return jnp.einsum("zcpxj,qkpj->zcqxk", volume, matrix, preferred_element_type=jnp.float32)


def column_x(volume, matrix):
    return jnp.einsum("zcpjy,qkpj->zcqky", volume, matrix, preferred_element_type=jnp.float32)


def expand_columns(sensitivity, warped):
    real_map = sensitivity[:, :, 0].astype(jnp.float32)
    imag_map = sensitivity[:, :, 1].astype(jnp.float32)
    real_warp = warped[:, 0][:, None]
    imag_warp = warped[:, 1][:, None]
    real_part = real_map * real_warp - imag_map * imag_warp
    imag_part = real_map * imag_warp + imag_map * real_warp
    return jnp.stack([real_part, imag_part], axis=2).astype(jnp.bfloat16)


def combine_columns(sensitivity, returned):
    real_map = sensitivity[:, :, 0].astype(jnp.float32)
    imag_map = sensitivity[:, :, 1].astype(jnp.float32)
    real_part = jnp.sum(real_map * returned[:, :, 0] + imag_map * returned[:, :, 1], axis=1)
    imag_part = jnp.sum(real_map * returned[:, :, 1] - imag_map * returned[:, :, 0], axis=1)
    return jnp.stack([real_part, imag_part], axis=1)


def per_device(image, adjoint_data, coil_maps, masks, sources, weights):
    slab_rank = lax.axis_index("slab")
    planes = image.shape[1]
    y_blocks = NY // BLK
    local_blocks = planes * y_blocks
    reach_slots = 2 * REACH + 1
    rounded = image.astype(jnp.bfloat16)
    forward_y = dft_table(NY, -1.0)
    inverse_y = dft_table(NY, 1.0)
    forward_x = dft_table(NX, -1.0)
    inverse_x = dft_table(NX, 1.0)
    nearby_list = []
    for offset in range(-REACH, REACH + 1):
        if offset == 0:
            nearby_list.append(rounded)
        else:
            nearby_list.append(shifted(rounded, "slab", -offset))
    nearby = jnp.stack(nearby_list, axis=1).reshape(2, reach_slots * local_blocks, BLK, NZ)
    maps_leading = jnp.transpose(coil_maps, (4, 0, 1, 2, 3))
    maps_columns = lax.all_to_all(maps_leading, "slab", split_axis=0, concat_axis=3, tiled=True)
    gradient = jnp.zeros((2, local_blocks, BLK, NZ), jnp.float32)
    link_ids = sources[0]
    matrices = weights[0].reshape(local_blocks, 2, BLK, BLK)
    positions = link_ids - (slab_rank - REACH) * local_blocks
    warped = jnp.zeros((2, local_blocks, BLK, NZ), jnp.float32)
    for member in range(2):
        picked = jnp.take(nearby, positions[:, member], axis=1)
        warped = warped + jnp.einsum(
            "tij,rtjz->rtiz", matrices[:, member], picked, preferred_element_type=jnp.float32
        )
    warped = warped.reshape(2, planes, NY, NZ)
    sampled = masks[0].astype(jnp.float32)
    warped_leading = jnp.transpose(warped, (3, 0, 1, 2))
    warped_columns = lax.all_to_all(warped_leading, "slab", split_axis=0, concat_axis=2, tiled=True)
    spectra = column_y(expand_columns(maps_columns, warped_columns), forward_y).astype(jnp.bfloat16)
    middle = (column_x(spectra, forward_x) * sampled[None, None, None, :, :]).astype(jnp.bfloat16)
    restored = column_x(middle, inverse_x).astype(jnp.bfloat16)
    combined_columns = combine_columns(maps_columns, column_y(restored, inverse_y)).astype(
        jnp.bfloat16
    )
    back_leading = lax.all_to_all(combined_columns, "slab", split_axis=2, concat_axis=0, tiled=True)
    grad_image = jnp.transpose(back_leading, (1, 2, 3, 0))
    grad_blocks = grad_image.reshape(2, local_blocks, BLK, NZ)
    spread = jnp.zeros((2, reach_slots * local_blocks, BLK, NZ), jnp.float32)
    for member in range(2):
        product = jnp.einsum(
            "tij,rtiz->rtjz", matrices[:, member], grad_blocks, preferred_element_type=jnp.float32
        )
        spread = spread.at[:, positions[:, member]].add(product)
    spread = spread.reshape(2, reach_slots, local_blocks, BLK, NZ)
    for offset in range(-REACH, REACH + 1):
        portion = spread[:, offset + REACH]
        if offset == 0:
            gradient = gradient + portion
        else:
            gradient = gradient + shifted(portion, "slab", offset)
    gradient = gradient.reshape(2, planes, NY, NZ)
    return image - 0.5 * (gradient - adjoint_data.astype(jnp.float32))


def solution(mesh):
    return jax.shard_map(
        per_device,
        mesh=mesh,
        in_specs=(
            P(None, ("grp", "slab"), None, None),
            P(None, ("grp", "slab"), None, None),
            P(None, None, ("grp", "slab"), None, None),
            P(None, "grp", None),
            P(None, ("grp", "slab"), None),
            P(None, ("grp", "slab"), None),
        ),
        out_specs=P(None, ("grp", "slab"), None, None),
        check_vma=False,
    )
```

profile of v0, /device:TPU:13, one launch (start us, length us, event | category | flops | bytes accessed | tf_op | source)
XLA Modules:
  0.0 1515.4 jit_solution(13383456892984787065)
XLA Ops:
  0.0 2.7 convert_element_type.99
  2.7 3.1 collective-permute-start
  5.8 4.0 collective-permute-start.1
  11.8 2.1 collective-permute-start.3
  13.9 2.2 reshape_squeeze.3
  16.8 115.8 %collective-permute-done = bf16[2,12,192,256]{3,2,1,0:T(8,128)(2,1)} collective-permute-done((bf16[2,12,192,256]{3,2,1,0:T(8,128)(2,1)S(1)}, bf16[2,12,192,256]{3,2,1,0:T(8,128)(2,1)}, u32[]{:S(2)}, u32[]{:S(2)}) %collective-permute-start) | collective-permute-done | bytes 2359328 | tf_op jit(solution)/shard_map/ppermute | solution.py:18
  132.6 3.3 bitcast_dynamic-update-slice_fusion.3
  135.9 3.4 bitcast_dynamic-update-slice_fusion.2
  141.1 3.3 bitcast_dynamic-update-slice_fusion
  144.5 3.3 bitcast_dynamic-update-slice_fusion.4
  147.8 6.6 gather_fusion.1
  154.4 5.0 gather_fusion
  159.5 2.5 fusion.35
  162.8 2.8 copy.77
  165.6 10.1 copy.78
  175.7 28.4 %all-to-all-start.1 = ((f32[256,2,12,192]{3,1,2,0:T(2,128)}), f32[256,2,12,192]{3,1,2,0:T(2,128)}, u32[]{:S(2)}, u32[]{:S(2)}) async-start(f32[256,2,12,192]{3,1,2,0:T(2,128)} %copy.78), calls=%async_computation.1 | async-start | bytes 12582912 | tf_op jit(solution)/shard_map/all_to_all | solution.py:92
  204.1 34.1 %copy.68 = bf16[8,2,12,192,256]{3,0,2,1,4:T(8,128)(2,1)} copy(bf16[8,2,12,192,256]{4,3,2,1,0:T(8,128)(2,1)} %param.10) | data formatting | bytes 37748736 | tf_op args[2]
  238.1 103.4 %all-to-all-done.1 = f32[256,2,12,192]{3,1,2,0:T(2,128)} async-done(((f32[256,2,12,192]{3,1,2,0:T(2,128)}), f32[256,2,12,192]{3,1,2,0:T(2,128)}, u32[]{:S(2)}, u32[]{:S(2)}) %all-to-all-start.1) | async-done | bytes 4718624 | tf_op jit(solution)/shard_map/all_to_all | solution.py:92
  341.5 5.8 all-to-all-start
  351.2 4.8 copy.79
  359.6 3.5 copy.83
  363.1 525.6 %all-to-all-done = bf16[256,8,2,12,192]{4,1,3,2,0:T(8,128)(2,1)} async-done(((bf16[256,8,2,12,192]{4,1,3,2,0:T(8,128)(2,1)}), bf16[256,8,2,12,192]{4,1,3,2,0:T(8,128)(2,1)}, u32[]{:S(2)}, u32[]{:S(2)}) %all-to-all-start) | async-done | bytes 18874400 | tf_op jit(solution)/shard_map/all_to_all | solution.py:78
  888.7 21.2 %copy.69 = bf16[16,8,2,16,12,192]{5,1,4,3,2,0:T(8,128)(2,1)} copy(bf16[16,8,2,16,12,192]{5,1,4,2,0,3:T(8,128)(2,1)} %bitcast.4) | data formatting | bytes 37748736 | tf_op jit(solution)/shard_map/all_to_all | solution.py:78
  909.9 9.8 fusion.77
  919.7 15.8 %fusion.2 = (bf16[16,8,1,192,192]{4,3,2,1,0:T(8,128)(2,1)}, bf16[16,8,1,192,192]{4,3,2,1,0:T(8,128)(2,1)}) fusion(f32[16,192,192]{2,1,0:T(8,128)S(1)} %copy-done.2, f32[16,192,192]{2,1,0:T(8,128)S(1)} %copy.81, bf16[16,8,1,192,192]{4,1,3,2,0:T(8,128)(2,1)S(1)} %get-tuple-element.15, bf16[16,8,1,192,192]{4,1,3,2,0:T(8,128)(2,1)S(1)} %get-tuple-element.14), kind=kLoop, calls=%fused_computation.17 | loop fusion | flops 47185920 | bytes 42467328 | tf_op jit(solution)/shard_map/convert.4
  935.5 22.6 %fusion.16 = bf16[2,192,16,8,192,1]{4,1,5,3,2,0:T(8,128)(2,1)} fusion(bf16[16,8,1,192,192]{4,3,2,1,0:T(8,128)(2,1)} %get-tuple-element.13, bf16[16,8,1,192,192]{4,3,2,1,0:T(8,128)(2,1)} %get-tuple-element.12, bf16[1,192,2,192]{3,1,2,0:T(8,128)(2,1)S(1)} %get-tuple-element.23, bf16[1,192,2,192]{3,1,2,0:T(8,128)(2,1)S(1)} %get-tuple-element.24), kind=kOutput, calls=%fused_computation.30 | convolution fusion | flops 7286095872 | bytes 38043648 | tf_op jit(solution)/shard_map/zcpxj,qkpj->zcqxk/dot_general | solution.py:34
  958.2 22.4 %fusion.15 = bf16[16,8,2,192,192,1]{4,3,1,0,2,5:T(8,128)(2,1)} fusion(f32[192,192]{1,0:T(8,128)S(1)} %copy-done.11, bf16[2,192,16,8,192,1]{4,1,5,3,2,0:T(8,128)(2,1)} %fusion.16, bf16[1,192,2,192]{3,1,2,0:T(8,128)(2,1)S(1)} %get-tuple-element.23, bf16[1,192,2,192]{3,1,2,0:T(8,128)(2,1)S(1)} %get-tuple-element.24), kind=kOutput, calls=%fused_computation.28 | convolution fusion | flops 7267221504 | bytes 38191104 | tf_op jit(solution)/shard_map/zcpjy,qkpj->zcqky/dot_general | solution.py:38
  980.6 34.7 %fusion.21 = f32[16,8,2,192,192]{4,3,2,1,0:T(8,128)} fusion(bf16[16,8,2,192,192,1]{4,3,1,0,2,5:T(8,128)(2,1)} %fusion.15, bf16[1,192,2,192]{3,1,2,0:T(8,128)(2,1)S(1)} %copy-done.9, bf16[1,192,2,192]{3,1,2,0:T(8,128)(2,1)S(1)} %copy-done.8), kind=kOutput, calls=%fused_computation.35 | convolution fusion | flops 14506131456 | bytes 56918016 | tf_op jit(solution)/shard_map/zcpxj,qkpj->zcqxk/dot_general | solution.py:34
  1015.3 26.2 %fusion.6 = (bf16[16,192,192]{2,1,0:T(8,128)(2,1)S(1)}, bf16[16,192,192]{2,1,0:T(8,128)(2,1)S(1)}) fusion(f32[16,8,2,192,192]{4,3,2,1,0:T(8,128)} %fusion.21, bf16[16,8,1,192,192]{4,1,3,2,0:T(8,128)(2,1)} %copy-done.1, bf16[16,8,1,192,192]{4,1,3,2,0:T(8,128)(2,1)} %copy-done), kind=kLoop, calls=%fused_computation.21 | loop fusion | flops 46006272 | bytes 58982400 | tf_op jit(solution)/shard_map/reduce_sum | solution.py:54
  1045.0 2.5 pad_maximum_fusion
  1047.5 3.9 copy.89
  1051.4 4.9 all-to-all-start.2
  1056.4 69.9 %all-to-all-done.2 = bf16[16,2,192,192]{3,0,1,2:T(8,128)(2,1)S(1)} async-done(((bf16[16,2,192,192]{3,0,1,2:T(8,128)(2,1)}), bf16[16,2,192,192]{3,0,1,2:T(8,128)(2,1)S(1)}, u32[]{:S(2)}, u32[]{:S(2)}) %all-to-all-start.2) | async-done | bytes 2359328 | tf_op jit(solution)/shard_map/all_to_all | solution.py:99
  1128.3 3.3 copy.92
  1131.6 3.0 convolution_bitcast_fusion.1
  1134.6 3.0 convolution_bitcast_fusion
  1137.6 10.8 broadcast_in_dim.8
  1148.4 14.9 scatter_fusion
  1163.3 14.8 scatter_fusion.1
  1178.1 7.7 slice_bitcast_fusion.3
  1189.6 4.5 collective-permute-start.6
  1194.2 3.5 collective-permute-start.7
  1197.7 243.3 %collective-permute-done.4 = f32[2,36,64,256]{3,2,1,0:T(8,128)S(1)} collective-permute-done((f32[2,36,64,256]{3,2,1,0:T(8,128)S(1)}, f32[2,36,64,256]{3,2,1,0:T(8,128)S(1)}, u32[]{:S(2)}, u32[]{:S(2)}) %collective-permute-start.4) | collective-permute-done | bytes 4718624 | tf_op jit(solution)/shard_map/ppermute | solution.py:18
  1441.0 2.1 copy-done.5
  1444.6 2.2 copy-done.7
  1446.8 47.4 %collective-permute-done.7 = f32[2,36,64,256]{3,2,1,0:T(8,128)} collective-permute-done((f32[2,36,64,256]{3,2,1,0:T(8,128)S(1)}, f32[2,36,64,256]{3,2,1,0:T(8,128)}, u32[]{:S(2)}, u32[]{:S(2)}) %collective-permute-start.7) | collective-permute-done | bytes 4718624 | tf_op jit(solution)/shard_map/ppermute | solution.py:18
  1494.2 13.2 fusion.32
  1507.4 7.8 fusion.34
  (58 shorter events, 23.7 us)
Async XLA Ops:
  0.0 16.1 %copy-start.14 = (s32[1,36,2]{1,2,0:T(2,128)S(1)}, s32[1,36,2]{1,2,0:T(2,128)}, u32[]{:S(2)}) copy-start(s32[1,36,2]{1,2,0:T(2,128)} %param.12) | copy-start | bytes 868
  2.7 130.0 %collective-permute-start = (bf16[2,12,192,256]{3,2,1,0:T(8,128)(2,1)S(1)}, bf16[2,12,192,256]{3,2,1,0:T(8,128)(2,1)}, u32[]{:S(2)}, u32[]{:S(2)}) collective-permute-start(bf16[2,12,192,256]{3,2,1,0:T(8,128)(2,1)S(1)} %convert_element_type.99), channel_id=1, source_target_pairs={{0,2},{1,3},{2,4},{3,5},{4,6},{5,7},{6,8},{7,9},{8,10},{9,11},{10,... | collective-permute-start | bytes 7077896 | tf_op jit(solution)/shard_map/ppermute | solution.py:18
  5.8 130.1 %collective-permute-start.1 = (bf16[2,12,192,256]{3,2,1,0:T(8,128)(2,1)S(1)}, bf16[2,12,192,256]{3,2,1,0:T(8,128)(2,1)}, u32[]{:S(2)}, u32[]{:S(2)}) collective-permute-start(bf16[2,12,192,256]{3,2,1,0:T(8,128)(2,1)S(1)} %convert_element_type.99), channel_id=1, source_target_pairs={{0,1},{1,2},{2,3},{3,4},{4,5},{5,6},{6,7},{7,8},{8,9},{9,10},{10,1... | collective-permute-start | bytes 7077896 | tf_op jit(solution)/shard_map/ppermute | solution.py:18
  9.8 131.3 %collective-permute-start.2 = (bf16[2,12,192,256]{3,2,1,0:T(8,128)(2,1)S(1)}, bf16[2,12,192,256]{3,2,1,0:T(8,128)(2,1)}, u32[]{:S(2)}, u32[]{:S(2)}) collective-permute-start(bf16[2,12,192,256]{3,2,1,0:T(8,128)(2,1)S(1)} %convert_element_type.99), channel_id=1, source_target_pairs={{1,0},{2,1},{3,2},{4,3},{5,4},{6,5},{7,6},{8,7},{9,8},{10,9},{11,1... | collective-permute-start | bytes 7077896 | tf_op jit(solution)/shard_map/ppermute | solution.py:18
  11.8 132.7 %collective-permute-start.3 = (bf16[2,12,192,256]{3,2,1,0:T(8,128)(2,1)S(1)}, bf16[2,12,192,256]{3,2,1,0:T(8,128)(2,1)}, u32[]{:S(2)}, u32[]{:S(2)}) collective-permute-start(bf16[2,12,192,256]{3,2,1,0:T(8,128)(2,1)S(1)} %convert_element_type.99), channel_id=1, source_target_pairs={{2,0},{3,1},{4,2},{5,3},{6,4},{7,5},{8,6},{9,7},{10,8},{11,9},{12,... | collective-permute-start | bytes 7077896 | tf_op jit(solution)/shard_map/ppermute | solution.py:18
  16.1 145.9 %copy-start.3 = (bf16[36,2,64,64]{3,2,1,0:T(8,128)(2,1)}, bf16[36,2,64,64]{3,2,1,0:T(8,128)(2,1)S(1)}, u32[]{:S(2)}) copy-start(bf16[36,2,64,64]{3,2,1,0:T(8,128)(2,1)S(1)} %reshape_squeeze.3) | copy-start | bytes 1769476
  16.1 0.7 copy-start.12
  16.8 122.5 %slice-start = ((s8[4718592]{0:T(1024)(128)(4,1)}), s8[4194304]{0:T(1024)(128)(4,1)S(1)}, s32[]{:S(2)}) async-start(s8[4718592]{0:T(1024)(128)(4,1)} %bitcast.213), calls=%async_computation.3 | async-start | bytes 8388608
  16.8 122.5 %slice-start.1 = ((s8[4718592]{0:T(1024)(128)(4,1)}), s8[524288]{0:T(1024)(128)(4,1)S(1)}, s32[]{:S(2)}) async-start(s8[4718592]{0:T(1024)(128)(4,1)} %bitcast.213), calls=%async_computation.4 | async-start | bytes 1048576
  175.7 165.8 %all-to-all-start.1 = ((f32[256,2,12,192]{3,1,2,0:T(2,128)}), f32[256,2,12,192]{3,1,2,0:T(2,128)}, u32[]{:S(2)}, u32[]{:S(2)}) async-start(f32[256,2,12,192]{3,1,2,0:T(2,128)} %copy.78), calls=%async_computation.1 | async-start | bytes 12582912 | tf_op jit(solution)/shard_map/all_to_all | solution.py:92
  341.5 9.0 copy-start.10
  341.5 547.2 %all-to-all-start = ((bf16[256,8,2,12,192]{4,1,3,2,0:T(8,128)(2,1)}), bf16[256,8,2,12,192]{4,1,3,2,0:T(8,128)(2,1)}, u32[]{:S(2)}, u32[]{:S(2)}) async-start(bf16[256,8,2,12,192]{4,1,3,2,0:T(8,128)(2,1)} %bitcast.212), calls=%async_computation | async-start | bytes 50331648 | tf_op jit(solution)/shard_map/all_to_all | solution.py:78
  909.9 9.8 copy-start.2
  919.7 15.9 %copy-start = (bf16[16,8,1,192,192]{4,1,3,2,0:T(8,128)(2,1)}, bf16[16,8,1,192,192]{4,1,3,2,0:T(8,128)(2,1)S(1)}, u32[]{:S(2)}) copy-start(bf16[16,8,1,192,192]{4,1,3,2,0:T(8,128)(2,1)S(1)} %get-tuple-element.14) | copy-start | bytes 28311556
  919.7 15.9 %copy-start.1 = (bf16[16,8,1,192,192]{4,1,3,2,0:T(8,128)(2,1)}, bf16[16,8,1,192,192]{4,1,3,2,0:T(8,128)(2,1)S(1)}, u32[]{:S(2)}) copy-start(bf16[16,8,1,192,192]{4,1,3,2,0:T(8,128)(2,1)S(1)} %get-tuple-element.15) | copy-start | bytes 28311556
  935.5 22.6 %copy-start.11 = (f32[192,192]{1,0:T(8,128)S(1)}, f32[192,192]{1,0:T(8,128)}, u32[]{:S(2)}) copy-start(f32[192,192]{1,0:T(8,128)} %convert_bitcast_fusion.2) | copy-start | bytes 442372
  958.2 22.5 %copy-start.8 = (bf16[1,192,2,192]{3,1,2,0:T(8,128)(2,1)S(1)}, bf16[1,192,2,192]{3,1,2,0:T(8,128)(2,1)}, u32[]{:S(2)}) copy-start(bf16[1,192,2,192]{3,1,2,0:T(8,128)(2,1)} %get-tuple-element.22) | copy-start | bytes 442372
  958.2 22.5 %copy-start.9 = (bf16[1,192,2,192]{3,1,2,0:T(8,128)(2,1)S(1)}, bf16[1,192,2,192]{3,1,2,0:T(8,128)(2,1)}, u32[]{:S(2)}) copy-start(bf16[1,192,2,192]{3,1,2,0:T(8,128)(2,1)} %get-tuple-element.25) | copy-start | bytes 442372
  1051.4 4.9 copy-start.13
  1051.4 74.8 %all-to-all-start.2 = ((bf16[16,2,192,192]{3,0,1,2:T(8,128)(2,1)}), bf16[16,2,192,192]{3,0,1,2:T(8,128)(2,1)S(1)}, u32[]{:S(2)}, u32[]{:S(2)}) async-start(bf16[16,2,192,192]{3,0,1,2:T(8,128)(2,1)} %copy.89), calls=%async_computation.2 | async-start | bytes 6291456 | tf_op jit(solution)/shard_map/all_to_all | solution.py:99
  1128.3 3.3 copy-start.4
  1185.8 255.2 %collective-permute-start.4 = (f32[2,36,64,256]{3,2,1,0:T(8,128)S(1)}, f32[2,36,64,256]{3,2,1,0:T(8,128)S(1)}, u32[]{:S(2)}, u32[]{:S(2)}) collective-permute-start(f32[2,36,64,256]{3,2,1,0:T(8,128)S(1)} %get-tuple-element.17), channel_id=1, source_target_pairs={{2,0},{3,1},{4,2},{5,3},{6,4},{7,5},{8,6},{9,7},{10,8},{11,9},{12,... | collective-permute-start | bytes 14155784 | tf_op jit(solution)/shard_map/ppermute | solution.py:18
  1187.7 253.3 %collective-permute-start.5 = (f32[2,36,64,256]{3,2,1,0:T(8,128)S(1)}, f32[2,36,64,256]{3,2,1,0:T(8,128)S(1)}, u32[]{:S(2)}, u32[]{:S(2)}) collective-permute-start(f32[2,36,64,256]{3,2,1,0:T(8,128)S(1)} %get-tuple-element.16), channel_id=1, source_target_pairs={{1,0},{2,1},{3,2},{4,3},{5,4},{6,5},{7,6},{8,7},{9,8},{10,9},{11,1... | collective-permute-start | bytes 14155784 | tf_op jit(solution)/shard_map/ppermute | solution.py:18
  1189.6 251.4 %collective-permute-start.6 = (f32[2,36,64,256]{3,2,1,0:T(8,128)S(1)}, f32[2,36,64,256]{3,2,1,0:T(8,128)S(1)}, u32[]{:S(2)}, u32[]{:S(2)}) collective-permute-start(f32[2,36,64,256]{3,2,1,0:T(8,128)S(1)} %get-tuple-element.19), channel_id=1, source_target_pairs={{0,1},{1,2},{2,3},{3,4},{4,5},{5,6},{6,7},{7,8},{8,9},{9,10},{10,1... | collective-permute-start | bytes 14155784 | tf_op jit(solution)/shard_map/ppermute | solution.py:18
  1194.2 300.0 %collective-permute-start.7 = (f32[2,36,64,256]{3,2,1,0:T(8,128)S(1)}, f32[2,36,64,256]{3,2,1,0:T(8,128)}, u32[]{:S(2)}, u32[]{:S(2)}) collective-permute-start(f32[2,36,64,256]{3,2,1,0:T(8,128)S(1)} %get-tuple-element.18), channel_id=1, source_target_pairs={{0,2},{1,3},{2,4},{3,5},{4,6},{5,7},{6,8},{7,9},{8,10},{9,11},{10,... | collective-permute-start | bytes 14155784 | tf_op jit(solution)/shard_map/ppermute | solution.py:18
  1441.0 2.1 copy-start.5
  1441.0 3.7 copy-start.6
  1444.6 2.2 copy-start.7
where the time goes:
time: 1530 us; the launch traced here: 1520 us
  waiting for transfers between devices  1110 us (73%)
  local copies, waits for them, and re-layouts  155 us (10%)
  other arithmetic  104 us (7%)
  matrix products  89.1 us (6%)
  starting transfers between devices  62.2 us (4%)
    all_to_all x1, waiting for transfers between devices, per_device(): lax.all_to_all(maps_leading, 'slab', split_axis=0, concat_axis=3, tiled=T...  526 us
    ppermute x8, waiting for transfers between devices, shifted(): return lax.ppermute(shard, axis, pairs)  406 us
    all_to_all x1, waiting for transfers between devices, per_device(): lax.all_to_all(warped_leading, 'slab', split_axis=0, concat_axis=2, tiled...  103 us
    all_to_all x1, waiting for transfers between devices, per_device(): lax.all_to_all(combined_columns, 'slab', split_axis=2, concat_axis=0, til...  69.9 us
    dot_general x2, matrix products, column_y(): jnp.einsum('zcpxj,qkpj->zcqxk', volume, matrix, preferred_element_type=jn...  57.3 us
    unnamed x40, local copies, waits for them, and re-layouts  54 us
  transfers between devices with their start and end apart: 11, of which 6 were waited for; matrix products, arithmetic and copies ran while one was open for 4% of the time, Pallas kernels for 0%

commit v1 on v0

v1 whole, which is shorter than its diff:
```python
import functools
import math

import jax
import jax.numpy as jnp
import numpy as np
from jax import lax
from jax.experimental import pallas as pl
from jax.experimental.pallas import tpu as pltpu
from jax.sharding import PartitionSpec as P

BLK = 64
LANES = 384
HALF = 256
VMEM_LIMIT = 56 * 1024 * 1024
BF = jnp.bfloat16
F32 = jnp.float32


def lane_order(length):
    lo, rest = 128, length - 128
    part = np.concatenate([np.zeros(lo), np.ones(lo), np.zeros(rest), np.ones(rest)])
    pos = np.concatenate([np.arange(lo), np.arange(lo), lo + np.arange(rest), lo + np.arange(rest)])
    return part.astype(np.int32), pos.astype(np.int32)


def dft_table(length, direction):
    positions = np.arange(length)
    phases = (positions[:, None] * positions[None, :] % length).astype(np.float32)
    phases = phases * np.float32(2.0 * math.pi / length)
    factor = np.float32(1.0 / math.sqrt(length))
    cosine = np.cos(phases) * factor
    sine = np.sin(phases) * (np.float32(direction) * factor)
    upper = np.stack([cosine, -sine], axis=1)
    lower = np.stack([sine, cosine], axis=1)
    return np.stack([upper, lower], axis=0)


def tables(nx, ny):
    part, pos = lane_order(ny)
    fwd_y, inv_y = dft_table(ny, -1.0), dft_table(ny, 1.0)
    into_y = np.zeros((2 * ny, 2, HALF), np.float32)
    into_y[:, :, :ny] = np.transpose(fwd_y[:, :, part, pos], (2, 0, 1))
    from_y = np.zeros((2, HALF, 2 * ny), np.float32)
    from_y[:, :ny, :] = np.transpose(inv_y[part, pos], (1, 2, 0))
    fwd_x = dft_table(nx, -1.0).reshape(2 * nx, 2 * nx)
    inv_x = dft_table(nx, 1.0).reshape(2 * nx, 2 * nx)
    out = (into_y.reshape(2 * ny, 2 * HALF), fwd_x, inv_x, from_y.reshape(2 * HALF, 2 * ny))
    return tuple(jnp.asarray(t, BF) for t in out)


def params():
    return pltpu.CompilerParams(vmem_limit_bytes=VMEM_LIMIT)


def to_rows(parts):
    stacked = jnp.concatenate(
        [parts[0, :128], parts[1, :128], parts[0, 128:], parts[1, 128:]], axis=0
    )
    return stacked.T


def spread_rows(out, rows, scratch, count, deep):
    if deep % 16 == 0:
        out[...] = rows.reshape(count, deep, LANES)
    else:
        scratch[...] = rows.astype(F32)
        for d in range(count):
            out[d] = scratch[pl.ds(d * deep, deep), :].astype(BF)


def image_kernel(count, deep, x_ref, o_ref, scratch):
    spread_rows(o_ref.at[:, 0], to_rows(x_ref[:, 0].astype(BF)), scratch, count, deep)


def image_columns(image, count):
    _, planes, ny, nz = image.shape
    deep = nz // count
    return pl.pallas_call(
        functools.partial(image_kernel, count, deep),
        out_shape=jax.ShapeDtypeStruct((count, planes, deep, LANES), BF),
        grid=(planes,),
        in_specs=[pl.BlockSpec((2, 1, ny, nz), lambda x: (0, x, 0, 0))],
        out_specs=pl.BlockSpec((count, 1, deep, LANES), lambda x: (0, x, 0, 0)),
        scratch_shapes=[pltpu.VMEM((nz, LANES), F32)],
        compiler_params=params(),
        cost_estimate=pl.CostEstimate(flops=0, bytes_accessed=image.size * 6, transcendentals=0),
        name="image_columns",
    )(image)


def maps_kernel(count, deep, x_ref, o_ref, scratch):
    spread_rows(o_ref.at[:, 0, 0], to_rows(x_ref[0, :, 0]), scratch, count, deep)


def maps_columns(coil_maps, count, first, coils):
    _, _, planes, ny, nz = coil_maps.shape
    deep = nz // count
    return pl.pallas_call(
        functools.partial(maps_kernel, count, deep),
        out_shape=jax.ShapeDtypeStruct((count, planes, coils, deep, LANES), BF),
        grid=(planes, coils),
        in_specs=[pl.BlockSpec((1, 2, 1, ny, nz), lambda x, c: (first + c, 0, x, 0, 0))],
        out_specs=pl.BlockSpec((count, 1, 1, deep, LANES), lambda x, c: (0, x, c, 0, 0)),
        scratch_shapes=[pltpu.VMEM((nz, LANES), F32)],
        compiler_params=params(),
        cost_estimate=pl.CostEstimate(
            flops=0, bytes_accessed=coils * 2 * planes * ny * nz * 4, transcendentals=0
        ),
        name="maps_columns",
    )(coil_maps)


def low_half(shape):
    return lax.broadcasted_iota(jnp.int32, shape, len(shape) - 1) < BLK


def warp_kernel(nx, deep, pad, links, g_ref, w_ref, o_ref, twice):
    planes = o_ref.shape[0]
    step = pl.program_id(0)

    @pl.when(step == 0)
    def _():
        def split(x, carry):
            low = low_half((deep, 128))
            for v in range(3):
                row = g_ref[x, :, v * 128 : (v + 1) * 128].astype(F32)
                turned = pltpu.roll(row, BLK, 1)
                first = jnp.where(low, row, turned).astype(BF)
                second = jnp.where(low, turned, row).astype(BF)
                if v < 2:
                    twice[3 * x, pl.ds(v * pad, deep), :] = first
                    twice[3 * x + 1, pl.ds(v * pad, deep), :] = second
                else:
                    twice[3 * x + 2, pl.ds(0, deep), :] = first
                    twice[3 * x + 2, pl.ds(pad, deep), :] = second
            return carry

        lax.fori_loop(0, nx, split, 0)

    low = low_half((2 * pad, 128))

    def plane(x, carry):
        outs = []
        for b in range(3):
            t = 3 * x + b
            g = 2 * (3 * planes * step + t)
            both = jnp.where(low, twice[links[g]], twice[links[g + 1]])
            outs.append(
                lax.dot_general(
                    both, w_ref[t], (((1,), (1,)), ((), ())), preferred_element_type=F32
                )
            )
        a, b, c = outs
        re = jnp.concatenate([a[:deep], b[:deep]], axis=1)
        im = jnp.concatenate([a[pad : pad + deep], b[pad : pad + deep]], axis=1)
        rest = jnp.concatenate([c[:deep], c[pad : pad + deep]], axis=1)
        o_ref[x, :, 0:128] = re
        o_ref[x, :, 128:256] = im
        o_ref[x, :, 256:384] = rest
        return carry

    lax.fori_loop(0, planes, plane, 0, unroll=True)


def warp(columns, weights, links, planes):
    nx, deep, _ = columns.shape
    blocks = weights.shape[0]
    pad = max(16, deep)
    return pl.pallas_call(
        functools.partial(warp_kernel, nx, deep, pad),
        out_shape=jax.ShapeDtypeStruct((nx, deep, LANES), F32),
        grid_spec=pltpu.PrefetchScalarGridSpec(
            num_scalar_prefetch=1,
            grid=(nx // planes,),
            in_specs=[
                pl.BlockSpec((nx, deep, LANES), lambda s, l: (0, 0, 0)),
                pl.BlockSpec((3 * planes, BLK, 2 * BLK), lambda s, l: (s, 0, 0)),
            ],
            out_specs=pl.BlockSpec((planes, deep, LANES), lambda s, l: (s, 0, 0)),
            scratch_shapes=[pltpu.VMEM((blocks, 2 * pad, 128), BF)],
        ),
        compiler_params=params(),
        cost_estimate=pl.CostEstimate(
            flops=2 * blocks * 256 * 256 * 32, bytes_accessed=20 << 20, transcendentals=0
        ),
        name="warp",
    )(links, columns, weights)


def spread_kernel(nx, deep, pad, links, c_ref, w_ref, o_ref, total):
    planes = c_ref.shape[0]
    step = pl.program_id(0)

    @pl.when(step == 0)
    def _():
        def clear(i, carry):
            total[pl.ds(i * 3, 3)] = jnp.zeros((3, 2 * pad, 128), F32)
            return carry

        lax.fori_loop(0, nx, clear, 0)

    low = low_half((2 * pad, 128))

    def tall(a, b):
        if deep == pad:
            return jnp.concatenate([a, b], axis=0)
        fill = jnp.zeros((pad - deep, a.shape[1]), a.dtype)
        return jnp.concatenate([a, fill, b, fill], axis=0)

    def plane(x, carry):
        re, im, rest = (c_ref[x, :, v * 128 : (v + 1) * 128] for v in range(3))
        blocks = (
            tall(re[:, :BLK], im[:, :BLK]),
            tall(re[:, BLK:], im[:, BLK:]),
            tall(rest[:, :BLK], rest[:, BLK:]),
        )
        for b in range(3):
            t = 3 * x + b
            g = 2 * (3 * planes * step + t)
            out = jnp.dot(blocks[b].astype(BF), w_ref[t], preferred_element_type=F32)
            zero = jnp.zeros_like(out)
            total[links[g]] += jnp.where(low, out, zero)
            total[links[g + 1]] += jnp.where(low, zero, out)
        return carry

    lax.fori_loop(0, planes, plane, 0, unroll=True)

    @pl.when(step == pl.num_programs(0) - 1)
    def _():
        low_row = low_half((deep, 128))

        def gather(x, carry):
            sums = []
            for b in range(3):
                value = total[3 * x + b]
                sums.append(value + pltpu.roll(value, BLK, 1))
            a, b, c = sums
            o_ref[x, :, 0:128] = jnp.where(low_row, a[:deep], b[:deep]).astype(BF)
            o_ref[x, :, 128:256] = jnp.where(
                low_row, a[pad : pad + deep], b[pad : pad + deep]
            ).astype(BF)
            o_ref[x, :, 256:384] = jnp.where(low_row, c[:deep], c[pad : pad + deep]).astype(BF)
            return carry

        lax.fori_loop(0, nx, gather, 0)


def spread(combined, weights, links, planes):
    nx, deep, _ = combined.shape
    blocks = weights.shape[0]
    pad = max(16, deep)
    return pl.pallas_call(
        functools.partial(spread_kernel, nx, deep, pad),
        out_shape=jax.ShapeDtypeStruct((nx, deep, LANES), BF),
        grid_spec=pltpu.PrefetchScalarGridSpec(
            num_scalar_prefetch=1,
            grid=(nx // planes,),
            in_specs=[
                pl.BlockSpec((planes, deep, LANES), lambda s, l: (s, 0, 0)),
                pl.BlockSpec((3 * planes, BLK, 2 * BLK), lambda s, l: (s, 0, 0)),
            ],
            out_specs=pl.BlockSpec((nx, deep, LANES), lambda s, l: (0, 0, 0)),
            scratch_shapes=[pltpu.VMEM((blocks, 2 * pad, 128), F32)],
        ),
        compiler_params=params(),
        cost_estimate=pl.CostEstimate(
            flops=2 * blocks * 256 * 256 * 32, bytes_accessed=20 << 20, transcendentals=0
        ),
        name="spread",
    )(links, combined, weights)


def coil_kernel(nx, deep, pad, fresh, *refs):
    if fresh:
        s_ref, w_ref, mask, iy, fx, bx, oy, o_ref, rows = refs
    else:
        s_ref, w_ref, mask, iy, fx, bx, oy, before, o_ref, rows = refs
    group = 8 if nx % 8 == 0 else 1
    cube = rows.reshape(3, nx, pad, 128)
    low = low_half((group, deep, 128))

    def thirds(ref, at):
        return tuple(ref[at, :, v * 128 : (v + 1) * 128].astype(F32) for v in range(3))

    def expand(i, carry):
        at = pl.ds(i * group, group)
        s0, s1, s2 = thirds(s_ref.at[:, 0], at)
        w0, w1, w2 = thirds(w_ref, at)
        turned = pltpu.roll(s2, BLK, 2)
        other = pltpu.roll(w2, BLK, 2)
        real = jnp.where(low, s2, turned)
        imag = jnp.where(low, turned, s2)
        cube[0, at, pl.ds(0, deep), :] = s0 * w0 - s1 * w1
        cube[1, at, pl.ds(0, deep), :] = s0 * w1 + s1 * w0
        cube[2, at, pl.ds(0, deep), :] = real * w2 + imag * jnp.where(low, -other, other)
        return carry

    lax.fori_loop(0, nx // group, expand, 0)

    def column(z, carry):
        at = pl.ds(z, nx, stride=pad)
        line = jnp.concatenate(
            [rows[v, at, :] for v in range(3)], axis=1
        ).astype(BF)
        y = jnp.dot(line, iy[...], preferred_element_type=F32).astype(BF)
        y = jnp.concatenate([y[:, :HALF], y[:, HALF:]], axis=0)
        y = jnp.dot(fx[...], y, preferred_element_type=F32) * mask[...]
        y = jnp.dot(bx[...], y.astype(BF), preferred_element_type=F32).astype(BF)
        y = jnp.concatenate([y[:nx], y[nx:]], axis=1)
        y = jnp.dot(y, oy[...], preferred_element_type=F32)
        for v in range(3):
            rows[v, at, :] = y[:, v * 128 : (v + 1) * 128]
        return carry

    lax.fori_loop(0, deep, column, 0)

    first = pl.program_id(0) == 0

    def combine(i, carry):
        at = pl.ds(i * group, group)
        s0, s1, s2 = thirds(s_ref.at[:, 0], at)
        r0, r1, r2 = (cube[v, at, pl.ds(0, deep), :] for v in range(3))
        turned = pltpu.roll(s2, BLK, 2)
        other = pltpu.roll(r2, BLK, 2)
        real = jnp.where(low, s2, turned)
        imag = jnp.where(low, turned, s2)
        terms = (
            s0 * r0 + s1 * r1,
            s0 * r1 - s1 * r0,
            real * r2 + imag * jnp.where(low, other, -other),
        )
        for v in range(3):
            lanes = slice(v * 128, (v + 1) * 128)
            old = o_ref[at, :, lanes]
            start = jnp.zeros_like(old) if fresh else before[at, :, lanes]
            o_ref[at, :, lanes] = jnp.where(first, start, old) + terms[v]
        return carry

    lax.fori_loop(0, nx // group, combine, 0)


def coils(maps, warped, mask, tabs, before):
    nx, deep, _ = warped.shape
    count = maps.shape[1]
    pad = max(8, deep)
    fresh = before is None
    whole = lambda shape: pl.BlockSpec(
        shape, lambda c: (0,) * len(shape), pipeline_mode=pl.Buffered(1)
    )
    in_specs = [pl.BlockSpec((nx, 1, deep, LANES), lambda c: (0, c, 0, 0))]
    args = [maps, warped, mask, *tabs] + ([] if fresh else [before])
    in_specs += [whole(a.shape) for a in args[1:]]
    return pl.pallas_call(
        functools.partial(coil_kernel, nx, deep, pad, fresh),
        out_shape=jax.ShapeDtypeStruct((nx, deep, LANES), F32),
        grid=(count,),
        in_specs=in_specs,
        out_specs=pl.BlockSpec((nx, deep, LANES), lambda c: (0, 0, 0)),
        scratch_shapes=[pltpu.VMEM((3, nx * pad, 128), F32)],
        compiler_params=params(),
        cost_estimate=pl.CostEstimate(
            flops=count * deep * 4 * 8 * nx * nx * 192 * 2,
            bytes_accessed=count * nx * deep * LANES * 2 + (14 << 20),
            transcendentals=0,
        ),
        name="coils",
    )(*args)


def update_kernel(count, deep, g_ref, i_ref, a_ref, o_ref, scratch):
    if deep % 16 == 0:
        rows = g_ref[:, 0].reshape(count * deep, LANES)
    else:
        for d in range(count):
            scratch[pl.ds(d * deep, deep), :] = g_ref[d, 0].astype(F32)
        rows = scratch[...]
    grad = rows.astype(F32).T
    real = jnp.concatenate([grad[0:128], grad[256:320]], axis=0)
    imag = jnp.concatenate([grad[128:256], grad[320:384]], axis=0)
    for part, value in enumerate((real, imag)):
        o_ref[part, 0] = i_ref[part, 0] - 0.5 * (value - a_ref[part, 0].astype(F32))


def update(back, image, adjoint):
    count, planes, deep, _ = back.shape
    _, _, ny, nz = image.shape
    block = pl.BlockSpec((2, 1, ny, nz), lambda x: (0, x, 0, 0))
    return pl.pallas_call(
        functools.partial(update_kernel, count, deep),
        out_shape=jax.ShapeDtypeStruct(image.shape, F32),
        grid=(planes,),
        in_specs=[
            pl.BlockSpec((count, 1, deep, LANES), lambda x: (0, x, 0, 0)),
            block,
            block,
        ],
        out_specs=block,
        scratch_shapes=[pltpu.VMEM((nz, LANES), F32)],
        compiler_params=params(),
        cost_estimate=pl.CostEstimate(flops=0, bytes_accessed=image.size * 12, transcendentals=0),
        name="update",
    )(back, image, adjoint)


def exchange(parts):
    return lax.all_to_all(parts, "slab", split_axis=0, concat_axis=0, tiled=True)


def split_coils(total):
    sizes = []
    left = total
    while left:
        size = 1 if left <= 2 else min(3, left - 1)
        sizes.append(size)
        left -= size
    return sizes


def per_device(image, adjoint_data, coil_maps, masks, sources, weights):
    count = lax.axis_size("slab")
    planes, ny, nz = image.shape[1:]
    nx = planes * count
    deep = nz // count
    tabs = tables(nx, ny)
    matrices = weights[0].reshape(3 * planes, 2, BLK, BLK)
    matrices = jnp.transpose(matrices, (0, 2, 1, 3)).reshape(3 * planes, BLK, 2 * BLK)
    matrices = lax.all_gather(matrices, "slab", axis=0, tiled=True)
    links = lax.all_gather(sources[0], "slab", axis=0, tiled=True).reshape(-1)
    sampled = jnp.pad(masks[0].astype(F32), ((0, 0), (0, HALF - ny)))
    mask = jnp.concatenate([sampled, sampled], axis=0)

    columns = exchange(image_columns(image, count)).reshape(nx, deep, LANES)
    sizes = split_coils(coil_maps.shape[0])
    sent, first = [], 0
    for size in sizes:
        sent.append(exchange(maps_columns(coil_maps, count, first, size)))
        first += size
    warped = warp(columns, matrices, links, planes)
    combined = None
    for size, part in zip(sizes, sent):
        maps = part.reshape(nx, size, deep, LANES)
        combined = coils(maps, warped, mask, tabs, combined)
    grad = spread(combined, matrices, links, planes)
    back = exchange(grad.reshape(count, planes, deep, LANES))
    return update(back, image, adjoint_data)


def solution(mesh):
    return jax.shard_map(
        per_device,
        mesh=mesh,
        in_specs=(
            P(None, ("grp", "slab"), None, None),
            P(None, ("grp", "slab"), None, None),
            P(None, None, ("grp", "slab"), None, None),
            P(None, "grp", None),
            P(None, ("grp", "slab"), None),
            P(None, ("grp", "slab"), None),
        ),
        out_specs=P(None, ("grp", "slab"), None, None),
        check_vma=False,
    )
```

time: 1530 us -> 894 us (0.58)
  waiting for transfers between devices: 1110 us -> 261 us
  Pallas kernels: 0 us -> 365 us
  blocking collectives: 0 us -> 215 us
  local copies, waits for them, and re-layouts: 155 us -> 6.67 us
  other arithmetic: 104 us -> 2.08 us
  matrix products: 89.1 us -> 0 us
  starting transfers between devices: 62.2 us -> 26.3 us
    all_to_all x3 -> x5, waiting for transfers between devices: 699 us -> 261 us  [exchange(): lax.all_to_all(parts, 'slab', split_axis=0, concat_axis=0, tiled=True)]
    ppermute x8 -> x0, waiting for transfers between devices: 406 us -> none  [shifted(): return lax.ppermute(shard, axis, pairs)]
    pallas_call x0 -> x12, Pallas kernels: none -> 365 us  [the longest x4 220 us: coils(): pl.pallas_call(functools.partial(coil_kernel, nx, deep, pad, fresh), out_...]
    all_gather x0 -> x1, blocking collectives: none -> 156 us  [per_device(): links = lax.all_gather(sources[0], 'slab', axis=0, tiled=True).reshape(-1)]
    dot_general x7 -> x0, matrix products: 89.1 us -> none  [the longest x2 57.3 us: column_y(): jnp.einsum('zcpxj,qkpj->zcqxk', volume, matrix, preferred_element_type=jn...]
    all_to_all x0 -> x1, blocking collectives: none -> 59 us  [exchange(): lax.all_to_all(parts, 'slab', split_axis=0, concat_axis=0, tiled=True)]
    unnamed x40 -> x11, local copies, waits for them, and re-layouts: 54 us -> 1.51 us
    scatter-add x2 -> x0, other arithmetic: 29.7 us -> none  [per_device(): spread = spread.at[:, positions[:, member]].add(product)]
  transfers between devices with their start and end apart: 11 -> 6, of which waited for: 6 -> 3; matrix products, arithmetic and copies ran while one was open for 4% -> 1% of each run, Pallas kernels for 0% -> 32%
where the time goes in v1:
time: 894 us; the launch traced here: 889 us
  Pallas kernels  365 us (41%)
  waiting for transfers between devices  261 us (29%)
  blocking collectives  215 us (24%)
  starting transfers between devices  26.3 us (3%)
  between operations  13.5 us (2%)
    all_to_all x5, waiting for transfers between devices, exchange(): lax.all_to_all(parts, 'slab', split_axis=0, concat_axis=0, tiled=True)  261 us
    pallas_call x4, Pallas kernels, coils(): pl.pallas_call(functools.partial(coil_kernel, nx, deep, pad, fresh), out_...  220 us
    all_gather x1, blocking collectives, per_device(): links = lax.all_gather(sources[0], 'slab', axis=0, tiled=True).reshape(-1)  156 us
    pallas_call x4, Pallas kernels, maps_columns(): pl.pallas_call(functools.partial(maps_kernel, count, deep), out_shape=jax...  61 us
    all_to_all x1, blocking collectives, exchange(): lax.all_to_all(parts, 'slab', split_axis=0, concat_axis=0, tiled=True)  59 us
    pallas_call x1, Pallas kernels, spread(): pl.pallas_call(functools.partial(spread_kernel, nx, deep, pad), out_shape...  33.7 us
    pallas_call x1, Pallas kernels, warp(): pl.pallas_call(functools.partial(warp_kernel, nx, deep, pad), out_shape=j...  31.2 us
    all_to_all x5, starting transfers between devices, exchange(): lax.all_to_all(parts, 'slab', split_axis=0, concat_axis=0, tiled=True)  26.3 us
  transfers between devices with their start and end apart: 6, of which 3 were waited for; matrix products, arithmetic and copies ran while one was open for 1% of the time, Pallas kernels for 32%

profile of v1, /device:TPU:13, one launch (start us, length us, event | category | flops | bytes accessed | tf_op | source)
XLA Modules:
  0.0 889.1 jit_solution(9176218770848574934)
XLA Ops:
  6.5 8.5 image_columns.1
  15.0 6.6 all-to-all-start.1
  21.6 8.2 maps_columns.5
  29.8 44.8 %all-to-all-done.1 = bf16[16,12,16,384]{3,2,1,0:T(8,128)(2,1)S(1)} async-done(((bf16[16,12,16,384]{3,2,1,0:T(8,128)(2,1)}), bf16[16,12,16,384]{3,2,1,0:T(8,128)(2,1)S(1)}, u32[]{:S(2)}, u32[]{:S(2)}) %all-to-all-start.1) | async-done | bytes 2359328 | tf_op jit(solution)/shard_map/all_to_all | solution.py:407
  74.6 0.0 copy-start
  74.6 4.9 all-to-all-start.2
  79.5 22.2 %maps_columns.7 = bf16[16,12,3,16,384]{4,3,2,1,0:T(8,128)(2,1)} custom-call(bf16[8,2,12,192,256]{4,3,2,1,0:T(8,128)(2,1)} %x_ref.9), custom_call_target="tpu_custom_call" | custom-call | bytes 14155776 | tf_op jit(solution)/shard_map/maps_columns/pallas_call | solution.py:99
  101.7 0.0 copy-done
  101.7 0.0 copy-start.2
  101.7 31.0 %all-to-all-done.2 = bf16[16,12,1,16,384]{4,3,2,1,0:T(8,128)(2,1)} async-done(((bf16[16,12,1,16,384]{4,3,2,1,0:T(8,128)(2,1)}), bf16[16,12,1,16,384]{4,3,2,1,0:T(8,128)(2,1)}, u32[]{:S(2)}, u32[]{:S(2)}) %all-to-all-start.2) | async-done | bytes 2359328 | tf_op jit(solution)/shard_map/all_to_all | solution.py:407
  132.7 4.9 all-to-all-start.4
  137.6 0.0 all-gather.3.cloned.1.call-start
  137.6 0.0 copy-done.2
  137.7 1.3 reshape_squeeze.3
  138.9 1.2 copy.17
  140.1 1.4 reshape.28
  141.5 0.0 all-gather.3.cloned.1.call-update
  141.5 22.3 %maps_columns.6 = bf16[16,12,3,16,384]{4,3,2,1,0:T(8,128)(2,1)} custom-call(bf16[8,2,12,192,256]{4,3,2,1,0:T(8,128)(2,1)} %x_ref.9), custom_call_target="tpu_custom_call" | custom-call | bytes 14155776 | tf_op jit(solution)/shard_map/maps_columns/pallas_call | solution.py:99
  163.8 184.9 %all-to-all-done.4 = bf16[16,12,3,16,384]{4,3,2,1,0:T(8,128)(2,1)} async-done(((bf16[16,12,3,16,384]{4,3,2,1,0:T(8,128)(2,1)}), bf16[16,12,3,16,384]{4,3,2,1,0:T(8,128)(2,1)}, u32[]{:S(2)}, u32[]{:S(2)}) %all-to-all-start.4) | async-done | bytes 7077920 | tf_op jit(solution)/shard_map/all_to_all | solution.py:407
  348.8 4.9 all-to-all-start.3
  353.7 0.0 copy-start.4
  353.7 0.0 copy-start.3
  353.7 8.3 maps_columns.4
  361.9 0.0 copy-done.4
  361.9 0.1 copy.14
  362.0 156.1 %all-gather = s32[1,576,2]{2,0,1:T(1,128)S(1)} all-gather(s32[1,36,2]{2,0,1:T(1,128)S(1)} %copy.14), channel_id=2, replica_groups=mesh['grp'=2,'slab'=16] {'slab'}, dimensions={1}, use_global_device_ids=true | all-gather | bytes 4896 | tf_op jit(solution)/shard_map/all_gather | solution.py:429
  518.2 0.5 broadcast.5
  518.7 1.3 reduce.3
  520.0 0.8 reshape.25.links
  520.8 0.0 copy-done.3
  520.8 0.8 pad_maximum_fusion.refs_2_
  521.6 0.0 all-gather.3.cloned.1.call-done.w_ref
  521.6 31.2 %warp.1.refs_1_ = f32[192,16,384]{2,1,0:T(8,128)} custom-call(s32[1152]{0:T(1024)} %reshape.25.links, bf16[192,16,384]{2,1,0:T(8,128)(2,1)} %bitcast.12, bf16[576,64,128]{2,1,0:T(8,128)(2,1)} %all-gather.3.cloned.1.call-done.w_ref), custom_call_target="tpu_custom_call" | custom-call | flops 2415919104 | bytes 20971520 | tf_op jit(solution)/shard_map/warp/pallas_call | solution.py:170
  552.8 0.0 all-to-all-done.3
  552.8 5.1 all-to-all-start
  557.9 77.7 %coils.4.refs_7_ = f32[192,16,384]{2,1,0:T(8,128)} custom-call(bf16[192,3,16,384]{3,2,1,0:T(8,128)(2,1)} %bitcast.6.refs_0_, f32[192,16,384]{2,1,0:T(8,128)} %warp.1.refs_1_, f32[384,256]{1,0:T(8,128)} %pad_maximum_fusion.refs_2_, bf16[384,512]{1,0:T(8,128)(2,1)} %constant.11.clone.refs_3_, bf16[384,384]{1,0:T(8,128)(2,1)} %constant.12.clone.refs_4_, ...), custom_call_target="tpu_custom_call" | custom-call | flops 21743271936 | bytes 21757952 | tf_op jit(solution)/shard_map/coils/pallas_call | solution.py:354
  635.5 79.6 %coils.5.refs_7_ = f32[192,16,384]{2,1,0:T(8,128)} custom-call(bf16[192,3,16,384]{3,2,1,0:T(8,128)(2,1)} %bitcast.5.refs_0_, f32[192,16,384]{2,1,0:T(8,128)} %warp.1.refs_1_, f32[384,256]{1,0:T(8,128)} %pad_maximum_fusion.refs_2_, bf16[384,512]{1,0:T(8,128)(2,1)} %constant.11.clone.refs_3_, bf16[384,384]{1,0:T(8,128)(2,1)} %constant.12.clone.refs_4_, ...), custom_call_target="tpu_custom_call" | custom-call | flops 21743271936 | bytes 21757952 | tf_op jit(solution)/shard_map/coils/pallas_call | solution.py:354
  715.1 31.5 %coils.6.refs_7_ = f32[192,16,384]{2,1,0:T(8,128)} custom-call(bf16[192,1,16,384]{3,2,1,0:T(8,128)(2,1)} %bitcast.4.refs_0_, f32[192,16,384]{2,1,0:T(8,128)} %warp.1.refs_1_, f32[384,256]{1,0:T(8,128)} %pad_maximum_fusion.refs_2_, bf16[384,512]{1,0:T(8,128)(2,1)} %constant.11.clone.refs_3_, bf16[384,384]{1,0:T(8,128)(2,1)} %constant.12.clone.refs_4_, ...), custom_call_target="tpu_custom_call" | custom-call | flops 7247757312 | bytes 17039360 | tf_op jit(solution)/shard_map/coils/pallas_call | solution.py:354
  746.6 0.0 all-to-all-done
  746.6 0.0 copy-start.1
  746.6 1.4 copy-done.1
  748.0 31.4 %coils.7.c_ref = f32[192,16,384]{2,1,0:T(8,128)} custom-call(bf16[192,1,16,384]{3,2,1,0:T(8,128)(2,1)} %bitcast.15, f32[192,16,384]{2,1,0:T(8,128)} %warp.1.refs_1_, f32[384,256]{1,0:T(8,128)} %pad_maximum_fusion.refs_2_, bf16[384,512]{1,0:T(8,128)(2,1)} %constant.11.clone.refs_3_, bf16[384,384]{1,0:T(8,128)(2,1)} %constant.12.clone.refs_4_, ...), custom_call_target="tpu_custom_call" | custom-call | flops 7247757312 | bytes 17039360 | tf_op jit(solution)/shard_map/coils/pallas_call | solution.py:354
  779.4 33.7 %spread.1 = bf16[192,16,384]{2,1,0:T(8,128)(2,1)} custom-call(s32[1152]{0:T(1024)} %reshape.25.links, f32[192,16,384]{2,1,0:T(8,128)} %coils.7.c_ref, bf16[576,64,128]{2,1,0:T(8,128)(2,1)} %all-gather.3.cloned.1.call-done.w_ref), custom_call_target="tpu_custom_call" | custom-call | flops 2415919104 | bytes 20971520 | tf_op jit(solution)/shard_map/spread/pallas_call | solution.py:253
  813.2 59.0 %all_to_all.30.g_ref = bf16[16,12,16,384]{3,2,1,0:T(8,128)(2,1)} all-to-all(bf16[16,12,16,384]{3,2,1,0:T(8,128)(2,1)} %bitcast.13), channel_id=1, replica_groups=mesh['grp'=2,'slab'=16] {'slab'}, dimensions={0} | all-to-all | bytes 4718592 | tf_op jit(solution)/shard_map/all_to_all | solution.py:407
  872.2 10.0 %update.1 = f32[2,12,192,256]{3,2,1,0:T(8,128)} custom-call(bf16[16,12,16,384]{3,2,1,0:T(8,128)(2,1)} %all_to_all.30.g_ref, f32[2,12,192,256]{3,2,1,0:T(8,128)} %i_ref.1, bf16[2,12,192,256]{3,2,1,0:T(8,128)(2,1)} %a_ref.1), custom_call_target="tpu_custom_call" | custom-call | bytes 14155776 | tf_op jit(solution)/shard_map/update/pallas_call | solution.py:389
  (2 shorter events, 0.0 us)
Async XLA Ops:
  15.0 59.6 %all-to-all-start.1 = ((bf16[16,12,16,384]{3,2,1,0:T(8,128)(2,1)}), bf16[16,12,16,384]{3,2,1,0:T(8,128)(2,1)S(1)}, u32[]{:S(2)}, u32[]{:S(2)}) async-start(bf16[16,12,16,384]{3,2,1,0:T(8,128)(2,1)} %image_columns.1), calls=%async_computation.1 | async-start | bytes 4718592 | tf_op jit(solution)/shard_map/all_to_all | solution.py:407
  74.6 27.1 %copy-start = (bf16[16,12,16,384]{3,2,1,0:T(8,128)(2,1)}, bf16[16,12,16,384]{3,2,1,0:T(8,128)(2,1)S(1)}, u32[]{:S(2)}) copy-start(bf16[16,12,16,384]{3,2,1,0:T(8,128)(2,1)S(1)} %all-to-all-done.1) | copy-start | bytes 7077892
  74.6 58.1 %all-to-all-start.2 = ((bf16[16,12,1,16,384]{4,3,2,1,0:T(8,128)(2,1)}), bf16[16,12,1,16,384]{4,3,2,1,0:T(8,128)(2,1)}, u32[]{:S(2)}, u32[]{:S(2)}) async-start(bf16[16,12,1,16,384]{4,3,2,1,0:T(8,128)(2,1)} %maps_columns.5), calls=%async_computation.2 | async-start | bytes 4718592 | tf_op jit(solution)/shard_map/all_to_all | solution.py:407
  101.7 35.9 %copy-start.2 = (bf16[1,36,8192]{2,1,0:T(8,128)(2,1)S(1)}, bf16[1,36,8192]{2,1,0:T(8,128)(2,1)}, u32[]{:S(2)}) copy-start(bf16[1,36,8192]{2,1,0:T(8,128)(2,1)} %param.15) | copy-start | bytes 1769476
  132.7 216.1 %all-to-all-start.4 = ((bf16[16,12,3,16,384]{4,3,2,1,0:T(8,128)(2,1)}), bf16[16,12,3,16,384]{4,3,2,1,0:T(8,128)(2,1)}, u32[]{:S(2)}, u32[]{:S(2)}) async-start(bf16[16,12,3,16,384]{4,3,2,1,0:T(8,128)(2,1)} %maps_columns.7), calls=%async_computation.4 | async-start | bytes 14155776 | tf_op jit(solution)/shard_map/all_to_all | solution.py:407
  137.6 384.0 %all-gather.3.cloned.1.call-start = ((), (), s32[]{:S(2)}) async-start(), calls=%async_computation.6 | async-start | bytes 10027008 | tf_op jit(solution)/shard_map/all_gather | solution.py:428
  348.8 204.0 %all-to-all-start.3 = ((bf16[16,12,3,16,384]{4,3,2,1,0:T(8,128)(2,1)}), bf16[16,12,3,16,384]{4,3,2,1,0:T(8,128)(2,1)}, u32[]{:S(2)}, u32[]{:S(2)}) async-start(bf16[16,12,3,16,384]{4,3,2,1,0:T(8,128)(2,1)} %maps_columns.6), calls=%async_computation.3 | async-start | bytes 14155776 | tf_op jit(solution)/shard_map/all_to_all | solution.py:407
  353.7 8.3 copy-start.4
  353.7 167.1 %copy-start.3 = (s32[1,192,192]{2,1,0:T(8,128)S(1)}, s32[1,192,192]{2,1,0:T(8,128)}, u32[]{:S(2)}) copy-start(s32[1,192,192]{2,1,0:T(8,128)} %param.13) | copy-start | bytes 442372
  552.8 193.8 %all-to-all-start = ((bf16[16,12,1,16,384]{4,3,2,1,0:T(8,128)(2,1)}), bf16[16,12,1,16,384]{4,3,2,1,0:T(8,128)(2,1)S(1)}, u32[]{:S(2)}, u32[]{:S(2)}) async-start(bf16[16,12,1,16,384]{4,3,2,1,0:T(8,128)(2,1)} %maps_columns.4), calls=%async_computation | async-start | bytes 4718592 | tf_op jit(solution)/shard_map/all_to_all | solution.py:407
  746.6 1.4 copy-start.1
Sparse Core Ops, SparseCore 0:
  141.7 177.2 all-gather.2

commit v2 on v1

--- a/solution.py
+++ b/solution.py
@@ -60,17 +60,19 @@
     return stacked.T
 
 
-def spread_rows(out, rows, scratch, count, deep):
-    if deep % 16 == 0:
-        out[...] = rows.reshape(count, deep, LANES)
-    else:
-        scratch[...] = rows.astype(F32)
+def spread_rows(outs, rows, scratch, count, deep):
+    if len(outs) == 1 and deep % 16 == 0:
+        outs[0][...] = rows.reshape(count, deep, LANES)
+        return
+    part = deep // len(outs)
+    scratch[...] = rows.astype(F32)
+    for h, out in enumerate(outs):
         for d in range(count):
-            out[d] = scratch[pl.ds(d * deep, deep), :].astype(BF)
+            out[d] = scratch[pl.ds(d * deep + h * part, part), :].astype(BF)
 
 
 def image_kernel(count, deep, x_ref, o_ref, scratch):
-    spread_rows(o_ref.at[:, 0], to_rows(x_ref[:, 0].astype(BF)), scratch, count, deep)
+    spread_rows([o_ref.at[:, 0]], to_rows(x_ref[:, 0].astype(BF)), scratch, count, deep)
 
 
 def image_columns(image, count):
@@ -89,19 +91,21 @@
     )(image)
 
 
-def maps_kernel(count, deep, x_ref, o_ref, scratch):
-    spread_rows(o_ref.at[:, 0, 0], to_rows(x_ref[0, :, 0]), scratch, count, deep)
-
-
-def maps_columns(coil_maps, count, first, coils):
+def maps_kernel(count, deep, x_ref, *refs):
+    outs = [o.at[:, 0, 0] for o in refs[:-1]]
+    spread_rows(outs, to_rows(x_ref[0, :, 0]), refs[-1], count, deep)
+
+
+def maps_columns(coil_maps, count, first, coils, parts):
     _, _, planes, ny, nz = coil_maps.shape
     deep = nz // count
+    part = deep // parts
     return pl.pallas_call(
         functools.partial(maps_kernel, count, deep),
-        out_shape=jax.ShapeDtypeStruct((count, planes, coils, deep, LANES), BF),
+        out_shape=[jax.ShapeDtypeStruct((count, planes, coils, part, LANES), BF)] * parts,
         grid=(planes, coils),
         in_specs=[pl.BlockSpec((1, 2, 1, ny, nz), lambda x, c: (first + c, 0, x, 0, 0))],
-        out_specs=pl.BlockSpec((count, 1, 1, deep, LANES), lambda x, c: (0, x, c, 0, 0)),
+        out_specs=[pl.BlockSpec((count, 1, 1, part, LANES), lambda x, c: (0, x, c, 0, 0))] * parts,
         scratch_shapes=[pltpu.VMEM((nz, LANES), F32)],
         compiler_params=params(),
         cost_estimate=pl.CostEstimate(
@@ -249,7 +253,7 @@
 def spread(combined, weights, links, planes):
     nx, deep, _ = combined.shape
     blocks = weights.shape[0]
-    pad = max(16, deep)
+    pad = max(8, deep)
     return pl.pallas_call(
         functools.partial(spread_kernel, nx, deep, pad),
         out_shape=jax.ShapeDtypeStruct((nx, deep, LANES), BF),
@@ -340,9 +344,8 @@
     lax.fori_loop(0, nx // group, combine, 0)
 
 
-def coils(maps, warped, mask, tabs, before):
-    nx, deep, _ = warped.shape
-    count = maps.shape[1]
+def coils(maps, warped, mask, tabs, before, part):
+    nx, count, deep, _ = maps.shape
     pad = max(8, deep)
     fresh = before is None
     whole = lambda shape: pl.BlockSpec(
@@ -350,7 +353,11 @@
     )
     in_specs = [pl.BlockSpec((nx, 1, deep, LANES), lambda c: (0, c, 0, 0))]
     args = [maps, warped, mask, *tabs] + ([] if fresh else [before])
-    in_specs += [whole(a.shape) for a in args[1:]]
+    columns = pl.BlockSpec(
+        (nx, deep, LANES), lambda c: (0, part, 0), pipeline_mode=pl.Buffered(1)
+    )
+    in_specs += [columns] + [whole(a.shape) for a in (mask, *tabs)]
+    in_specs += [] if fresh else [columns]
     return pl.pallas_call(
         functools.partial(coil_kernel, nx, deep, pad, fresh),
         out_shape=jax.ShapeDtypeStruct((nx, deep, LANES), F32),
@@ -368,53 +375,53 @@
     )(*args)
 
 
-def update_kernel(count, deep, g_ref, i_ref, a_ref, o_ref, scratch):
-    if deep % 16 == 0:
-        rows = g_ref[:, 0].reshape(count * deep, LANES)
-    else:
+def update_kernel(count, parts, *refs):
+    backs = refs[:parts]
+    i_ref, a_ref, o_ref, scratch = refs[parts:]
+    part = backs[0].shape[2]
+    for h, back in enumerate(backs):
         for d in range(count):
-            scratch[pl.ds(d * deep, deep), :] = g_ref[d, 0].astype(F32)
-        rows = scratch[...]
-    grad = rows.astype(F32).T
+            scratch[pl.ds((d * parts + h) * part, part), :] = back[d, 0].astype(F32)
+    grad = scratch[...].T
     real = jnp.concatenate([grad[0:128], grad[256:320]], axis=0)
     imag = jnp.concatenate([grad[128:256], grad[320:384]], axis=0)
-    for part, value in enumerate((real, imag)):
-        o_ref[part, 0] = i_ref[part, 0] - 0.5 * (value - a_ref[part, 0].astype(F32))
-
-
-def update(back, image, adjoint):
-    count, planes, deep, _ = back.shape
+    for p, value in enumerate((real, imag)):
+        o_ref[p, 0] = i_ref[p, 0] - 0.5 * (value - a_ref[p, 0].astype(F32))
+
+
+def update(backs, image, adjoint):
+    parts = len(backs)
+    count, planes, part, _ = backs[0].shape
     _, _, ny, nz = image.shape
     block = pl.BlockSpec((2, 1, ny, nz), lambda x: (0, x, 0, 0))
-    return pl.pallas_call(
-        functools.partial(update_kernel, count, deep),
+    back = pl.BlockSpec((count, 1, part, LANES), lambda x: (0, x, 0, 0))
+    return pl.pallas_call(
+        functools.partial(update_kernel, count, parts),
         out_shape=jax.ShapeDtypeStruct(image.shape, F32),
         grid=(planes,),
-        in_specs=[
-            pl.BlockSpec((count, 1, deep, LANES), lambda x: (0, x, 0, 0)),
-            block,
-            block,
-        ],
+        in_specs=[back] * parts + [block, block],
         out_specs=block,
         scratch_shapes=[pltpu.VMEM((nz, LANES), F32)],
         compiler_params=params(),
         cost_estimate=pl.CostEstimate(flops=0, bytes_accessed=image.size * 12, transcendentals=0),
         name="update",
-    )(back, image, adjoint)
+    )(*backs, image, adjoint)
 
 
 def exchange(parts):
     return lax.all_to_all(parts, "slab", split_axis=0, concat_axis=0, tiled=True)
 
 
+def after(value, *others):
+    return lax.optimization_barrier((value, *others))[0]
+
+
 def split_coils(total):
     sizes = []
-    left = total
-    while left:
-        size = 1 if left <= 2 else min(3, left - 1)
-        sizes.append(size)
-        left -= size
-    return sizes
+    while total > 1:
+        sizes.append(total // 2)
+        total -= total // 2
+    return sizes + [1]
 
 
 def per_device(image, adjoint_data, coil_maps, masks, sources, weights):
@@ -422,28 +429,56 @@
     planes, ny, nz = image.shape[1:]
     nx = planes * count
     deep = nz // count
+    parts = 2 if deep % 16 == 0 else 1
     tabs = tables(nx, ny)
+    sampled = jnp.pad(masks[0].astype(F32), ((0, 0), (0, HALF - ny)))
+    mask = jnp.concatenate([sampled, sampled], axis=0)
+
     matrices = weights[0].reshape(3 * planes, 2, BLK, BLK)
     matrices = jnp.transpose(matrices, (0, 2, 1, 3)).reshape(3 * planes, BLK, 2 * BLK)
-    matrices = lax.all_gather(matrices, "slab", axis=0, tiled=True)
-    links = lax.all_gather(sources[0], "slab", axis=0, tiled=True).reshape(-1)
-    sampled = jnp.pad(masks[0].astype(F32), ((0, 0), (0, HALF - ny)))
-    mask = jnp.concatenate([sampled, sampled], axis=0)
-
-    columns = exchange(image_columns(image, count)).reshape(nx, deep, LANES)
+    digits = jnp.concatenate([sources[0] // BLK, sources[0] % BLK], axis=1).astype(BF)
+    digits = jnp.pad(digits[:, None, :], ((0, 0), (0, 7), (0, 2 * BLK - 4)))
+    packed = jnp.concatenate([matrices, digits], axis=1)
+    packed = lax.all_gather(packed, "slab", axis=0, tiled=True)
+    digits = packed[:, BLK, :4].astype(jnp.int32)
+    links = (digits[:, :2] * BLK + digits[:, 2:]).reshape(-1)
+
+    columns = exchange(image_columns(image, count))
     sizes = split_coils(coil_maps.shape[0])
-    sent, first = [], 0
-    for size in sizes:
-        sent.append(exchange(maps_columns(coil_maps, count, first, size)))
+    outgoing, first = [], 0
+    for i, size in enumerate(sizes):
+        cut = parts if i == len(sizes) - 1 else 1
+        pieces = maps_columns(coil_maps, count, first, size, cut)
+        outgoing += [(size, h if cut > 1 else 0, piece) for h, piece in enumerate(pieces)]
         first += size
-    warped = warp(columns, matrices, links, planes)
-    combined = None
-    for size, part in zip(sizes, sent):
-        maps = part.reshape(nx, size, deep, LANES)
-        combined = coils(maps, warped, mask, tabs, combined)
-    grad = spread(combined, matrices, links, planes)
-    back = exchange(grad.reshape(count, planes, deep, LANES))
-    return update(back, image, adjoint_data)
+    whole = len(sizes) - 1 if parts > 1 else len(sizes)
+
+    before = columns
+    columns = columns.reshape(nx, deep, LANES)
+    warped = warp(columns, packed, links, planes)
+    received, done, combined, backs, grad = [], [], None, [], None
+    for k, (size, h, piece) in enumerate(outgoing):
+        needs = [before] + (done[k - 2 : k - 1] if k >= 2 else [])
+        before = exchange(after(piece, *needs))
+        received.append((size, h, before))
+        if k >= 1:
+            size, h, got = received[k - 1]
+            combined_k = coils(
+                got.reshape(nx, size, -1, LANES), warped, mask, tabs, combined, h
+            )
+            done.append(combined_k)
+            if k - 1 < whole:
+                combined = combined_k
+            else:
+                grad = spread(combined_k, packed, links, planes)
+                backs.append(exchange(after(grad, before).reshape(count, planes, -1, LANES)))
+    size, h, got = received[-1]
+    if grad is not None:
+        got = after(got, grad)
+    combined = coils(got.reshape(nx, size, -1, LANES), warped, mask, tabs, combined, h)
+    grad = spread(combined, packed, links, planes)
+    backs.append(exchange(grad.reshape(count, planes, -1, LANES)))
+    return update(backs, image, adjoint_data)
 
 
 def solution(mesh):

time: 894 us -> 801 us (0.90)
  blocking collectives: 215 us -> 32.4 us
  waiting for transfers between devices: 261 us -> 301 us
  Pallas kernels: 365 us -> 396 us
  starting transfers between devices: 26.3 us -> 40.6 us
    all_gather x1 -> x0, blocking collectives: 156 us -> none  [per_device(): links = lax.all_gather(sources[0], 'slab', axis=0, tiled=True).reshape(-1)]
    all_to_all x5 -> x7, waiting for transfers between devices: 261 us -> 301 us  [exchange(): lax.all_to_all(parts, 'slab', split_axis=0, concat_axis=0, tiled=True)]
    pallas_call x1 -> x2, Pallas kernels: 33.7 us -> 62.3 us  [spread(): pl.pallas_call(functools.partial(spread_kernel, nx, deep, pad), out_shape...]
    all_to_all x1, blocking collectives: 59 us -> 32.4 us  [exchange(): lax.all_to_all(parts, 'slab', split_axis=0, concat_axis=0, tiled=True)]
    all_to_all x5 -> x7, starting transfers between devices: 26.3 us -> 40.5 us  [exchange(): lax.all_to_all(parts, 'slab', split_axis=0, concat_axis=0, tiled=True)]
    pallas_call x4 -> x5, Pallas kernels: 220 us -> 224 us  [coils(): pl.pallas_call(functools.partial(coil_kernel, nx, deep, pad, fresh), out_...]
  transfers between devices with their start and end apart: 6 -> 8, of which waited for: 3 -> 3; matrix products, arithmetic and copies ran while one was open for 1% -> 1% of each run, Pallas kernels for 32% -> 41%
where the time goes in v2:
time: 801 us; the launch traced here: 795 us
  Pallas kernels  396 us (49%)
  waiting for transfers between devices  301 us (38%)
  starting transfers between devices  40.6 us (5%)
  blocking collectives  32.4 us (4%)
  between operations  13.5 us (2%)
    all_to_all x7, waiting for transfers between devices, exchange(): lax.all_to_all(parts, 'slab', split_axis=0, concat_axis=0, tiled=True)  301 us
    pallas_call x5, Pallas kernels, coils(): pl.pallas_call(functools.partial(coil_kernel, nx, deep, pad, fresh), out_...  224 us
    pallas_call x2, Pallas kernels, spread(): pl.pallas_call(functools.partial(spread_kernel, nx, deep, pad), out_shape...  62.3 us
    pallas_call x4, Pallas kernels, maps_columns(): pl.pallas_call(functools.partial(maps_kernel, count, deep), out_shape=[ja...  60.9 us
    all_to_all x7, starting transfers between devices, exchange(): lax.all_to_all(parts, 'slab', split_axis=0, concat_axis=0, tiled=True)  40.5 us
    all_to_all x1, blocking collectives, exchange(): lax.all_to_all(parts, 'slab', split_axis=0, concat_axis=0, tiled=True)  32.4 us
    pallas_call x1, Pallas kernels, warp(): pl.pallas_call(functools.partial(warp_kernel, nx, deep, pad), out_shape=j...  31.2 us
  transfers between devices with their start and end apart: 8, of which 3 were waited for; matrix products, arithmetic and copies ran while one was open for 1% of the time, Pallas kernels for 41%

profile of v2, /device:TPU:13, one launch (start us, length us, event | category | flops | bytes accessed | tf_op | source)
XLA Modules:
  0.0 795.1 jit_solution(373541200016228842)
XLA Ops:
  6.5 8.5 %image_columns.1 = bf16[16,12,16,384]{3,2,1,0:T(8,128)(2,1)} custom-call(f32[2,12,192,256]{3,2,1,0:T(8,128)} %refs_2_.1), custom_call_target="tpu_custom_call" | custom-call | bytes 7077888 | tf_op jit(solution)/shard_map/image_columns/pallas_call | solution.py:81
  15.0 6.6 all-to-all-start
  21.6 29.2 %maps_columns.7 = bf16[16,12,4,16,384]{4,3,2,1,0:T(8,128)(2,1)} custom-call(bf16[8,2,12,192,256]{4,3,2,1,0:T(8,128)(2,1)} %x_ref.8), custom_call_target="tpu_custom_call" | custom-call | bytes 18874368 | tf_op jit(solution)/shard_map/maps_columns/pallas_call | solution.py:103
  50.8 23.8 %all-to-all-done = bf16[16,12,16,384]{3,2,1,0:T(8,128)(2,1)S(1)} async-done(((bf16[16,12,16,384]{3,2,1,0:T(8,128)(2,1)}), bf16[16,12,16,384]{3,2,1,0:T(8,128)(2,1)S(1)}, u32[]{:S(2)}, u32[]{:S(2)}) %all-to-all-start) | async-done | bytes 2359328 | tf_op jit(solution)/shard_map/all_to_all | solution.py:412
  74.6 1.4 copy-done
  76.0 4.9 all-to-all-start.1
  80.9 0.0 all-gather.2.cloned.1.call-start
  81.0 0.0 copy-done.8
  81.0 0.1 copy.18
  81.1 0.0 copy-done.6
  81.1 1.3 reshape_squeeze.3
  82.4 1.2 copy.20
  83.6 0.5 reshape.64
  84.2 0.9 fusion.1
  85.1 0.0 all-gather.2.cloned.1.call-update
  85.1 15.2 %maps_columns.6 = bf16[16,12,2,16,384]{4,3,2,1,0:T(8,128)(2,1)} custom-call(bf16[8,2,12,192,256]{4,3,2,1,0:T(8,128)(2,1)} %x_ref.8), custom_call_target="tpu_custom_call" | custom-call | bytes 9437184 | tf_op jit(solution)/shard_map/maps_columns/pallas_call | solution.py:103
  100.3 249.4 %all-to-all-done.1 = bf16[16,12,4,16,384]{4,3,2,1,0:T(8,128)(2,1)} async-done(((bf16[16,12,4,16,384]{4,3,2,1,0:T(8,128)(2,1)}), bf16[16,12,4,16,384]{4,3,2,1,0:T(8,128)(2,1)}, u32[]{:S(2)}, u32[]{:S(2)}) %all-to-all-start.1) | async-done | bytes 9437216 | tf_op jit(solution)/shard_map/all_to_all | solution.py:412
  349.7 4.9 all-to-all-start.2
  354.6 8.2 %maps_columns.5 = bf16[16,12,1,16,384]{4,3,2,1,0:T(8,128)(2,1)} custom-call(bf16[8,2,12,192,256]{4,3,2,1,0:T(8,128)(2,1)} %x_ref.8), custom_call_target="tpu_custom_call" | custom-call | bytes 4718592 | tf_op jit(solution)/shard_map/maps_columns/pallas_call | solution.py:103
  362.8 0.0 copy-done.7
  362.9 0.8 pad_maximum_fusion.refs_2_
  363.7 1.5 slice_convert_fusion
  365.2 0.1 slice_add_fusion
  365.3 0.8 reshape.65.links
  366.1 31.2 %warp.1.refs_1_ = f32[192,16,384]{2,1,0:T(8,128)} custom-call(s32[1152]{0:T(1024)} %reshape.65.links, bf16[192,16,384]{2,1,0:T(8,128)(2,1)} %bitcast.42, bf16[576,72,128]{2,1,0:T(8,128)(2,1)} %all-gather.2.cloned.1.call-done.w_ref), custom_call_target="tpu_custom_call" | custom-call | flops 2415919104 | bytes 20971520 | tf_op jit(solution)/shard_map/warp/pallas_call | solution.py:174
  397.3 101.8 %coils.5.refs_7_ = f32[192,16,384]{2,1,0:T(8,128)} custom-call(bf16[192,4,16,384]{3,2,1,0:T(8,128)(2,1)} %bitcast.5.refs_0_, f32[192,16,384]{2,1,0:T(8,128)} %warp.1.refs_1_, f32[384,256]{1,0:T(8,128)} %pad_maximum_fusion.refs_2_, bf16[384,512]{1,0:T(8,128)(2,1)} %constant.42.clone.refs_3_, bf16[384,384]{1,0:T(8,128)(2,1)} %constant.43.clone.refs_4_, ...), custom_call_target="tpu_custom_call" | custom-call | flops 28991029248 | bytes 24117248 | tf_op jit(solution)/shard_map/coils/pallas_call | solution.py:361
  499.1 0.0 all-to-all-done.2
  499.1 6.0 all-to-all-start.3
  505.1 8.3 %maps_columns.4 = (bf16[16,12,1,8,384]{4,3,2,1,0:T(8,128)(2,1)}, bf16[16,12,1,8,384]{4,3,2,1,0:T(8,128)(2,1)}) custom-call(bf16[8,2,12,192,256]{4,3,2,1,0:T(8,128)(2,1)} %x_ref.8), custom_call_target="tpu_custom_call" | custom-call | bytes 4718592 | tf_op jit(solution)/shard_map/maps_columns/pallas_call | solution.py:103
  513.4 55.3 %coils.6.refs_7_ = f32[192,16,384]{2,1,0:T(8,128)} custom-call(bf16[192,2,16,384]{3,2,1,0:T(8,128)(2,1)} %bitcast.8.refs_0_, f32[192,16,384]{2,1,0:T(8,128)} %warp.1.refs_1_, f32[384,256]{1,0:T(8,128)} %pad_maximum_fusion.refs_2_, bf16[384,512]{1,0:T(8,128)(2,1)} %constant.42.clone.refs_3_, bf16[384,384]{1,0:T(8,128)(2,1)} %constant.43.clone.refs_4_, ...), custom_call_target="tpu_custom_call" | custom-call | flops 14495514624 | bytes 19398656 | tf_op jit(solution)/shard_map/coils/pallas_call | solution.py:361
  568.7 0.0 all-to-all-done.3
  568.7 1.4 copy-done.5
  570.1 6.0 all-to-all-start.4
  576.1 31.5 %coils.7.refs_7_ = f32[192,16,384]{2,1,0:T(8,128)} custom-call(bf16[192,1,16,384]{3,2,1,0:T(8,128)(2,1)} %bitcast.49, f32[192,16,384]{2,1,0:T(8,128)} %warp.1.refs_1_, f32[384,256]{1,0:T(8,128)} %pad_maximum_fusion.refs_2_, bf16[384,512]{1,0:T(8,128)(2,1)} %constant.42.clone.refs_3_, bf16[384,384]{1,0:T(8,128)(2,1)} %constant.43.clone.refs_4_, ...), custom_call_target="tpu_custom_call" | custom-call | flops 7247757312 | bytes 17039360 | tf_op jit(solution)/shard_map/coils/pallas_call | solution.py:361
  607.6 0.0 all-to-all-done.4
  607.7 6.0 all-to-all-start.5
  613.7 17.5 %coils.8.c_ref = f32[192,8,384]{2,1,0:T(8,128)} custom-call(bf16[192,1,8,384]{3,2,1,0:T(8,128)(2,1)} %bitcast.45, f32[192,16,384]{2,1,0:T(8,128)} %warp.1.refs_1_, f32[384,256]{1,0:T(8,128)} %pad_maximum_fusion.refs_2_, bf16[384,512]{1,0:T(8,128)(2,1)} %constant.42.clone.refs_3_, bf16[384,384]{1,0:T(8,128)(2,1)} %constant.43.clone.refs_4_, ...), custom_call_target="tpu_custom_call" | custom-call | flops 3623878656 | bytes 15859712 | tf_op jit(solution)/shard_map/coils/pallas_call | solution.py:361
  631.1 31.1 %spread.2 = bf16[192,8,384]{2,1,0:T(8,128)(2,1)} custom-call(s32[1152]{0:T(1024)} %reshape.65.links, f32[192,8,384]{2,1,0:T(8,128)} %coils.8.c_ref, bf16[576,72,128]{2,1,0:T(8,128)(2,1)} %all-gather.2.cloned.1.call-done.w_ref), custom_call_target="tpu_custom_call" | custom-call | flops 2415919104 | bytes 20971520 | tf_op jit(solution)/shard_map/spread/pallas_call | solution.py:257
  662.3 0.0 all-to-all-done.5
  662.3 1.0 copy-done.2
  663.3 17.5 %coils.9.c_ref = f32[192,8,384]{2,1,0:T(8,128)} custom-call(bf16[192,1,8,384]{3,2,1,0:T(8,128)(2,1)} %bitcast.44, f32[192,16,384]{2,1,0:T(8,128)} %warp.1.refs_1_, f32[384,256]{1,0:T(8,128)} %pad_maximum_fusion.refs_2_, bf16[384,512]{1,0:T(8,128)(2,1)} %constant.42.clone.refs_3_, bf16[384,384]{1,0:T(8,128)(2,1)} %constant.43.clone.refs_4_, ...), custom_call_target="tpu_custom_call" | custom-call | flops 3623878656 | bytes 15859712 | tf_op jit(solution)/shard_map/coils/pallas_call | solution.py:361
  680.8 31.1 %spread.3 = bf16[192,8,384]{2,1,0:T(8,128)(2,1)} custom-call(s32[1152]{0:T(1024)} %reshape.65.links, f32[192,8,384]{2,1,0:T(8,128)} %coils.9.c_ref, bf16[576,72,128]{2,1,0:T(8,128)(2,1)} %all-gather.2.cloned.1.call-done.w_ref), custom_call_target="tpu_custom_call" | custom-call | flops 2415919104 | bytes 20971520 | tf_op jit(solution)/shard_map/spread/pallas_call | solution.py:257
  711.9 6.1 all-to-all-start.7
  718.1 27.8 %all-to-all-done.7.refs_1_ = bf16[16,12,8,384]{3,2,1,0:T(8,128)(2,1)S(1)} async-done(((bf16[16,12,8,384]{3,2,1,0:T(8,128)(2,1)}), bf16[16,12,8,384]{3,2,1,0:T(8,128)(2,1)S(1)}, u32[]{:S(2)}, u32[]{:S(2)}) %all-to-all-start.7) | async-done | bytes 1179680 | tf_op jit(solution)/shard_map/all_to_all | solution.py:412
  745.8 0.0 copy-done.1
  745.8 32.4 %all_to_all.40.refs_0_ = bf16[16,12,8,384]{3,2,1,0:T(8,128)(2,1)} all-to-all(bf16[16,12,8,384]{3,2,1,0:T(8,128)(2,1)S(1)} %bitcast.43), channel_id=1, replica_groups=mesh['grp'=2,'slab'=16] {'slab'}, dimensions={0} | all-to-all | bytes 2359296 | tf_op jit(solution)/shard_map/all_to_all | solution.py:412
  778.2 0.0 copy-done.4
  778.2 10.0 %update.1 = f32[2,12,192,256]{3,2,1,0:T(8,128)} custom-call(bf16[16,12,8,384]{3,2,1,0:T(8,128)(2,1)} %all_to_all.40.refs_0_, bf16[16,12,8,384]{3,2,1,0:T(8,128)(2,1)} %copy-done.4, f32[2,12,192,256]{3,2,1,0:T(8,128)} %refs_2_.1, bf16[2,12,192,256]{3,2,1,0:T(8,128)(2,1)} %refs_3_.6), custom_call_target="tpu_custom_call" | custom-call | bytes 14155776 | tf_op jit(solution)/shard_map/update/pallas_call | solution.py:398
  (15 shorter events, 0.1 us)
Async XLA Ops:
  15.0 59.6 %all-to-all-start = ((bf16[16,12,16,384]{3,2,1,0:T(8,128)(2,1)}), bf16[16,12,16,384]{3,2,1,0:T(8,128)(2,1)S(1)}, u32[]{:S(2)}, u32[]{:S(2)}) async-start(bf16[16,12,16,384]{3,2,1,0:T(8,128)(2,1)} %image_columns.1), calls=%async_computation | async-start | bytes 4718592 | tf_op jit(solution)/shard_map/all_to_all | solution.py:412
  50.8 30.2 %copy-start.8 = (s32[1,36,2]{1,2,0:T(2,128)S(1)}, s32[1,36,2]{1,2,0:T(2,128)}, u32[]{:S(2)}) copy-start(s32[1,36,2]{1,2,0:T(2,128)} %param.14) | copy-start | bytes 868
  50.8 30.3 %copy-start.6 = (bf16[1,36,8192]{2,1,0:T(8,128)(2,1)S(1)}, bf16[1,36,8192]{2,1,0:T(8,128)(2,1)}, u32[]{:S(2)}) copy-start(bf16[1,36,8192]{2,1,0:T(8,128)(2,1)} %param.15) | copy-start | bytes 1769476
  74.6 1.4 copy-start
  76.0 273.7 %all-to-all-start.1 = ((bf16[16,12,4,16,384]{4,3,2,1,0:T(8,128)(2,1)}), bf16[16,12,4,16,384]{4,3,2,1,0:T(8,128)(2,1)}, u32[]{:S(2)}, u32[]{:S(2)}) async-start(bf16[16,12,4,16,384]{4,3,2,1,0:T(8,128)(2,1)} %maps_columns.7), calls=%async_computation.1 | async-start | bytes 18874368 | tf_op jit(solution)/shard_map/all_to_all | solution.py:412
  80.9 282.7 %all-gather.2.cloned.1.call-start = ((), (), s32[]{:S(2)}) async-start(), calls=%async_computation.8 | async-start | bytes 11280384 | tf_op jit(solution)/shard_map/all_gather | solution.py:442
  349.7 149.4 %all-to-all-start.2 = ((bf16[16,12,2,16,384]{4,3,2,1,0:T(8,128)(2,1)}), bf16[16,12,2,16,384]{4,3,2,1,0:T(8,128)(2,1)}, u32[]{:S(2)}, u32[]{:S(2)}) async-start(bf16[16,12,2,16,384]{4,3,2,1,0:T(8,128)(2,1)} %maps_columns.6), calls=%async_computation.2 | async-start | bytes 9437184 | tf_op jit(solution)/shard_map/all_to_all | solution.py:412
  354.6 8.2 %copy-start.7 = (s32[1,192,192]{2,1,0:T(8,128)S(1)}, s32[1,192,192]{2,1,0:T(8,128)}, u32[]{:S(2)}) copy-start(s32[1,192,192]{2,1,0:T(8,128)} %param.13) | copy-start | bytes 442372
  499.1 69.6 %all-to-all-start.3 = ((bf16[16,12,1,16,384]{4,3,2,1,0:T(8,128)(2,1)}), bf16[16,12,1,16,384]{4,3,2,1,0:T(8,128)(2,1)S(1)}, u32[]{:S(2)}, u32[]{:S(2)}) async-start(bf16[16,12,1,16,384]{4,3,2,1,0:T(8,128)(2,1)} %maps_columns.5), calls=%async_computation.3 | async-start | bytes 4718592 | tf_op jit(solution)/shard_map/all_to_all | solution.py:412
  568.7 1.4 copy-start.5
  570.1 37.5 %all-to-all-start.4 = ((bf16[16,12,1,8,384]{4,3,2,1,0:T(8,128)(2,1)}), bf16[16,12,1,8,384]{4,3,2,1,0:T(8,128)(2,1)S(1)}, u32[]{:S(2)}, u32[]{:S(2)}) async-start(bf16[16,12,1,8,384]{4,3,2,1,0:T(8,128)(2,1)} %get-tuple-element.18), calls=%async_computation.4 | async-start | bytes 2359296 | tf_op jit(solution)/shard_map/all_to_all | solution.py:412
  607.6 6.0 copy-start.3
  607.7 54.6 %all-to-all-start.5 = ((bf16[16,12,1,8,384]{4,3,2,1,0:T(8,128)(2,1)}), bf16[16,12,1,8,384]{4,3,2,1,0:T(8,128)(2,1)S(1)}, u32[]{:S(2)}, u32[]{:S(2)}) async-start(bf16[16,12,1,8,384]{4,3,2,1,0:T(8,128)(2,1)} %get-tuple-element.20), calls=%async_computation.5 | async-start | bytes 2359296 | tf_op jit(solution)/shard_map/all_to_all | solution.py:412
  662.3 1.0 copy-start.2
  711.9 33.9 %copy-start.1 = (bf16[192,8,384]{2,1,0:T(8,128)(2,1)S(1)}, bf16[192,8,384]{2,1,0:T(8,128)(2,1)}, u32[]{:S(2)}) copy-start(bf16[192,8,384]{2,1,0:T(8,128)(2,1)} %spread.2) | copy-start | bytes 3538948
  711.9 33.9 %all-to-all-start.7 = ((bf16[16,12,8,384]{3,2,1,0:T(8,128)(2,1)}), bf16[16,12,8,384]{3,2,1,0:T(8,128)(2,1)S(1)}, u32[]{:S(2)}, u32[]{:S(2)}) async-start(bf16[16,12,8,384]{3,2,1,0:T(8,128)(2,1)} %bitcast.46), calls=%async_computation.7 | async-start | bytes 2359296 | tf_op jit(solution)/shard_map/all_to_all | solution.py:412
  745.8 32.4 %copy-start.4 = (bf16[16,12,8,384]{3,2,1,0:T(8,128)(2,1)}, bf16[16,12,8,384]{3,2,1,0:T(8,128)(2,1)S(1)}, u32[]{:S(2)}) copy-start(bf16[16,12,8,384]{3,2,1,0:T(8,128)(2,1)S(1)} %all-to-all-done.7.refs_1_) | copy-start | bytes 3538948
Sparse Core Ops, SparseCore 0:
  85.2 220.5 all-gather.1

commit v3 on v2

v3 whole, which is shorter than its diff:
```python
import functools
import math

import jax
import jax.numpy as jnp
import numpy as np
from jax import lax
from jax.experimental import pallas as pl
from jax.experimental.pallas import tpu as pltpu
from jax.sharding import PartitionSpec as P

BLK = 64
LANES = 384
HALF = 256
VMEM_LIMIT = 56 * 1024 * 1024
BF = jnp.bfloat16
F32 = jnp.float32


def lane_order(length):
    lo, rest = 128, length - 128
    part = np.concatenate([np.zeros(lo), np.ones(lo), np.zeros(rest), np.ones(rest)])
    pos = np.concatenate([np.arange(lo), np.arange(lo), lo + np.arange(rest), lo + np.arange(rest)])
    return part.astype(np.int32), pos.astype(np.int32)


def dft_table(length, direction):
    positions = np.arange(length)
    phases = (positions[:, None] * positions[None, :] % length).astype(np.float32)
    phases = phases * np.float32(2.0 * math.pi / length)
    factor = np.float32(1.0 / math.sqrt(length))
    cosine = np.cos(phases) * factor
    sine = np.sin(phases) * (np.float32(direction) * factor)
    upper = np.stack([cosine, -sine], axis=1)
    lower = np.stack([sine, cosine], axis=1)
    return np.stack([upper, lower], axis=0)


def tables(nx, ny):
    part, pos = lane_order(ny)
    fwd_y, inv_y = dft_table(ny, -1.0), dft_table(ny, 1.0)
    into_y = np.zeros((2 * ny, 2, HALF), np.float32)
    into_y[:, :, :ny] = np.transpose(fwd_y[:, :, part, pos], (2, 0, 1))
    from_y = np.zeros((2, HALF, 2 * ny), np.float32)
    from_y[:, :ny, :] = np.transpose(inv_y[part, pos], (1, 2, 0))
    fwd_x = dft_table(nx, -1.0).reshape(2 * nx, 2 * nx)
    inv_x = dft_table(nx, 1.0).reshape(2 * nx, 2 * nx)
    out = (into_y.reshape(2 * ny, 2 * HALF), fwd_x, inv_x, from_y.reshape(2 * HALF, 2 * ny))
    return tuple(jnp.asarray(t, BF) for t in out)


def params():
    return pltpu.CompilerParams(vmem_limit_bytes=VMEM_LIMIT)


def to_rows(parts):
    stacked = jnp.concatenate(
        [parts[0, :128], parts[1, :128], parts[0, 128:], parts[1, 128:]], axis=0
    )
    return stacked.T


def spread_rows(outs, rows, scratch, count, deep):
    if len(outs) == 1 and deep % 16 == 0:
        outs[0][...] = rows.reshape(count, deep, LANES)
        return
    part = deep // len(outs)
    scratch[...] = rows.astype(F32)
    for h, out in enumerate(outs):
        for d in range(count):
            out[d] = scratch[pl.ds(d * deep + h * part, part), :].astype(BF)


def image_kernel(count, deep, x_ref, o_ref, scratch):
    for x in range(x_ref.shape[1]):
        rows = to_rows(x_ref[:, x].astype(BF))
        spread_rows([o_ref.at[:, x]], rows, scratch, count, deep)


def image_columns(image, count):
    _, planes, ny, nz = image.shape
    deep = nz // count
    group = 3 if planes % 3 == 0 else 1
    return pl.pallas_call(
        functools.partial(image_kernel, count, deep),
        out_shape=jax.ShapeDtypeStruct((count, planes, deep, LANES), BF),
        grid=(planes // group,),
        in_specs=[pl.BlockSpec((2, group, ny, nz), lambda x: (0, x, 0, 0))],
        out_specs=pl.BlockSpec((count, group, deep, LANES), lambda x: (0, x, 0, 0)),
        scratch_shapes=[pltpu.VMEM((nz, LANES), F32)],
        compiler_params=params(),
        cost_estimate=pl.CostEstimate(flops=0, bytes_accessed=image.size * 6, transcendentals=0),
        name="image_columns",
    )(image)


def maps_kernel(count, deep, x_ref, o_ref, scratch):
    spread_rows([o_ref.at[:, 0, 0]], to_rows(x_ref[0, :, 0]), scratch, count, deep)


def last_maps_kernel(count, deep, x_ref, both_ref, first_ref, second_ref, scratch):
    part = deep // 2
    scratch[...] = to_rows(x_ref[0, :, 0]).astype(F32)
    coil = pl.program_id(1)
    for d in range(count):
        both_ref[d, 0, 0] = scratch[pl.ds(d * deep, part), :].astype(BF)

    def rest(out):
        for d in range(count):
            out[d, 0, 0] = scratch[pl.ds(d * deep + part, part), :].astype(BF)

    @pl.when(coil == 0)
    def _():
        rest(first_ref)

    @pl.when(coil == 1)
    def _():
        rest(second_ref)


def maps_columns(coil_maps, count, first, coils):
    _, _, planes, ny, nz = coil_maps.shape
    deep = nz // count
    return pl.pallas_call(
        functools.partial(maps_kernel, count, deep),
        out_shape=jax.ShapeDtypeStruct((count, planes, coils, deep, LANES), BF),
        grid=(planes, coils),
        in_specs=[pl.BlockSpec((1, 2, 1, ny, nz), lambda x, c: (first + c, 0, x, 0, 0))],
        out_specs=pl.BlockSpec((count, 1, 1, deep, LANES), lambda x, c: (0, x, c, 0, 0)),
        scratch_shapes=[pltpu.VMEM((nz, LANES), F32)],
        compiler_params=params(),
        cost_estimate=pl.CostEstimate(
            flops=0, bytes_accessed=coils * 2 * planes * ny * nz * 4, transcendentals=0
        ),
        name="maps_columns",
    )(coil_maps)


def last_maps_columns(coil_maps, count, first):
    _, _, planes, ny, nz = coil_maps.shape
    deep = nz // count
    part = deep // 2
    shapes = [(count, planes, coils, part, LANES) for coils in (2, 1, 1)]
    alone = pl.BlockSpec((count, 1, 1, part, LANES), lambda x, c: (0, x, 0, 0, 0))
    return pl.pallas_call(
        functools.partial(last_maps_kernel, count, deep),
        out_shape=[jax.ShapeDtypeStruct(shape, BF) for shape in shapes],
        grid=(planes, 2),
        in_specs=[pl.BlockSpec((1, 2, 1, ny, nz), lambda x, c: (first + c, 0, x, 0, 0))],
        out_specs=[
            pl.BlockSpec((count, 1, 1, part, LANES), lambda x, c: (0, x, c, 0, 0)),
            alone,
            alone,
        ],
        scratch_shapes=[pltpu.VMEM((nz, LANES), F32)],
        compiler_params=params(),
        cost_estimate=pl.CostEstimate(
            flops=0, bytes_accessed=4 * planes * ny * nz * 4, transcendentals=0
        ),
        name="last_maps_columns",
    )(coil_maps)


def low_half(shape):
    return lax.broadcasted_iota(jnp.int32, shape, len(shape) - 1) < BLK


def fetch(w_hbm, held, sems, k):
    size = held.shape[0] // sems.shape[0]
    at = pl.ds(k * size, size)
    return pltpu.make_async_copy(w_hbm.at[at, pl.ds(0, BLK), :], held.at[at], sems.at[k])


def fetch_all(w_hbm, held, sems):
    for k in range(sems.shape[0]):
        fetch(w_hbm, held, sems, k).start()


def warp_kernel(nx, deep, pad, links, owner, g_ref, w_hbm, o_ref, held, twice, sems):
    fetch_all(w_hbm, held, sems)
    count = sems.shape[0]
    planes = nx // count
    low = low_half((deep, 128))

    def split(x, carry):
        for v in range(3):
            row = g_ref[x, :, v * 128 : (v + 1) * 128].astype(F32)
            turned = pltpu.roll(row, BLK, 1)
            first = jnp.where(low, row, turned).astype(BF)
            second = jnp.where(low, turned, row).astype(BF)
            if v < 2:
                twice[3 * x, pl.ds(v * pad, deep), :] = first
                twice[3 * x + 1, pl.ds(v * pad, deep), :] = second
            else:
                twice[3 * x + 2, pl.ds(0, deep), :] = first
                twice[3 * x + 2, pl.ds(pad, deep), :] = second
        return carry

    lax.fori_loop(0, nx, split, 0, unroll=8)
    low_both = low_half((2 * pad, 128))

    def block(k, carry):
        fetch(w_hbm, held, sems, k).wait()
        row = owner[k] * planes
        start = k * 3 * planes
        for x in range(planes):
            outs = []
            for b in range(3):
                t = start + 3 * x + b
                both = jnp.where(low_both, twice[links[2 * t]], twice[links[2 * t + 1]])
                outs.append(
                    lax.dot_general(
                        both, held[t], (((1,), (1,)), ((), ())), preferred_element_type=F32
                    )
                )
            a, b, c = outs
            re = jnp.concatenate([a[:deep], b[:deep]], axis=1)
            im = jnp.concatenate([a[pad : pad + deep], b[pad : pad + deep]], axis=1)
            rest = jnp.concatenate([c[:deep], c[pad : pad + deep]], axis=1)
            o_ref[row + x, :, 0:128] = re
            o_ref[row + x, :, 128:256] = im
            o_ref[row + x, :, 256:384] = rest
        return carry

    lax.fori_loop(0, count, block, 0)


def warp(columns, weights, links, owner):
    nx, deep, _ = columns.shape
    blocks = weights.shape[0]
    pad = max(16, deep)
    whole = pl.BlockSpec((nx, deep, LANES), lambda i, l, p: (0, 0, 0))
    return pl.pallas_call(
        functools.partial(warp_kernel, nx, deep, pad),
        out_shape=jax.ShapeDtypeStruct((nx, deep, LANES), F32),
        grid_spec=pltpu.PrefetchScalarGridSpec(
            num_scalar_prefetch=2,
            grid=(1,),
            in_specs=[whole, pl.BlockSpec(memory_space=pl.ANY)],
            out_specs=whole,
            scratch_shapes=[
                pltpu.VMEM((blocks, BLK, 2 * BLK), BF),
                pltpu.VMEM((blocks, 2 * pad, 128), BF),
                pltpu.SemaphoreType.DMA((owner.shape[0],)),
            ],
        ),
        compiler_params=params(),
        cost_estimate=pl.CostEstimate(
            flops=2 * blocks * 256 * 256 * 32, bytes_accessed=20 << 20, transcendentals=0
        ),
        name="warp",
    )(links, owner, columns, weights)


def spread_kernel(nx, deep, pad, links, owner, c_ref, w_hbm, o_ref, held, total, sems):
    fetch_all(w_hbm, held, sems)
    count = sems.shape[0]
    planes = nx // count

    def clear(i, carry):
        total[pl.ds(i * 3, 3)] = jnp.zeros((3, 2 * pad, 128), F32)
        return carry

    lax.fori_loop(0, nx, clear, 0, unroll=8)
    low = low_half((2 * pad, 128))

    def tall(a, b):
        if deep == pad:
            return jnp.concatenate([a, b], axis=0)
        fill = jnp.zeros((pad - deep, a.shape[1]), a.dtype)
        return jnp.concatenate([a, fill, b, fill], axis=0)

    def block(k, carry):
        fetch(w_hbm, held, sems, k).wait()
        row = owner[k] * planes
        start = k * 3 * planes
        for x in range(planes):
            re, im, rest = (c_ref[row + x, :, v * 128 : (v + 1) * 128] for v in range(3))
            tiles = (
                tall(re[:, :BLK], im[:, :BLK]),
                tall(re[:, BLK:], im[:, BLK:]),
                tall(rest[:, :BLK], rest[:, BLK:]),
            )
            for b in range(3):
                t = start + 3 * x + b
                out = jnp.dot(tiles[b].astype(BF), held[t], preferred_element_type=F32)
                zero = jnp.zeros_like(out)
                total[links[2 * t]] += jnp.where(low, out, zero)
                total[links[2 * t + 1]] += jnp.where(low, zero, out)
        return carry

    lax.fori_loop(0, count, block, 0)
    low_row = low_half((deep, 128))

    def gather(x, carry):
        sums = []
        for b in range(3):
            value = total[3 * x + b]
            sums.append(value + pltpu.roll(value, BLK, 1))
        a, b, c = sums
        o_ref[x, :, 0:128] = jnp.where(low_row, a[:deep], b[:deep]).astype(BF)
        o_ref[x, :, 128:256] = jnp.where(
            low_row, a[pad : pad + deep], b[pad : pad + deep]
        ).astype(BF)
        o_ref[x, :, 256:384] = jnp.where(low_row, c[:deep], c[pad : pad + deep]).astype(BF)
        return carry

    lax.fori_loop(0, nx, gather, 0, unroll=8)


def spread(combined, weights, links, owner):
    nx, deep, _ = combined.shape
    blocks = weights.shape[0]
    pad = max(8, deep)
    whole = pl.BlockSpec((nx, deep, LANES), lambda i, l, p: (0, 0, 0))
    return pl.pallas_call(
        functools.partial(spread_kernel, nx, deep, pad),
        out_shape=jax.ShapeDtypeStruct((nx, deep, LANES), BF),
        grid_spec=pltpu.PrefetchScalarGridSpec(
            num_scalar_prefetch=2,
            grid=(1,),
            in_specs=[whole, pl.BlockSpec(memory_space=pl.ANY)],
            out_specs=whole,
            scratch_shapes=[
                pltpu.VMEM((blocks, BLK, 2 * BLK), BF),
                pltpu.VMEM((blocks, 2 * pad, 128), F32),
                pltpu.SemaphoreType.DMA((owner.shape[0],)),
            ],
        ),
        compiler_params=params(),
        cost_estimate=pl.CostEstimate(
            flops=2 * blocks * 256 * 256 * 32, bytes_accessed=20 << 20, transcendentals=0
        ),
        name="spread",
    )(links, owner, combined, weights)


def coil_kernel(nx, deep, pad, fresh, *refs):
    if fresh:
        s_ref, w_ref, mask, iy, fx, bx, oy, o_ref, rows = refs
    else:
        s_ref, w_ref, mask, iy, fx, bx, oy, before, o_ref, rows = refs
    group = 8 if nx % 8 == 0 else 1
    cube = rows.reshape(3, nx, pad, 128)
    low = low_half((group, deep, 128))

    def thirds(ref, at):
        return tuple(ref[at, :, v * 128 : (v + 1) * 128].astype(F32) for v in range(3))

    def expand(i, carry):
        at = pl.ds(i * group, group)
        s0, s1, s2 = thirds(s_ref.at[:, 0], at)
        w0, w1, w2 = thirds(w_ref, at)
        turned = pltpu.roll(s2, BLK, 2)
        other = pltpu.roll(w2, BLK, 2)
        real = jnp.where(low, s2, turned)
        imag = jnp.where(low, turned, s2)
        cube[0, at, pl.ds(0, deep), :] = s0 * w0 - s1 * w1
        cube[1, at, pl.ds(0, deep), :] = s0 * w1 + s1 * w0
        cube[2, at, pl.ds(0, deep), :] = real * w2 + imag * jnp.where(low, -other, other)
        return carry

    lax.fori_loop(0, nx // group, expand, 0, unroll=4)

    batch = 4 if deep % 4 == 0 else 1

    def column(i, carry):
        ats = [pl.ds(i * batch + b, nx, stride=pad) for b in range(batch)]
        line = jnp.concatenate(
            [jnp.concatenate([rows[v, at, :] for v in range(3)], axis=1) for at in ats], axis=0
        ).astype(BF)
        y = jnp.dot(line, iy[...], preferred_element_type=F32).astype(BF)
        y = jnp.concatenate(
            [
                jnp.concatenate([y[b * nx : (b + 1) * nx, h * HALF : (h + 1) * HALF] for b in range(batch)], axis=1)
                for h in range(2)
            ],
            axis=0,
        )
        y = jnp.dot(fx[...], y, preferred_element_type=F32)
        y = jnp.concatenate([(y[:, b * HALF : (b + 1) * HALF] * mask[...]).astype(BF) for b in range(batch)], axis=1)
        y = jnp.dot(bx[...], y, preferred_element_type=F32).astype(BF)
        y = jnp.concatenate(
            [
                jnp.concatenate([y[h * nx : (h + 1) * nx, b * HALF : (b + 1) * HALF] for h in range(2)], axis=1)
                for b in range(batch)
            ],
            axis=0,
        )
        y = jnp.dot(y, oy[...], preferred_element_type=F32)
        for b, at in enumerate(ats):
            for v in range(3):
                rows[v, at, :] = y[b * nx : (b + 1) * nx, v * 128 : (v + 1) * 128]
        return carry

    lax.fori_loop(0, deep // batch, column, 0)

    first = pl.program_id(0) == 0

    def combine(i, carry):
        at = pl.ds(i * group, group)
        s0, s1, s2 = thirds(s_ref.at[:, 0], at)
        r0, r1, r2 = (cube[v, at, pl.ds(0, deep), :] for v in range(3))
        turned = pltpu.roll(s2, BLK, 2)
        other = pltpu.roll(r2, BLK, 2)
        real = jnp.where(low, s2, turned)
        imag = jnp.where(low, turned, s2)
        terms = (
            s0 * r0 + s1 * r1,
            s0 * r1 - s1 * r0,
            real * r2 + imag * jnp.where(low, other, -other),
        )
        for v in range(3):
            lanes = slice(v * 128, (v + 1) * 128)
            old = o_ref[at, :, lanes]
            start = jnp.zeros_like(old) if fresh else before[at, :, lanes]
            o_ref[at, :, lanes] = jnp.where(first, start, old) + terms[v]
        return carry

    lax.fori_loop(0, nx // group, combine, 0, unroll=4)


def coils(maps, warped, mask, tabs, before, part):
    nx, count, deep, _ = maps.shape
    pad = max(8, deep)
    fresh = before is None
    whole = lambda shape: pl.BlockSpec(
        shape, lambda c: (0,) * len(shape), pipeline_mode=pl.Buffered(1)
    )
    in_specs = [pl.BlockSpec((nx, 1, deep, LANES), lambda c: (0, c, 0, 0))]
    args = [maps, warped, mask, *tabs] + ([] if fresh else [before])
    def columns(array):
        at = part if array.shape[1] > deep else 0
        return pl.BlockSpec(
            (nx, deep, LANES), lambda c: (0, at, 0), pipeline_mode=pl.Buffered(1)
        )

    in_specs += [columns(warped)] + [whole(a.shape) for a in (mask, *tabs)]
    in_specs += [] if fresh else [columns(before)]
    return pl.pallas_call(
        functools.partial(coil_kernel, nx, deep, pad, fresh),
        out_shape=jax.ShapeDtypeStruct((nx, deep, LANES), F32),
        grid=(count,),
        in_specs=in_specs,
        out_specs=pl.BlockSpec((nx, deep, LANES), lambda c: (0, 0, 0)),
        scratch_shapes=[pltpu.VMEM((3, nx * pad, 128), F32)],
        compiler_params=params(),
        cost_estimate=pl.CostEstimate(
            flops=count * deep * 4 * 8 * nx * nx * 192 * 2,
            bytes_accessed=count * nx * deep * LANES * 2 + (14 << 20),
            transcendentals=0,
        ),
        name="coils",
    )(*args)


def update_kernel(count, parts, *refs):
    backs = refs[:parts]
    i_ref, a_ref, o_ref, scratch = refs[parts:]
    part = backs[0].shape[2]
    for x in range(o_ref.shape[1]):
        for h, back in enumerate(backs):
            for d in range(count):
                scratch[x, pl.ds((d * parts + h) * part, part), :] = back[d, x].astype(F32)
        grad = scratch[x].astype(BF).T.astype(F32)
        real = jnp.concatenate([grad[0:128], grad[256:320]], axis=0)
        imag = jnp.concatenate([grad[128:256], grad[320:384]], axis=0)
        for p, value in enumerate((real, imag)):
            o_ref[p, x] = i_ref[p, x] - 0.5 * (value - a_ref[p, x].astype(F32))


def update(backs, image, adjoint):
    parts = len(backs)
    count, planes, part, _ = backs[0].shape
    _, _, ny, nz = image.shape
    group = 3 if planes % 3 == 0 else 1
    block = pl.BlockSpec((2, group, ny, nz), lambda x: (0, x, 0, 0))
    back = pl.BlockSpec((count, group, part, LANES), lambda x: (0, x, 0, 0))
    return pl.pallas_call(
        functools.partial(update_kernel, count, parts),
        out_shape=jax.ShapeDtypeStruct(image.shape, F32),
        grid=(planes // group,),
        in_specs=[back] * parts + [block, block],
        out_specs=block,
        scratch_shapes=[pltpu.VMEM((group, nz, LANES), F32)],
        compiler_params=params(),
        cost_estimate=pl.CostEstimate(flops=0, bytes_accessed=image.size * 12, transcendentals=0),
        name="update",
    )(*backs, image, adjoint)


def exchange(parts):
    return lax.all_to_all(parts, "slab", split_axis=0, concat_axis=0, tiled=True)


def after(value, *others):
    return lax.optimization_barrier((value, *others))[0]


def gather_doubling(value):
    count = lax.axis_size("slab")
    order = [0]
    bit = count // 2
    while bit:
        other = lax.ppermute(value, "slab", [(i, i ^ bit) for i in range(count)])
        value = jnp.concatenate([value, other], axis=0)
        order += [k ^ bit for k in order]
        bit //= 2
    return value, jnp.asarray(order, jnp.int32) ^ lax.axis_index("slab")


def per_device(image, adjoint_data, coil_maps, masks, sources, weights):
    count = lax.axis_size("slab")
    planes, ny, nz = image.shape[1:]
    nx = planes * count
    deep = nz // count
    total = coil_maps.shape[0]
    tabs = tables(nx, ny)
    sampled = jnp.pad(masks[0].astype(F32), ((0, 0), (0, HALF - ny)))
    mask = jnp.concatenate([sampled, sampled], axis=0)

    matrices = weights[0].reshape(3 * planes, 2, BLK, BLK)
    matrices = jnp.transpose(matrices, (0, 2, 1, 3)).reshape(3 * planes, BLK, 2 * BLK)
    digits = jnp.concatenate([sources[0] // BLK, sources[0] % BLK], axis=1).astype(BF)
    digits = jnp.pad(digits[:, None, :], ((0, 0), (0, 7), (0, 2 * BLK - 4)))
    packed, owner = gather_doubling(jnp.concatenate([matrices, digits], axis=1))
    digits = packed[:, BLK, :4].astype(jnp.int32)
    links = (digits[:, :2] * BLK + digits[:, 2:]).reshape(-1)

    columns = exchange(image_columns(image, count))
    halves = deep % 16 == 0
    sizes = [total // 2, total // 4] if halves else [total // 2, total // 4, total // 8]
    sizes += [] if halves else [total - sum(sizes)]
    outgoing = []
    for i, size in enumerate(sizes):
        outgoing.append(maps_columns(coil_maps, count, sum(sizes[:i]), size))
    last = columns
    warped = warp(columns.reshape(nx, deep, LANES), packed, links, owner)

    def run(received, before, part):
        size = received.shape[2]
        return coils(received.reshape(nx, size, -1, LANES), warped, mask, tabs, before, part)

    def back(combined, *needs):
        grad = spread(combined, packed, links, owner)
        return exchange(after(grad, *needs).reshape(count, planes, -1, LANES))

    combined, waiting, ready = None, None, []
    for piece in outgoing:
        arrived = exchange(after(piece, last, *ready))
        if waiting is not None:
            combined = run(waiting, combined, 0)
            ready = [combined]
        last = waiting = arrived
    if not halves:
        combined = run(waiting, combined, 0)
        return update([back(combined)], image, adjoint_data)

    both, first, second = last_maps_columns(coil_maps, count, sum(sizes))
    got_both = exchange(after(both, last, *ready))
    combined = run(waiting, combined, 0)
    got_first = exchange(after(first, got_both, combined))
    half = run(got_both, combined, 0)
    back_first = back(half, got_first)
    half = run(got_first, combined, 1)
    got_second = exchange(after(second, back_first, half))
    half = run(got_second, half, 1)
    return update([back_first, back(half)], image, adjoint_data)


def solution(mesh):
    return jax.shard_map(
        per_device,
        mesh=mesh,
        in_specs=(
            P(None, ("grp", "slab"), None, None),
            P(None, ("grp", "slab"), None, None),
            P(None, None, ("grp", "slab"), None, None),
            P(None, "grp", None),
            P(None, ("grp", "slab"), None),
            P(None, ("grp", "slab"), None),
        ),
        out_specs=P(None, ("grp", "slab"), None, None),
        check_vma=False,
    )
```

time: 801 us -> 755 us (0.943)
  Pallas kernels: 396 us -> 243 us
  waiting for transfers between devices: 301 us -> 375 us
  blocking collectives: 32.4 us -> 66.2 us
  between operations: 13.5 us -> 0.17 us
  local copies, waits for them, and re-layouts: 7.84 us -> 16.8 us
    ppermute x0 -> x4, waiting for transfers between devices: none -> 311 us  [gather_doubling(): other = lax.ppermute(value, 'slab', [(i, i ^ bit) for i in range(count)])]
    all_to_all x7 -> x6, waiting for transfers between devices: 301 us -> 64.5 us  [exchange(): lax.all_to_all(parts, 'slab', split_axis=0, concat_axis=0, tiled=True)]
    pallas_call x5, Pallas kernels: 224 us -> 125 us  [coils(): pl.pallas_call(functools.partial(coil_kernel, nx, deep, pad, fresh), out_...]
    all_to_all x1 -> x2, blocking collectives: 32.4 us -> 66.2 us  [exchange(): lax.all_to_all(parts, 'slab', split_axis=0, concat_axis=0, tiled=True)]
    pallas_call x2, Pallas kernels: 62.3 us -> 31.3 us  [spread(): pl.pallas_call(functools.partial(spread_kernel, nx, deep, pad), out_shape...]
    pallas_call x1, Pallas kernels: 31.2 us -> 15 us  [warp(): pl.pallas_call(functools.partial(warp_kernel, nx, deep, pad), out_shape=j...]
    ppermute x0 -> x4, starting transfers between devices: none -> 8.07 us  [gather_doubling(): other = lax.ppermute(value, 'slab', [(i, i ^ bit) for i in range(count)])]
    all_to_all x7 -> x6, starting transfers between devices: 40.5 us -> 32.7 us  [exchange(): lax.all_to_all(parts, 'slab', split_axis=0, concat_axis=0, tiled=True)]
  transfers between devices with their start and end apart: 8 -> 10, of which waited for: 3 -> 7; matrix products, arithmetic and copies ran while one was open for 1% -> 3% of each run, Pallas kernels for 41% -> 27%
where the time goes in v3:
time: 755 us; the launch traced here: 750 us
  waiting for transfers between devices  375 us (50%)
  Pallas kernels  243 us (32%)
  blocking collectives  66.2 us (9%)
  starting transfers between devices  40.8 us (5%)
  local copies, waits for them, and re-layouts  16.8 us (2%)
  other arithmetic  8.23 us (1%)
    ppermute x4, waiting for transfers between devices, gather_doubling(): other = lax.ppermute(value, 'slab', [(i, i ^ bit) for i in range(count)])  311 us
    pallas_call x5, Pallas kernels, coils(): pl.pallas_call(functools.partial(coil_kernel, nx, deep, pad, fresh), out_...  125 us
    all_to_all x2, blocking collectives, exchange(): lax.all_to_all(parts, 'slab', split_axis=0, concat_axis=0, tiled=True)  66.2 us
    all_to_all x6, waiting for transfers between devices, exchange(): lax.all_to_all(parts, 'slab', split_axis=0, concat_axis=0, tiled=True)  64.5 us
    pallas_call x2, Pallas kernels, maps_columns(): pl.pallas_call(functools.partial(maps_kernel, count, deep), out_shape=jax...  44.5 us
    all_to_all x6, starting transfers between devices, exchange(): lax.all_to_all(parts, 'slab', split_axis=0, concat_axis=0, tiled=True)  32.7 us
    pallas_call x2, Pallas kernels, spread(): pl.pallas_call(functools.partial(spread_kernel, nx, deep, pad), out_shape...  31.3 us
    pallas_call x1, Pallas kernels, last_maps_columns(): pl.pallas_call(functools.partial(last_maps_kernel, count, deep), out_shap...  15.5 us
  transfers between devices with their start and end apart: 10, of which 7 were waited for; matrix products, arithmetic and copies ran while one was open for 3% of the time, Pallas kernels for 27%

profile of v3, /device:TPU:13, one launch (start us, length us, event | category | flops | bytes accessed | tf_op | source)
XLA Modules:
  0.0 750.0 jit_solution(12322207842797036683)
XLA Ops:
  0.0 4.7 image_columns.1
  4.7 6.6 all-to-all-start
  11.2 29.3 %maps_columns.3 = bf16[16,12,4,16,384]{4,3,2,1,0:T(8,128)(2,1)} custom-call(bf16[8,2,12,192,256]{4,3,2,1,0:T(8,128)(2,1)} %x_ref.6), custom_call_target="tpu_custom_call" | custom-call | bytes 18874368 | tf_op jit(solution)/shard_map/maps_columns/pallas_call | solution.py:124
  40.5 23.7 %all-to-all-done = bf16[16,12,16,384]{3,2,1,0:T(8,128)(2,1)S(1)} async-done(((bf16[16,12,16,384]{3,2,1,0:T(8,128)(2,1)}), bf16[16,12,16,384]{3,2,1,0:T(8,128)(2,1)S(1)}, u32[]{:S(2)}, u32[]{:S(2)}) %all-to-all-start) | async-done | bytes 2359328 | tf_op jit(solution)/shard_map/all_to_all | solution.py:493
  64.3 1.5 copy-done.2
  65.7 4.9 all-to-all-start.1
  70.8 1.3 reshape_squeeze.3
  72.1 1.2 copy.21
  73.3 0.5 reshape.64
  73.9 1.0 pad_maximum_fusion.3
  74.9 2.1 collective-permute-start
  77.0 224.6 %collective-permute-done = bf16[36,72,128]{2,1,0:T(8,128)(2,1)S(1)} collective-permute-done((bf16[36,72,128]{2,1,0:T(8,128)(2,1)S(1)}, bf16[36,72,128]{2,1,0:T(8,128)(2,1)S(1)}, u32[]{:S(2)}, u32[]{:S(2)}) %collective-permute-start) | collective-permute-done | bytes 663584 | tf_op jit(solution)/shard_map/ppermute | solution.py:505
  301.7 3.3 collective-permute-start.1
  305.0 28.6 %collective-permute-done.1 = bf16[72,72,128]{2,1,0:T(8,128)(2,1)S(1)} collective-permute-done((bf16[72,72,128]{2,1,0:T(8,128)(2,1)S(1)}, bf16[72,72,128]{2,1,0:T(8,128)(2,1)S(1)}, u32[]{:S(2)}, u32[]{:S(2)}) %collective-permute-start.1) | collective-permute-done | bytes 1327136 | tf_op jit(solution)/shard_map/ppermute | solution.py:505
  333.6 0.4 pad_maximum_fusion.1
  334.0 0.3 collective-permute-start.2
  334.4 57.3 %collective-permute-done.2 = bf16[144,72,128]{2,1,0:T(8,128)(2,1)S(1)} collective-permute-done((bf16[144,72,128]{2,1,0:T(8,128)(2,1)S(1)}, bf16[144,72,128]{2,1,0:T(8,128)(2,1)S(1)}, u32[]{:S(2)}, u32[]{:S(2)}) %collective-permute-start.2) | collective-permute-done | bytes 2654240 | tf_op jit(solution)/shard_map/ppermute | solution.py:505
  391.7 3.7 pad_maximum_fusion
  395.4 2.4 collective-permute-start.3
  397.8 15.2 %maps_columns.2 = bf16[16,12,2,16,384]{4,3,2,1,0:T(8,128)(2,1)} custom-call(bf16[8,2,12,192,256]{4,3,2,1,0:T(8,128)(2,1)} %x_ref.6), custom_call_target="tpu_custom_call" | custom-call | bytes 9437184 | tf_op jit(solution)/shard_map/maps_columns/pallas_call | solution.py:124
  412.9 5.4 all-to-all-start.2
  418.4 15.5 %last_maps_columns.1 = (bf16[16,12,2,8,384]{4,3,2,1,0:T(8,128)(2,1)}, bf16[16,12,1,8,384]{4,3,2,1,0:T(8,128)(2,1)}, bf16[16,12,1,8,384]{4,3,2,1,0:T(8,128)(2,1)}) custom-call(bf16[8,2,12,192,256]{4,3,2,1,0:T(8,128)(2,1)} %x_ref.6), custom_call_target="tpu_custom_call" | custom-call | bytes 9437184 | tf_op jit(solution)/shard_map/last_maps_columns/pallas_call | solution.py:145
  433.9 0.8 pad_maximum_fusion.4.refs_2_
  434.7 0.5 broadcast_xor_fusion.owner
  435.2 0.9 constant_dynamic-update-slice_fusion.3
  436.2 1.2 constant_dynamic-update-slice_fusion.2
  437.4 2.0 constant_dynamic-update-slice_fusion.1
  439.4 5.8 constant_dynamic-update-slice_fusion.w_hbm
  445.2 1.5 slice_convert_fusion
  446.8 0.8 reshape.65.links
  447.6 15.0 %warp.1.refs_1_ = f32[192,16,384]{2,1,0:T(8,128)} custom-call(s32[1152]{0:T(1024)} %reshape.65.links, s32[16]{0:T(128)} %broadcast_xor_fusion.owner, bf16[192,16,384]{2,1,0:T(8,128)(2,1)} %bitcast.42, bf16[576,72,128]{2,1,0:T(8,128)(2,1)} %constant_dynamic-update-slice_fusion.w_hbm), custom_call_target="tpu_custom_call" | custom-call | flops 2415919104 | bytes 20971520 | tf_op jit(solution)/shard_map/warp/pallas_call | solution.py:233
  462.7 56.5 %coils.5.refs_7_ = f32[192,16,384]{2,1,0:T(8,128)} custom-call(bf16[192,4,16,384]{3,2,1,0:T(8,128)(2,1)} %bitcast.5.refs_0_, f32[192,16,384]{2,1,0:T(8,128)} %warp.1.refs_1_, f32[384,256]{1,0:T(8,128)} %pad_maximum_fusion.4.refs_2_, bf16[384,512]{1,0:T(8,128)(2,1)} %constant.48.clone.refs_3_, bf16[384,384]{1,0:T(8,128)(2,1)} %constant.49.clone.refs_4_, ...), custom_call_target="tpu_custom_call" | custom-call | flops 28991029248 | bytes 24117248 | tf_op jit(solution)/shard_map/coils/pallas_call | solution.py:440
  519.1 2.9 all-to-all-done.2
  522.1 4.9 all-to-all-start.3
  527.0 32.7 %coils.6.refs_7_ = f32[192,16,384]{2,1,0:T(8,128)} custom-call(bf16[192,2,16,384]{3,2,1,0:T(8,128)(2,1)} %bitcast.9.refs_0_, f32[192,16,384]{2,1,0:T(8,128)} %warp.1.refs_1_, f32[384,256]{1,0:T(8,128)} %pad_maximum_fusion.4.refs_2_, bf16[384,512]{1,0:T(8,128)(2,1)} %constant.48.clone.refs_3_, bf16[384,384]{1,0:T(8,128)(2,1)} %constant.49.clone.refs_4_, ...), custom_call_target="tpu_custom_call" | custom-call | flops 14495514624 | bytes 19398656 | tf_op jit(solution)/shard_map/coils/pallas_call | solution.py:440
  559.7 20.3 %all-to-all-done.3 = bf16[16,12,2,8,384]{4,3,2,1,0:T(8,128)(2,1)S(1)} async-done(((bf16[16,12,2,8,384]{4,3,2,1,0:T(8,128)(2,1)}), bf16[16,12,2,8,384]{4,3,2,1,0:T(8,128)(2,1)S(1)}, u32[]{:S(2)}, u32[]{:S(2)}) %all-to-all-start.3) | async-done | bytes 2359328 | tf_op jit(solution)/shard_map/all_to_all | solution.py:493
  580.0 1.4 copy-done.5
  581.4 4.9 all-to-all-start.4
  586.3 15.7 %coils.7.c_ref = f32[192,8,384]{2,1,0:T(8,128)} custom-call(bf16[192,2,8,384]{3,2,1,0:T(8,128)(2,1)} %bitcast.48, f32[192,16,384]{2,1,0:T(8,128)} %warp.1.refs_1_, f32[384,256]{1,0:T(8,128)} %pad_maximum_fusion.4.refs_2_, bf16[384,512]{1,0:T(8,128)(2,1)} %constant.48.clone.refs_3_, bf16[384,384]{1,0:T(8,128)(2,1)} %constant.49.clone.refs_4_, ...), custom_call_target="tpu_custom_call" | custom-call | flops 7247757312 | bytes 17039360 | tf_op jit(solution)/shard_map/coils/pallas_call | solution.py:440
  602.0 15.6 %spread.2 = bf16[192,8,384]{2,1,0:T(8,128)(2,1)} custom-call(s32[1152]{0:T(1024)} %reshape.65.links, s32[16]{0:T(128)} %broadcast_xor_fusion.owner, f32[192,8,384]{2,1,0:T(8,128)} %coils.7.c_ref, bf16[576,72,128]{2,1,0:T(8,128)(2,1)} %constant_dynamic-update-slice_fusion.w_hbm), custom_call_target="tpu_custom_call" | custom-call | flops 2415919104 | bytes 20971520 | tf_op jit(solution)/shard_map/spread/pallas_call | solution.py:316
  617.7 6.0 all-to-all-start.5
  623.7 10.2 %coils.8.refs_7_ = f32[192,8,384]{2,1,0:T(8,128)} custom-call(bf16[192,1,8,384]{3,2,1,0:T(8,128)(2,1)} %bitcast.43, f32[192,16,384]{2,1,0:T(8,128)} %warp.1.refs_1_, f32[384,256]{1,0:T(8,128)} %pad_maximum_fusion.4.refs_2_, bf16[384,512]{1,0:T(8,128)(2,1)} %constant.48.clone.refs_3_, bf16[384,384]{1,0:T(8,128)(2,1)} %constant.49.clone.refs_4_, ...), custom_call_target="tpu_custom_call" | custom-call | flops 3623878656 | bytes 15859712 | tf_op jit(solution)/shard_map/coils/pallas_call | solution.py:440
  634.0 17.5 %all-to-all-done.5.refs_0_ = bf16[16,12,8,384]{3,2,1,0:T(8,128)(2,1)S(1)} async-done(((bf16[16,12,8,384]{3,2,1,0:T(8,128)(2,1)}), bf16[16,12,8,384]{3,2,1,0:T(8,128)(2,1)S(1)}, u32[]{:S(2)}, u32[]{:S(2)}) %all-to-all-start.5) | async-done | bytes 1179680 | tf_op jit(solution)/shard_map/all_to_all | solution.py:493
  651.5 32.4 %all_to_all.40 = bf16[16,12,1,8,384]{4,3,2,1,0:T(8,128)(2,1)} all-to-all(bf16[16,12,1,8,384]{4,3,2,1,0:T(8,128)(2,1)S(1)} %copy-done.6), channel_id=1, replica_groups=mesh['grp'=2,'slab'=16] {'slab'}, dimensions={0} | all-to-all | bytes 2359296 | tf_op jit(solution)/shard_map/all_to_all | solution.py:493
  683.9 10.3 %coils.9.c_ref = f32[192,8,384]{2,1,0:T(8,128)} custom-call(bf16[192,1,8,384]{3,2,1,0:T(8,128)(2,1)} %bitcast.49, f32[192,16,384]{2,1,0:T(8,128)} %warp.1.refs_1_, f32[384,256]{1,0:T(8,128)} %pad_maximum_fusion.4.refs_2_, bf16[384,512]{1,0:T(8,128)(2,1)} %constant.48.clone.refs_3_, bf16[384,384]{1,0:T(8,128)(2,1)} %constant.49.clone.refs_4_, ...), custom_call_target="tpu_custom_call" | custom-call | flops 3623878656 | bytes 15859712 | tf_op jit(solution)/shard_map/coils/pallas_call | solution.py:440
  694.2 15.6 %spread.3 = bf16[192,8,384]{2,1,0:T(8,128)(2,1)} custom-call(s32[1152]{0:T(1024)} %reshape.65.links, s32[16]{0:T(128)} %broadcast_xor_fusion.owner, f32[192,8,384]{2,1,0:T(8,128)} %coils.9.c_ref, bf16[576,72,128]{2,1,0:T(8,128)(2,1)} %constant_dynamic-update-slice_fusion.w_hbm), custom_call_target="tpu_custom_call" | custom-call | flops 2415919104 | bytes 20971520 | tf_op jit(solution)/shard_map/spread/pallas_call | solution.py:316
  709.8 33.8 %all_to_all.41.refs_1_ = bf16[16,12,8,384]{3,2,1,0:T(8,128)(2,1)} all-to-all(bf16[16,12,8,384]{3,2,1,0:T(8,128)(2,1)} %bitcast.46), channel_id=1, replica_groups=mesh['grp'=2,'slab'=16] {'slab'}, dimensions={0} | all-to-all | bytes 2359296 | tf_op jit(solution)/shard_map/all_to_all | solution.py:493
  743.6 6.4 update.1
  (31 shorter events, 0.5 us)
Async XLA Ops:
  4.7 59.6 %all-to-all-start = ((bf16[16,12,16,384]{3,2,1,0:T(8,128)(2,1)}), bf16[16,12,16,384]{3,2,1,0:T(8,128)(2,1)S(1)}, u32[]{:S(2)}, u32[]{:S(2)}) async-start(bf16[16,12,16,384]{3,2,1,0:T(8,128)(2,1)} %image_columns.1), calls=%async_computation | async-start | bytes 4718592 | tf_op jit(solution)/shard_map/all_to_all | solution.py:493
  40.5 30.1 %copy-start.9 = (s32[1,36,2]{1,2,0:T(2,128)S(1)}, s32[1,36,2]{1,2,0:T(2,128)}, u32[]{:S(2)}) copy-start(s32[1,36,2]{1,2,0:T(2,128)} %param.15) | copy-start | bytes 868
  40.5 30.3 %copy-start.7 = (bf16[1,36,8192]{2,1,0:T(8,128)(2,1)S(1)}, bf16[1,36,8192]{2,1,0:T(8,128)(2,1)}, u32[]{:S(2)}) copy-start(bf16[1,36,8192]{2,1,0:T(8,128)(2,1)} %param.16) | copy-start | bytes 1769476
  64.3 1.5 copy-start.2
  65.7 347.2 %all-to-all-start.1 = ((bf16[16,12,4,16,384]{4,3,2,1,0:T(8,128)(2,1)}), bf16[16,12,4,16,384]{4,3,2,1,0:T(8,128)(2,1)}, u32[]{:S(2)}, u32[]{:S(2)}) async-start(bf16[16,12,4,16,384]{4,3,2,1,0:T(8,128)(2,1)} %maps_columns.3), calls=%async_computation.1 | async-start | bytes 18874368 | tf_op jit(solution)/shard_map/all_to_all | solution.py:493
  74.9 226.7 %collective-permute-start = (bf16[36,72,128]{2,1,0:T(8,128)(2,1)S(1)}, bf16[36,72,128]{2,1,0:T(8,128)(2,1)S(1)}, u32[]{:S(2)}, u32[]{:S(2)}) collective-permute-start(bf16[36,72,128]{2,1,0:T(8,128)(2,1)S(1)} %get-tuple-element.23), channel_id=1, source_target_pairs={{0,8},{1,9},{2,10},{3,11},{4,12},{5,13},{6,14},{7,15},{8,0},{9,1},... | collective-permute-start | bytes 1990664 | tf_op jit(solution)/shard_map/ppermute | solution.py:505
  301.7 31.9 %collective-permute-start.1 = (bf16[72,72,128]{2,1,0:T(8,128)(2,1)S(1)}, bf16[72,72,128]{2,1,0:T(8,128)(2,1)S(1)}, u32[]{:S(2)}, u32[]{:S(2)}) collective-permute-start(bf16[72,72,128]{2,1,0:T(8,128)(2,1)S(1)} %pad_maximum_fusion.2), channel_id=1, source_target_pairs={{0,4},{1,5},{2,6},{3,7},{4,0},{5,1},{6,2},{7,3},{8,12},{9,13},{10,... | collective-permute-start | bytes 3981320 | tf_op jit(solution)/shard_map/ppermute | solution.py:505
  334.0 57.7 %collective-permute-start.2 = (bf16[144,72,128]{2,1,0:T(8,128)(2,1)S(1)}, bf16[144,72,128]{2,1,0:T(8,128)(2,1)S(1)}, u32[]{:S(2)}, u32[]{:S(2)}) collective-permute-start(bf16[144,72,128]{2,1,0:T(8,128)(2,1)S(1)} %pad_maximum_fusion.1), channel_id=1, source_target_pairs={{0,2},{1,3},{2,0},{3,1},{4,6},{5,7},{6,4},{7,5},{8,10},{9,11},{10,... | collective-permute-start | bytes 7962632 | tf_op jit(solution)/shard_map/ppermute | solution.py:505
  391.7 3.7 copy-start
  395.4 44.0 %collective-permute-start.3 = (bf16[288,72,128]{2,1,0:T(8,128)(2,1)}, bf16[288,72,128]{2,1,0:T(8,128)(2,1)}, u32[]{:S(2)}, u32[]{:S(2)}) collective-permute-start(bf16[288,72,128]{2,1,0:T(8,128)(2,1)} %pad_maximum_fusion), channel_id=1, source_target_pairs={{0,1},{1,0},{2,3},{3,2},{4,5},{5,4},{6,7},{7,6},{8,9},{9,8},{10,11... | collective-permute-start | bytes 15925256 | tf_op jit(solution)/shard_map/ppermute | solution.py:505
  412.9 109.1 %all-to-all-start.2 = ((bf16[16,12,2,16,384]{4,3,2,1,0:T(8,128)(2,1)}), bf16[16,12,2,16,384]{4,3,2,1,0:T(8,128)(2,1)}, u32[]{:S(2)}, u32[]{:S(2)}) async-start(bf16[16,12,2,16,384]{4,3,2,1,0:T(8,128)(2,1)} %maps_columns.2), calls=%async_computation.2 | async-start | bytes 9437184 | tf_op jit(solution)/shard_map/all_to_all | solution.py:493
  418.3 15.5 %copy-start.8 = (s32[1,192,192]{2,1,0:T(8,128)S(1)}, s32[1,192,192]{2,1,0:T(8,128)}, u32[]{:S(2)}) copy-start(s32[1,192,192]{2,1,0:T(8,128)} %param.14) | copy-start | bytes 442372
  418.4 16.3 %copy-start.10 = (s32[16]{0:T(128)S(1)}, s32[16]{0:T(128)}, u32[]{:S(2)}) copy-start(s32[16]{0:T(128)} %constant.52.clone) | copy-start | bytes 196
  433.9 3.5 copy-start.1
  522.1 57.9 %all-to-all-start.3 = ((bf16[16,12,2,8,384]{4,3,2,1,0:T(8,128)(2,1)}), bf16[16,12,2,8,384]{4,3,2,1,0:T(8,128)(2,1)S(1)}, u32[]{:S(2)}, u32[]{:S(2)}) async-start(bf16[16,12,2,8,384]{4,3,2,1,0:T(8,128)(2,1)} %get-tuple-element.17), calls=%async_computation.3 | async-start | bytes 4718592 | tf_op jit(solution)/shard_map/all_to_all | solution.py:493
  580.0 1.4 copy-start.5
  581.4 36.3 %all-to-all-start.4 = ((bf16[16,12,1,8,384]{4,3,2,1,0:T(8,128)(2,1)}), bf16[16,12,1,8,384]{4,3,2,1,0:T(8,128)(2,1)S(1)}, u32[]{:S(2)}, u32[]{:S(2)}) async-start(bf16[16,12,1,8,384]{4,3,2,1,0:T(8,128)(2,1)} %get-tuple-element.19), calls=%async_computation.4 | async-start | bytes 2359296 | tf_op jit(solution)/shard_map/all_to_all | solution.py:493
  617.7 6.0 copy-start.4
  617.7 33.8 %all-to-all-start.5 = ((bf16[16,12,8,384]{3,2,1,0:T(8,128)(2,1)}), bf16[16,12,8,384]{3,2,1,0:T(8,128)(2,1)S(1)}, u32[]{:S(2)}, u32[]{:S(2)}) async-start(bf16[16,12,8,384]{3,2,1,0:T(8,128)(2,1)} %bitcast.45), calls=%async_computation.5 | async-start | bytes 2359296 | tf_op jit(solution)/shard_map/all_to_all | solution.py:493
  623.7 27.8 %copy-start.6 = (bf16[16,12,1,8,384]{4,3,2,1,0:T(8,128)(2,1)S(1)}, bf16[16,12,1,8,384]{4,3,2,1,0:T(8,128)(2,1)}, u32[]{:S(2)}) copy-start(bf16[16,12,1,8,384]{4,3,2,1,0:T(8,128)(2,1)} %get-tuple-element.22) | copy-start | bytes 3538948
  651.5 42.7 %copy-start.3 = (bf16[16,12,8,384]{3,2,1,0:T(8,128)(2,1)}, bf16[16,12,8,384]{3,2,1,0:T(8,128)(2,1)S(1)}, u32[]{:S(2)}) copy-start(bf16[16,12,8,384]{3,2,1,0:T(8,128)(2,1)S(1)} %all-to-all-done.5.refs_0_) | copy-start | bytes 3538948

commit v4 on v3

--- a/solution.py
+++ b/solution.py
@@ -497,16 +497,21 @@
     return lax.optimization_barrier((value, *others))[0]
 
 
-def gather_doubling(value):
+def swap_halves(value):
     count = lax.axis_size("slab")
-    order = [0]
-    bit = count // 2
-    while bit:
-        other = lax.ppermute(value, "slab", [(i, i ^ bit) for i in range(count)])
-        value = jnp.concatenate([value, other], axis=0)
-        order += [k ^ bit for k in order]
-        bit //= 2
-    return value, jnp.asarray(order, jnp.int32) ^ lax.axis_index("slab")
+    half = count // 2
+    other = lax.ppermute(value, "slab", [(i, i ^ half) for i in range(count)])
+    return jnp.concatenate([value, other], axis=0)
+
+
+def gather_half(pair):
+    count = lax.axis_size("slab")
+    half = count // 2
+    groups = [list(range(half)), list(range(half, count))]
+    gathered = lax.all_gather(pair, "slab", axis=0, tiled=True, axis_index_groups=groups)
+    mine = lax.axis_index("slab") // half
+    place = jnp.arange(count, dtype=jnp.int32)
+    return gathered, place // 2 + half * ((place % 2) ^ mine)
 
 
 def per_device(image, adjoint_data, coil_maps, masks, sources, weights):
@@ -523,7 +528,8 @@
     matrices = jnp.transpose(matrices, (0, 2, 1, 3)).reshape(3 * planes, BLK, 2 * BLK)
     digits = jnp.concatenate([sources[0] // BLK, sources[0] % BLK], axis=1).astype(BF)
     digits = jnp.pad(digits[:, None, :], ((0, 0), (0, 7), (0, 2 * BLK - 4)))
-    packed, owner = gather_doubling(jnp.concatenate([matrices, digits], axis=1))
+    pair = swap_halves(jnp.concatenate([matrices, digits], axis=1))
+    packed, owner = gather_half(pair)
     digits = packed[:, BLK, :4].astype(jnp.int32)
     links = (digits[:, :2] * BLK + digits[:, 2:]).reshape(-1)
 
@@ -547,7 +553,7 @@
 
     combined, waiting, ready = None, None, []
     for piece in outgoing:
-        arrived = exchange(after(piece, last, *ready))
+        arrived = exchange(after(piece, last, pair, *ready))
         if waiting is not None:
             combined = run(waiting, combined, 0)
             ready = [combined]

time: 755 us -> 665 us (0.88)
  waiting for transfers between devices: 375 us -> 279 us
  between operations: 0.17 us -> 13.5 us
    ppermute x4 -> x1, waiting for transfers between devices: 311 us -> 39.3 us  [swap_halves(): other = lax.ppermute(value, 'slab', [(i, i ^ half) for i in range(count)])]
    all_to_all x6, waiting for transfers between devices: 64.5 us -> 239 us  [exchange(): lax.all_to_all(parts, 'slab', split_axis=0, concat_axis=0, tiled=True)]
  transfers between devices with their start and end apart: 10 -> 8, of which waited for: 7 -> 5; matrix products, arithmetic and copies ran while one was open for 3% -> 2% of each run, Pallas kernels for 27% -> 31%
where the time goes in v4:
time: 665 us; the launch traced here: 659 us
  waiting for transfers between devices  279 us (42%)
  Pallas kernels  243 us (37%)
  blocking collectives  66.2 us (10%)
  starting transfers between devices  41 us (6%)
  between operations  13.5 us (2%)
  local copies, waits for them, and re-layouts  12.1 us (2%)
    all_to_all x6, waiting for transfers between devices, exchange(): lax.all_to_all(parts, 'slab', split_axis=0, concat_axis=0, tiled=True)  239 us
    pallas_call x5, Pallas kernels, coils(): pl.pallas_call(functools.partial(coil_kernel, nx, deep, pad, fresh), out_...  125 us
    all_to_all x2, blocking collectives, exchange(): lax.all_to_all(parts, 'slab', split_axis=0, concat_axis=0, tiled=True)  66.2 us
    pallas_call x2, Pallas kernels, maps_columns(): pl.pallas_call(functools.partial(maps_kernel, count, deep), out_shape=jax...  44.6 us
    ppermute x1, waiting for transfers between devices, swap_halves(): other = lax.ppermute(value, 'slab', [(i, i ^ half) for i in range(count)])  39.3 us
    all_to_all x6, starting transfers between devices, exchange(): lax.all_to_all(parts, 'slab', split_axis=0, concat_axis=0, tiled=True)  38.8 us
    pallas_call x2, Pallas kernels, spread(): pl.pallas_call(functools.partial(spread_kernel, nx, deep, pad), out_shape...  31.3 us
    pallas_call x1, Pallas kernels, last_maps_columns(): pl.pallas_call(functools.partial(last_maps_kernel, count, deep), out_shap...  15.5 us
  transfers between devices with their start and end apart: 8, of which 5 were waited for; matrix products, arithmetic and copies ran while one was open for 2% of the time, Pallas kernels for 31%

profile of v4, /device:TPU:13, one launch (start us, length us, event | category | flops | bytes accessed | tf_op | source)
XLA Modules:
  0.0 659.5 jit_solution(16157997265208289633)
XLA Ops:
  6.5 4.7 image_columns.1
  11.2 6.7 %all-to-all-start = ((bf16[16,12,16,384]{3,2,1,0:T(8,128)(2,1)}), bf16[16,12,16,384]{3,2,1,0:T(8,128)(2,1)S(1)}, u32[]{:S(2)}, u32[]{:S(2)}) async-start(bf16[16,12,16,384]{3,2,1,0:T(8,128)(2,1)} %image_columns.1), calls=%async_computation | async-start | bytes 4718592 | tf_op jit(solution)/shard_map/all_to_all | solution.py:493
  17.9 0.0 copy-done.6
  17.9 0.7 copy.18
  18.6 2.2 reshape_squeeze.3
  20.8 2.2 copy.20
  23.1 2.6 reshape.64
  25.7 0.7 pad.8
  26.4 0.1 pad_maximum_fusion.1
  26.5 2.2 collective-permute-start
  28.6 29.3 %maps_columns.3 = bf16[16,12,4,16,384]{4,3,2,1,0:T(8,128)(2,1)} custom-call(bf16[8,2,12,192,256]{4,3,2,1,0:T(8,128)(2,1)} %x_ref.6), custom_call_target="tpu_custom_call" | custom-call | bytes 18874368 | tf_op jit(solution)/shard_map/maps_columns/pallas_call | solution.py:124
  57.9 39.3 %collective-permute-done = bf16[36,72,128]{2,1,0:T(8,128)(2,1)S(1)} collective-permute-done((bf16[36,72,128]{2,1,0:T(8,128)(2,1)S(1)}, bf16[36,72,128]{2,1,0:T(8,128)(2,1)S(1)}, u32[]{:S(2)}, u32[]{:S(2)}) %collective-permute-start) | collective-permute-done | bytes 663584 | tf_op jit(solution)/shard_map/ppermute | solution.py:503
  97.2 1.2 pad_maximum_fusion
  98.4 0.0 all-to-all-done
  98.4 1.4 copy-done
  99.8 8.5 %all-to-all-start.1 = ((bf16[16,12,4,16,384]{4,3,2,1,0:T(8,128)(2,1)}), bf16[16,12,4,16,384]{4,3,2,1,0:T(8,128)(2,1)}, u32[]{:S(2)}, u32[]{:S(2)}) async-start(bf16[16,12,4,16,384]{4,3,2,1,0:T(8,128)(2,1)} %maps_columns.3), calls=%async_computation.1 | async-start | bytes 18874368 | tf_op jit(solution)/shard_map/all_to_all | solution.py:493
  108.3 0.0 all-gather.2.cloned.1.call-start
  108.3 0.7 all-gather.2.cloned.1.call-update
  109.0 15.3 %maps_columns.2 = bf16[16,12,2,16,384]{4,3,2,1,0:T(8,128)(2,1)} custom-call(bf16[8,2,12,192,256]{4,3,2,1,0:T(8,128)(2,1)} %x_ref.6), custom_call_target="tpu_custom_call" | custom-call | bytes 9437184 | tf_op jit(solution)/shard_map/maps_columns/pallas_call | solution.py:124
  124.4 188.8 %all-to-all-done.1 = bf16[16,12,4,16,384]{4,3,2,1,0:T(8,128)(2,1)} async-done(((bf16[16,12,4,16,384]{4,3,2,1,0:T(8,128)(2,1)}), bf16[16,12,4,16,384]{4,3,2,1,0:T(8,128)(2,1)}, u32[]{:S(2)}, u32[]{:S(2)}) %all-to-all-start.1) | async-done | bytes 9437216 | tf_op jit(solution)/shard_map/all_to_all | solution.py:493
  313.2 7.8 %all-to-all-start.2 = ((bf16[16,12,2,16,384]{4,3,2,1,0:T(8,128)(2,1)}), bf16[16,12,2,16,384]{4,3,2,1,0:T(8,128)(2,1)}, u32[]{:S(2)}, u32[]{:S(2)}) async-start(bf16[16,12,2,16,384]{4,3,2,1,0:T(8,128)(2,1)} %maps_columns.2), calls=%async_computation.2 | async-start | bytes 9437184 | tf_op jit(solution)/shard_map/all_to_all | solution.py:493
  321.0 15.5 %last_maps_columns.1 = (bf16[16,12,2,8,384]{4,3,2,1,0:T(8,128)(2,1)}, bf16[16,12,1,8,384]{4,3,2,1,0:T(8,128)(2,1)}, bf16[16,12,1,8,384]{4,3,2,1,0:T(8,128)(2,1)}) custom-call(bf16[8,2,12,192,256]{4,3,2,1,0:T(8,128)(2,1)} %x_ref.6), custom_call_target="tpu_custom_call" | custom-call | bytes 9437184 | tf_op jit(solution)/shard_map/last_maps_columns/pallas_call | solution.py:145
  336.5 0.6 fusion.4.owner
  337.1 0.8 pad_maximum_fusion.2.refs_2_
  337.9 1.5 slice_convert_fusion
  339.4 0.1 slice_add_fusion
  339.6 0.8 reshape.65.links
  340.4 15.0 %warp.1.refs_1_ = f32[192,16,384]{2,1,0:T(8,128)} custom-call(s32[1152]{0:T(1024)} %reshape.65.links, s32[16]{0:T(128)} %fusion.4.owner, bf16[192,16,384]{2,1,0:T(8,128)(2,1)} %bitcast.42, bf16[576,72,128]{2,1,0:T(8,128)(2,1)} %all-gather.2.cloned.1.call-done.w_hbm), custom_call_target="tpu_custom_call" | custom-call | flops 2415919104 | bytes 20971520 | tf_op jit(solution)/shard_map/warp/pallas_call | solution.py:233
  355.4 56.6 %coils.5.refs_7_ = f32[192,16,384]{2,1,0:T(8,128)} custom-call(bf16[192,4,16,384]{3,2,1,0:T(8,128)(2,1)} %bitcast.5.refs_0_, f32[192,16,384]{2,1,0:T(8,128)} %warp.1.refs_1_, f32[384,256]{1,0:T(8,128)} %pad_maximum_fusion.2.refs_2_, bf16[384,512]{1,0:T(8,128)(2,1)} %constant.87.clone.refs_3_, bf16[384,384]{1,0:T(8,128)(2,1)} %constant.88.clone.refs_4_, ...), custom_call_target="tpu_custom_call" | custom-call | flops 28991029248 | bytes 24117248 | tf_op jit(solution)/shard_map/coils/pallas_call | solution.py:440
  412.0 12.7 %all-to-all-done.2 = bf16[16,12,2,16,384]{4,3,2,1,0:T(8,128)(2,1)} async-done(((bf16[16,12,2,16,384]{4,3,2,1,0:T(8,128)(2,1)}), bf16[16,12,2,16,384]{4,3,2,1,0:T(8,128)(2,1)}, u32[]{:S(2)}, u32[]{:S(2)}) %all-to-all-start.2) | async-done | bytes 4718624 | tf_op jit(solution)/shard_map/all_to_all | solution.py:493
  424.7 4.9 all-to-all-start.3
  429.6 32.7 %coils.6.refs_7_ = f32[192,16,384]{2,1,0:T(8,128)} custom-call(bf16[192,2,16,384]{3,2,1,0:T(8,128)(2,1)} %bitcast.9.refs_0_, f32[192,16,384]{2,1,0:T(8,128)} %warp.1.refs_1_, f32[384,256]{1,0:T(8,128)} %pad_maximum_fusion.2.refs_2_, bf16[384,512]{1,0:T(8,128)(2,1)} %constant.87.clone.refs_3_, bf16[384,384]{1,0:T(8,128)(2,1)} %constant.88.clone.refs_4_, ...), custom_call_target="tpu_custom_call" | custom-call | flops 14495514624 | bytes 19398656 | tf_op jit(solution)/shard_map/coils/pallas_call | solution.py:440
  462.3 20.3 %all-to-all-done.3 = bf16[16,12,2,8,384]{4,3,2,1,0:T(8,128)(2,1)S(1)} async-done(((bf16[16,12,2,8,384]{4,3,2,1,0:T(8,128)(2,1)}), bf16[16,12,2,8,384]{4,3,2,1,0:T(8,128)(2,1)S(1)}, u32[]{:S(2)}, u32[]{:S(2)}) %all-to-all-start.3) | async-done | bytes 2359328 | tf_op jit(solution)/shard_map/all_to_all | solution.py:493
  482.6 1.4 copy-done.3
  484.0 4.9 all-to-all-start.4
  488.9 15.7 %coils.7.c_ref = f32[192,8,384]{2,1,0:T(8,128)} custom-call(bf16[192,2,8,384]{3,2,1,0:T(8,128)(2,1)} %bitcast.48, f32[192,16,384]{2,1,0:T(8,128)} %warp.1.refs_1_, f32[384,256]{1,0:T(8,128)} %pad_maximum_fusion.2.refs_2_, bf16[384,512]{1,0:T(8,128)(2,1)} %constant.87.clone.refs_3_, bf16[384,384]{1,0:T(8,128)(2,1)} %constant.88.clone.refs_4_, ...), custom_call_target="tpu_custom_call" | custom-call | flops 7247757312 | bytes 17039360 | tf_op jit(solution)/shard_map/coils/pallas_call | solution.py:440
  504.6 15.7 %spread.2 = bf16[192,8,384]{2,1,0:T(8,128)(2,1)} custom-call(s32[1152]{0:T(1024)} %reshape.65.links, s32[16]{0:T(128)} %fusion.4.owner, f32[192,8,384]{2,1,0:T(8,128)} %coils.7.c_ref, bf16[576,72,128]{2,1,0:T(8,128)(2,1)} %all-gather.2.cloned.1.call-done.w_hbm), custom_call_target="tpu_custom_call" | custom-call | flops 2415919104 | bytes 20971520 | tf_op jit(solution)/shard_map/spread/pallas_call | solution.py:316
  520.3 0.0 all-to-all-done.4
  520.3 0.0 copy-start.2
  520.3 6.0 all-to-all-start.5
  526.4 10.2 %coils.8.refs_7_ = f32[192,8,384]{2,1,0:T(8,128)} custom-call(bf16[192,1,8,384]{3,2,1,0:T(8,128)(2,1)} %bitcast.43, f32[192,16,384]{2,1,0:T(8,128)} %warp.1.refs_1_, f32[384,256]{1,0:T(8,128)} %pad_maximum_fusion.2.refs_2_, bf16[384,512]{1,0:T(8,128)(2,1)} %constant.87.clone.refs_3_, bf16[384,384]{1,0:T(8,128)(2,1)} %constant.88.clone.refs_4_, ...), custom_call_target="tpu_custom_call" | custom-call | flops 3623878656 | bytes 15859712 | tf_op jit(solution)/shard_map/coils/pallas_call | solution.py:440
  536.6 17.5 %all-to-all-done.5.refs_0_ = bf16[16,12,8,384]{3,2,1,0:T(8,128)(2,1)S(1)} async-done(((bf16[16,12,8,384]{3,2,1,0:T(8,128)(2,1)}), bf16[16,12,8,384]{3,2,1,0:T(8,128)(2,1)S(1)}, u32[]{:S(2)}, u32[]{:S(2)}) %all-to-all-start.5) | async-done | bytes 1179680 | tf_op jit(solution)/shard_map/all_to_all | solution.py:493
  554.1 0.0 copy-done.4
  554.1 32.4 %all_to_all.40 = bf16[16,12,1,8,384]{4,3,2,1,0:T(8,128)(2,1)} all-to-all(bf16[16,12,1,8,384]{4,3,2,1,0:T(8,128)(2,1)S(1)} %copy-done.4), channel_id=1, replica_groups=mesh['grp'=2,'slab'=16] {'slab'}, dimensions={0} | all-to-all | bytes 2359296 | tf_op jit(solution)/shard_map/all_to_all | solution.py:493
  586.5 10.2 %coils.9.c_ref = f32[192,8,384]{2,1,0:T(8,128)} custom-call(bf16[192,1,8,384]{3,2,1,0:T(8,128)(2,1)} %bitcast.49, f32[192,16,384]{2,1,0:T(8,128)} %warp.1.refs_1_, f32[384,256]{1,0:T(8,128)} %pad_maximum_fusion.2.refs_2_, bf16[384,512]{1,0:T(8,128)(2,1)} %constant.87.clone.refs_3_, bf16[384,384]{1,0:T(8,128)(2,1)} %constant.88.clone.refs_4_, ...), custom_call_target="tpu_custom_call" | custom-call | flops 3623878656 | bytes 15859712 | tf_op jit(solution)/shard_map/coils/pallas_call | solution.py:440
  596.8 15.6 %spread.3 = bf16[192,8,384]{2,1,0:T(8,128)(2,1)} custom-call(s32[1152]{0:T(1024)} %reshape.65.links, s32[16]{0:T(128)} %fusion.4.owner, f32[192,8,384]{2,1,0:T(8,128)} %coils.9.c_ref, bf16[576,72,128]{2,1,0:T(8,128)(2,1)} %all-gather.2.cloned.1.call-done.w_hbm), custom_call_target="tpu_custom_call" | custom-call | flops 2415919104 | bytes 20971520 | tf_op jit(solution)/shard_map/spread/pallas_call | solution.py:316
  612.4 33.8 %all_to_all.41.refs_1_ = bf16[16,12,8,384]{3,2,1,0:T(8,128)(2,1)} all-to-all(bf16[16,12,8,384]{3,2,1,0:T(8,128)(2,1)} %bitcast.46), channel_id=1, replica_groups=mesh['grp'=2,'slab'=16] {'slab'}, dimensions={0} | all-to-all | bytes 2359296 | tf_op jit(solution)/shard_map/all_to_all | solution.py:493
  646.2 6.4 update.1
  (14 shorter events, 0.1 us)
Async XLA Ops:
  11.2 6.7 %copy-start.6 = (s32[1,36,2]{1,2,0:T(2,128)S(1)}, s32[1,36,2]{1,2,0:T(2,128)}, u32[]{:S(2)}) copy-start(s32[1,36,2]{1,2,0:T(2,128)} %param.14) | copy-start | bytes 868
  11.2 87.2 %all-to-all-start = ((bf16[16,12,16,384]{3,2,1,0:T(8,128)(2,1)}), bf16[16,12,16,384]{3,2,1,0:T(8,128)(2,1)S(1)}, u32[]{:S(2)}, u32[]{:S(2)}) async-start(bf16[16,12,16,384]{3,2,1,0:T(8,128)(2,1)} %image_columns.1), calls=%async_computation | async-start | bytes 4718592 | tf_op jit(solution)/shard_map/all_to_all | solution.py:493
  26.5 70.7 %collective-permute-start = (bf16[36,72,128]{2,1,0:T(8,128)(2,1)S(1)}, bf16[36,72,128]{2,1,0:T(8,128)(2,1)S(1)}, u32[]{:S(2)}, u32[]{:S(2)}) collective-permute-start(bf16[36,72,128]{2,1,0:T(8,128)(2,1)S(1)} %pad_maximum_fusion.1), channel_id=1, source_target_pairs={{0,8},{1,9},{2,10},{3,11},{4,12},{5,13},{6,14},{7,15},{8,0},{9,1},... | collective-permute-start | bytes 1990664 | tf_op jit(solution)/shard_map/ppermute | solution.py:503
  98.4 1.4 copy-start
  99.8 213.4 %all-to-all-start.1 = ((bf16[16,12,4,16,384]{4,3,2,1,0:T(8,128)(2,1)}), bf16[16,12,4,16,384]{4,3,2,1,0:T(8,128)(2,1)}, u32[]{:S(2)}, u32[]{:S(2)}) async-start(bf16[16,12,4,16,384]{4,3,2,1,0:T(8,128)(2,1)} %maps_columns.3), calls=%async_computation.1 | async-start | bytes 18874368 | tf_op jit(solution)/shard_map/all_to_all | solution.py:493
  108.3 229.6 %all-gather.2.cloned.1.call-start = ((), (), s32[]{:S(2)}) async-start(), calls=%async_computation.8 | async-start | bytes 11943936 | tf_op jit(solution)/shard_map/all_gather | solution.py:511
  313.2 111.5 %all-to-all-start.2 = ((bf16[16,12,2,16,384]{4,3,2,1,0:T(8,128)(2,1)}), bf16[16,12,2,16,384]{4,3,2,1,0:T(8,128)(2,1)}, u32[]{:S(2)}, u32[]{:S(2)}) async-start(bf16[16,12,2,16,384]{4,3,2,1,0:T(8,128)(2,1)} %maps_columns.2), calls=%async_computation.2 | async-start | bytes 9437184 | tf_op jit(solution)/shard_map/all_to_all | solution.py:493
  321.0 15.5 %copy-start.5 = (s32[1,192,192]{2,1,0:T(8,128)S(1)}, s32[1,192,192]{2,1,0:T(8,128)}, u32[]{:S(2)}) copy-start(s32[1,192,192]{2,1,0:T(8,128)} %param.13) | copy-start | bytes 442372
  424.7 57.9 %all-to-all-start.3 = ((bf16[16,12,2,8,384]{4,3,2,1,0:T(8,128)(2,1)}), bf16[16,12,2,8,384]{4,3,2,1,0:T(8,128)(2,1)S(1)}, u32[]{:S(2)}, u32[]{:S(2)}) async-start(bf16[16,12,2,8,384]{4,3,2,1,0:T(8,128)(2,1)} %get-tuple-element.17), calls=%async_computation.3 | async-start | bytes 4718592 | tf_op jit(solution)/shard_map/all_to_all | solution.py:493
  482.6 1.4 copy-start.3
  484.0 36.3 %all-to-all-start.4 = ((bf16[16,12,1,8,384]{4,3,2,1,0:T(8,128)(2,1)}), bf16[16,12,1,8,384]{4,3,2,1,0:T(8,128)(2,1)S(1)}, u32[]{:S(2)}, u32[]{:S(2)}) async-start(bf16[16,12,1,8,384]{4,3,2,1,0:T(8,128)(2,1)} %get-tuple-element.19), calls=%async_computation.4 | async-start | bytes 2359296 | tf_op jit(solution)/shard_map/all_to_all | solution.py:493
  520.3 6.0 copy-start.2
  520.3 33.8 %all-to-all-start.5 = ((bf16[16,12,8,384]{3,2,1,0:T(8,128)(2,1)}), bf16[16,12,8,384]{3,2,1,0:T(8,128)(2,1)S(1)}, u32[]{:S(2)}, u32[]{:S(2)}) async-start(bf16[16,12,8,384]{3,2,1,0:T(8,128)(2,1)} %bitcast.45), calls=%async_computation.5 | async-start | bytes 2359296 | tf_op jit(solution)/shard_map/all_to_all | solution.py:493
  526.4 27.8 %copy-start.4 = (bf16[16,12,1,8,384]{4,3,2,1,0:T(8,128)(2,1)S(1)}, bf16[16,12,1,8,384]{4,3,2,1,0:T(8,128)(2,1)}, u32[]{:S(2)}) copy-start(bf16[16,12,1,8,384]{4,3,2,1,0:T(8,128)(2,1)} %get-tuple-element.22) | copy-start | bytes 3538948
  554.1 42.7 %copy-start.1 = (bf16[16,12,8,384]{3,2,1,0:T(8,128)(2,1)}, bf16[16,12,8,384]{3,2,1,0:T(8,128)(2,1)S(1)}, u32[]{:S(2)}) copy-start(bf16[16,12,8,384]{3,2,1,0:T(8,128)(2,1)S(1)} %all-to-all-done.5.refs_0_) | copy-start | bytes 3538948
Sparse Core Ops, SparseCore 0:
  110.8 173.1 all-gather.1

commit v5 on v4

--- a/solution.py
+++ b/solution.py
@@ -11,6 +11,7 @@
 
 BLK = 64
 LANES = 384
+TAIL = 16
 HALF = 256
 VMEM_LIMIT = 56 * 1024 * 1024
 BF = jnp.bfloat16
@@ -98,24 +99,9 @@
     spread_rows([o_ref.at[:, 0, 0]], to_rows(x_ref[0, :, 0]), scratch, count, deep)
 
 
-def last_maps_kernel(count, deep, x_ref, both_ref, first_ref, second_ref, scratch):
-    part = deep // 2
-    scratch[...] = to_rows(x_ref[0, :, 0]).astype(F32)
-    coil = pl.program_id(1)
-    for d in range(count):
-        both_ref[d, 0, 0] = scratch[pl.ds(d * deep, part), :].astype(BF)
-
-    def rest(out):
-        for d in range(count):
-            out[d, 0, 0] = scratch[pl.ds(d * deep + part, part), :].astype(BF)
-
-    @pl.when(coil == 0)
-    def _():
-        rest(first_ref)
-
-    @pl.when(coil == 1)
-    def _():
-        rest(second_ref)
+def last_maps_kernel(count, deep, x_ref, first_ref, second_ref, scratch):
+    outs = [first_ref.at[:, 0, 0], second_ref.at[:, 0, 0]]
+    spread_rows(outs, to_rows(x_ref[0, :, 0]), scratch, count, deep)
 
 
 def maps_columns(coil_maps, count, first, coils):
@@ -136,26 +122,20 @@
     )(coil_maps)
 
 
-def last_maps_columns(coil_maps, count, first):
+def last_maps_columns(coil_maps, count, first, coils):
     _, _, planes, ny, nz = coil_maps.shape
     deep = nz // count
     part = deep // 2
-    shapes = [(count, planes, coils, part, LANES) for coils in (2, 1, 1)]
-    alone = pl.BlockSpec((count, 1, 1, part, LANES), lambda x, c: (0, x, 0, 0, 0))
     return pl.pallas_call(
         functools.partial(last_maps_kernel, count, deep),
-        out_shape=[jax.ShapeDtypeStruct(shape, BF) for shape in shapes],
-        grid=(planes, 2),
+        out_shape=[jax.ShapeDtypeStruct((count, planes, coils, part, LANES), BF)] * 2,
+        grid=(planes, coils),
         in_specs=[pl.BlockSpec((1, 2, 1, ny, nz), lambda x, c: (first + c, 0, x, 0, 0))],
-        out_specs=[
-            pl.BlockSpec((count, 1, 1, part, LANES), lambda x, c: (0, x, c, 0, 0)),
-            alone,
-            alone,
-        ],
+        out_specs=[pl.BlockSpec((count, 1, 1, part, LANES), lambda x, c: (0, x, c, 0, 0))] * 2,
         scratch_shapes=[pltpu.VMEM((nz, LANES), F32)],
         compiler_params=params(),
         cost_estimate=pl.CostEstimate(
-            flops=0, bytes_accessed=4 * planes * ny * nz * 4, transcendentals=0
+            flops=0, bytes_accessed=coils * 2 * planes * ny * nz * 4, transcendentals=0
         ),
         name="last_maps_columns",
     )(coil_maps)
@@ -167,8 +147,8 @@
 
 def fetch(w_hbm, held, sems, k):
     size = held.shape[0] // sems.shape[0]
-    at = pl.ds(k * size, size)
-    return pltpu.make_async_copy(w_hbm.at[at, pl.ds(0, BLK), :], held.at[at], sems.at[k])
+    source = w_hbm.at[pl.ds(k * (size + TAIL), size)]
+    return pltpu.make_async_copy(source, held.at[pl.ds(k * size, size)], sems.at[k])
 
 
 def fetch_all(w_hbm, held, sems):
@@ -206,11 +186,13 @@
         for x in range(planes):
             outs = []
             for b in range(3):
-                t = start + 3 * x + b
-                both = jnp.where(low_both, twice[links[2 * t]], twice[links[2 * t + 1]])
+                t = 3 * x + b
+                one, two = links[2 * start + t], links[2 * start + 3 * planes + t]
+                both = jnp.where(low_both, twice[one], twice[two])
+                weight = held[pl.ds((start + t) * BLK, BLK), :]
                 outs.append(
                     lax.dot_general(
-                        both, held[t], (((1,), (1,)), ((), ())), preferred_element_type=F32
+                        both, weight, (((1,), (1,)), ((), ())), preferred_element_type=F32
                     )
                 )
             a, b, c = outs
@@ -227,7 +209,7 @@
 
 def warp(columns, weights, links, owner):
     nx, deep, _ = columns.shape
-    blocks = weights.shape[0]
+    blocks = 3 * nx
     pad = max(16, deep)
     whole = pl.BlockSpec((nx, deep, LANES), lambda i, l, p: (0, 0, 0))
     return pl.pallas_call(
@@ -239,7 +221,7 @@
             in_specs=[whole, pl.BlockSpec(memory_space=pl.ANY)],
             out_specs=whole,
             scratch_shapes=[
-                pltpu.VMEM((blocks, BLK, 2 * BLK), BF),
+                pltpu.VMEM((blocks * BLK, 2 * BLK), BF),
                 pltpu.VMEM((blocks, 2 * pad, 128), BF),
                 pltpu.SemaphoreType.DMA((owner.shape[0],)),
             ],
@@ -282,11 +264,13 @@
                 tall(rest[:, :BLK], rest[:, BLK:]),
             )
             for b in range(3):
-                t = start + 3 * x + b
-                out = jnp.dot(tiles[b].astype(BF), held[t], preferred_element_type=F32)
+                t = 3 * x + b
+                one, two = links[2 * start + t], links[2 * start + 3 * planes + t]
+                weight = held[pl.ds((start + t) * BLK, BLK), :]
+                out = jnp.dot(tiles[b].astype(BF), weight, preferred_element_type=F32)
                 zero = jnp.zeros_like(out)
-                total[links[2 * t]] += jnp.where(low, out, zero)
-                total[links[2 * t + 1]] += jnp.where(low, zero, out)
+                total[one] += jnp.where(low, out, zero)
+                total[two] += jnp.where(low, zero, out)
         return carry
 
     lax.fori_loop(0, count, block, 0)
@@ -310,7 +294,7 @@
 
 def spread(combined, weights, links, owner):
     nx, deep, _ = combined.shape
-    blocks = weights.shape[0]
+    blocks = 3 * nx
     pad = max(8, deep)
     whole = pl.BlockSpec((nx, deep, LANES), lambda i, l, p: (0, 0, 0))
     return pl.pallas_call(
@@ -322,7 +306,7 @@
             in_specs=[whole, pl.BlockSpec(memory_space=pl.ANY)],
             out_specs=whole,
             scratch_shapes=[
-                pltpu.VMEM((blocks, BLK, 2 * BLK), BF),
+                pltpu.VMEM((blocks * BLK, 2 * BLK), BF),
                 pltpu.VMEM((blocks, 2 * pad, 128), F32),
                 pltpu.SemaphoreType.DMA((owner.shape[0],)),
             ],
@@ -524,24 +508,17 @@
     sampled = jnp.pad(masks[0].astype(F32), ((0, 0), (0, HALF - ny)))
     mask = jnp.concatenate([sampled, sampled], axis=0)
 
-    matrices = weights[0].reshape(3 * planes, 2, BLK, BLK)
-    matrices = jnp.transpose(matrices, (0, 2, 1, 3)).reshape(3 * planes, BLK, 2 * BLK)
-    digits = jnp.concatenate([sources[0] // BLK, sources[0] % BLK], axis=1).astype(BF)
-    digits = jnp.pad(digits[:, None, :], ((0, 0), (0, 7), (0, 2 * BLK - 4)))
-    pair = swap_halves(jnp.concatenate([matrices, digits], axis=1))
+    targets = 3 * planes
+    matrices = weights[0].reshape(targets, 2, BLK, BLK)
+    matrices = jnp.transpose(matrices, (0, 2, 1, 3)).reshape(targets * BLK, 2 * BLK)
+    chosen = sources[0].T
+    digits = jnp.concatenate([chosen // BLK, chosen % BLK], axis=0).astype(BF)
+    digits = jnp.pad(digits, ((0, TAIL - 4), (0, 2 * BLK - targets)))
+    pair = swap_halves(jnp.concatenate([matrices, digits], axis=0))
     packed, owner = gather_half(pair)
-    digits = packed[:, BLK, :4].astype(jnp.int32)
+    digits = packed.reshape(count, targets * BLK + TAIL, 2 * BLK)[:, targets * BLK :]
+    digits = digits[:, :4, :targets].astype(jnp.int32)
     links = (digits[:, :2] * BLK + digits[:, 2:]).reshape(-1)
-
-    columns = exchange(image_columns(image, count))
-    halves = deep % 16 == 0
-    sizes = [total // 2, total // 4] if halves else [total // 2, total // 4, total // 8]
-    sizes += [] if halves else [total - sum(sizes)]
-    outgoing = []
-    for i, size in enumerate(sizes):
-        outgoing.append(maps_columns(coil_maps, count, sum(sizes[:i]), size))
-    last = columns
-    warped = warp(columns.reshape(nx, deep, LANES), packed, links, owner)
 
     def run(received, before, part):
         size = received.shape[2]
@@ -551,27 +528,26 @@
         grad = spread(combined, packed, links, owner)
         return exchange(after(grad, *needs).reshape(count, planes, -1, LANES))
 
-    combined, waiting, ready = None, None, []
-    for piece in outgoing:
-        arrived = exchange(after(piece, last, pair, *ready))
-        if waiting is not None:
-            combined = run(waiting, combined, 0)
-            ready = [combined]
-        last = waiting = arrived
+    columns = exchange(image_columns(image, count))
+    warped = warp(columns.reshape(nx, deep, LANES), packed, links, owner)
+    halves = deep % 16 == 0
+    early = total - total // 4 if halves else total - 1
+    late = total - early
+    maps = maps_columns(coil_maps, count, 0, early)
+    arrived = exchange(after(maps, columns, pair))
     if not halves:
-        combined = run(waiting, combined, 0)
+        maps = maps_columns(coil_maps, count, early, late)
+        last = exchange(after(maps, arrived, warped))
+        combined = run(last, run(arrived, None, 0), 0)
         return update([back(combined)], image, adjoint_data)
 
-    both, first, second = last_maps_columns(coil_maps, count, sum(sizes))
-    got_both = exchange(after(both, last, *ready))
-    combined = run(waiting, combined, 0)
-    got_first = exchange(after(first, got_both, combined))
-    half = run(got_both, combined, 0)
-    back_first = back(half, got_first)
-    half = run(got_first, combined, 1)
-    got_second = exchange(after(second, back_first, half))
-    half = run(got_second, half, 1)
-    return update([back_first, back(half)], image, adjoint_data)
+    first, second = last_maps_columns(coil_maps, count, early, late)
+    first = exchange(after(first, arrived, warped))
+    combined = run(arrived, None, 0)
+    second = exchange(after(second, first, combined))
+    back_first = back(run(first, combined, 0), second)
+    back_second = back(run(second, combined, 1), back_first)
+    return update([back_first, back_second], image, adjoint_data)
 
 
 def solution(mesh):

time: 665 us -> 648 us (0.974)
  waiting for transfers between devices: 279 us -> 319 us
  blocking collectives: 66.2 us -> 33.8 us
  Pallas kernels: 243 us -> 230 us
  starting transfers between devices: 41 us -> 33.4 us
    all_gather x1, waiting for transfers between devices: 0.01 us -> 131 us  [gather_half(): lax.all_gather(pair, 'slab', axis=0, tiled=True, axis_index_groups=groups)]
    all_to_all x6 -> x5, waiting for transfers between devices: 239 us -> 163 us  [exchange(): lax.all_to_all(parts, 'slab', split_axis=0, concat_axis=0, tiled=True)]
    all_to_all x2 -> x1, blocking collectives: 66.2 us -> 33.8 us  [exchange(): lax.all_to_all(parts, 'slab', split_axis=0, concat_axis=0, tiled=True)]
    ppermute x1, waiting for transfers between devices: 39.3 us -> 23.7 us  [swap_halves(): other = lax.ppermute(value, 'slab', [(i, i ^ half) for i in range(count)])]
    pallas_call x5 -> x3, Pallas kernels: 125 us -> 113 us  [coils(): pl.pallas_call(functools.partial(coil_kernel, nx, deep, pad, fresh), out_...]
    all_to_all x6 -> x5, starting transfers between devices: 38.8 us -> 31.3 us  [exchange(): lax.all_to_all(parts, 'slab', split_axis=0, concat_axis=0, tiled=True)]
    pallas_call x2 -> x1, Pallas kernels: 44.6 us -> 43.4 us  [maps_columns(): pl.pallas_call(functools.partial(maps_kernel, count, deep), out_shape=jax...]
  transfers between devices with their start and end apart: 8 -> 7, of which waited for: 5 -> 4; matrix products, arithmetic and copies ran while one was open for 2% -> 2% of each run, Pallas kernels for 31% -> 34%
where the time goes in v5:
time: 648 us; the launch traced here: 643 us
  waiting for transfers between devices  319 us (49%)
  Pallas kernels  230 us (35%)
  blocking collectives  33.8 us (5%)
  starting transfers between devices  33.4 us (5%)
  between operations  13.5 us (2%)
  local copies, waits for them, and re-layouts  10.6 us (2%)
    all_to_all x5, waiting for transfers between devices, exchange(): lax.all_to_all(parts, 'slab', split_axis=0, concat_axis=0, tiled=True)  163 us
    all_gather x1, waiting for transfers between devices, gather_half(): lax.all_gather(pair, 'slab', axis=0, tiled=True, axis_index_groups=groups)  131 us
    pallas_call x3, Pallas kernels, coils(): pl.pallas_call(functools.partial(coil_kernel, nx, deep, pad, fresh), out_...  113 us
    pallas_call x1, Pallas kernels, maps_columns(): pl.pallas_call(functools.partial(maps_kernel, count, deep), out_shape=jax...  43.4 us
    all_to_all x1, blocking collectives, exchange(): lax.all_to_all(parts, 'slab', split_axis=0, concat_axis=0, tiled=True)  33.8 us
    pallas_call x2, Pallas kernels, spread(): pl.pallas_call(functools.partial(spread_kernel, nx, deep, pad), out_shape...  31.3 us
    all_to_all x5, starting transfers between devices, exchange(): lax.all_to_all(parts, 'slab', split_axis=0, concat_axis=0, tiled=True)  31.3 us
    ppermute x1, waiting for transfers between devices, swap_halves(): other = lax.ppermute(value, 'slab', [(i, i ^ half) for i in range(count)])  23.7 us
  transfers between devices with their start and end apart: 7, of which 4 were waited for; matrix products, arithmetic and copies ran while one was open for 2% of the time, Pallas kernels for 34%

profile of v5, /device:TPU:13, one launch (start us, length us, event | category | flops | bytes accessed | tf_op | source)
XLA Modules:
  0.0 642.8 jit_solution(11224046305695413602)
XLA Ops:
  6.5 4.7 image_columns.1
  11.2 6.6 %all-to-all-start = ((bf16[16,12,16,384]{3,2,1,0:T(8,128)(2,1)}), bf16[16,12,16,384]{3,2,1,0:T(8,128)(2,1)S(1)}, u32[]{:S(2)}, u32[]{:S(2)}) async-start(bf16[16,12,16,384]{3,2,1,0:T(8,128)(2,1)} %image_columns.1), calls=%async_computation | async-start | bytes 4718592 | tf_op jit(solution)/shard_map/all_to_all | solution.py:477
  17.8 2.2 reshape_squeeze.3
  20.0 0.0 copy-start.5
  20.0 2.3 copy.13
  22.2 2.6 reshape.28
  24.8 0.0 copy-done.5
  24.9 2.2 collective-permute-start
  27.0 43.4 %maps_columns.1 = bf16[16,12,6,16,384]{4,3,2,1,0:T(8,128)(2,1)} custom-call(bf16[8,2,12,192,256]{4,3,2,1,0:T(8,128)(2,1)} %x_ref.4), custom_call_target="tpu_custom_call" | custom-call | bytes 28311552 | tf_op jit(solution)/shard_map/maps_columns/pallas_call | solution.py:110
  70.4 23.7 %collective-permute-done = bf16[2320,128]{1,0:T(8,128)(2,1)S(1)} collective-permute-done((bf16[2320,128]{1,0:T(8,128)(2,1)S(1)}, bf16[2320,128]{1,0:T(8,128)(2,1)S(1)}, u32[]{:S(2)}, u32[]{:S(2)}) %collective-permute-start) | collective-permute-done | bytes 593952 | tf_op jit(solution)/shard_map/ppermute | solution.py:487
  94.1 1.1 pad_maximum_fusion
  95.1 0.0 all-to-all-done
  95.1 0.0 copy-start
  95.1 1.4 copy-done
  96.6 8.7 %all-to-all-start.1 = ((bf16[16,12,6,16,384]{4,3,2,1,0:T(8,128)(2,1)}), bf16[16,12,6,16,384]{4,3,2,1,0:T(8,128)(2,1)}, u32[]{:S(2)}, u32[]{:S(2)}) async-start(bf16[16,12,6,16,384]{4,3,2,1,0:T(8,128)(2,1)} %maps_columns.1), calls=%async_computation.1 | async-start | bytes 28311552 | tf_op jit(solution)/shard_map/all_to_all | solution.py:477
  105.3 0.0 all-gather.2.cloned.1.call-start
  105.3 0.7 all-gather.2.cloned.1.call-update
  106.0 15.4 %last_maps_columns.1 = (bf16[16,12,2,8,384]{4,3,2,1,0:T(8,128)(2,1)}, bf16[16,12,2,8,384]{4,3,2,1,0:T(8,128)(2,1)}) custom-call(bf16[8,2,12,192,256]{4,3,2,1,0:T(8,128)(2,1)} %x_ref.4), custom_call_target="tpu_custom_call" | custom-call | bytes 9437184 | tf_op jit(solution)/shard_map/last_maps_columns/pallas_call | solution.py:129
  121.5 0.5 fusion.10.owner
  122.0 130.9 %all-gather.2.cloned.1.call-done.w_hbm = bf16[37120,128]{1,0:T(8,128)(2,1)} async-done(((bf16[4640,128]{1,0:T(8,128)(2,1)}), bf16[37120,128]{1,0:T(8,128)(2,1)}) %all-gather.2.cloned.1.call-update) | async-done | bytes 9502736 | tf_op jit(solution)/shard_map/all_gather | solution.py:495
  252.9 0.8 slice_convert_fusion
  253.7 0.7 reshape.30.links
  254.4 15.0 %warp.1.refs_1_ = f32[192,16,384]{2,1,0:T(8,128)} custom-call(s32[1152]{0:T(1024)} %reshape.30.links, s32[16]{0:T(128)} %fusion.10.owner, bf16[192,16,384]{2,1,0:T(8,128)(2,1)} %bitcast.37, bf16[37120,128]{1,0:T(8,128)(2,1)} %all-gather.2.cloned.1.call-done.w_hbm), custom_call_target="tpu_custom_call" | custom-call | flops 2415919104 | bytes 20971520 | tf_op jit(solution)/shard_map/warp/pallas_call | solution.py:215
  269.4 141.8 %all-to-all-done.1 = bf16[16,12,6,16,384]{4,3,2,1,0:T(8,128)(2,1)} async-done(((bf16[16,12,6,16,384]{4,3,2,1,0:T(8,128)(2,1)}), bf16[16,12,6,16,384]{4,3,2,1,0:T(8,128)(2,1)}, u32[]{:S(2)}, u32[]{:S(2)}) %all-to-all-start.1) | async-done | bytes 14155808 | tf_op jit(solution)/shard_map/all_to_all | solution.py:477
  411.2 0.0 copy-start.4
  411.2 5.1 all-to-all-start.2
  416.3 0.0 copy-done.4
  416.3 0.8 pad_maximum_fusion.2.refs_2_
  417.1 81.8 %coils.3.refs_7_ = f32[192,16,384]{2,1,0:T(8,128)} custom-call(bf16[192,6,16,384]{3,2,1,0:T(8,128)(2,1)} %bitcast.8.refs_0_, f32[192,16,384]{2,1,0:T(8,128)} %warp.1.refs_1_, f32[384,256]{1,0:T(8,128)} %pad_maximum_fusion.2.refs_2_, bf16[384,512]{1,0:T(8,128)(2,1)} %constant.87.clone.refs_3_, bf16[384,384]{1,0:T(8,128)(2,1)} %constant.88.clone.refs_4_, ...), custom_call_target="tpu_custom_call" | custom-call | flops 43486543872 | bytes 28835840 | tf_op jit(solution)/shard_map/coils/pallas_call | solution.py:424
  498.9 0.0 all-to-all-done.2
  498.9 0.0 copy-start.3
  498.9 1.4 copy-done.3
  500.4 6.0 all-to-all-start.3
  506.4 15.7 %coils.4.c_ref = f32[192,8,384]{2,1,0:T(8,128)} custom-call(bf16[192,2,8,384]{3,2,1,0:T(8,128)(2,1)} %bitcast.42, f32[192,16,384]{2,1,0:T(8,128)} %warp.1.refs_1_, f32[384,256]{1,0:T(8,128)} %pad_maximum_fusion.2.refs_2_, bf16[384,512]{1,0:T(8,128)(2,1)} %constant.87.clone.refs_3_, bf16[384,384]{1,0:T(8,128)(2,1)} %constant.88.clone.refs_4_, ...), custom_call_target="tpu_custom_call" | custom-call | flops 7247757312 | bytes 17039360 | tf_op jit(solution)/shard_map/coils/pallas_call | solution.py:424
  522.1 15.7 %spread.2 = bf16[192,8,384]{2,1,0:T(8,128)(2,1)} custom-call(s32[1152]{0:T(1024)} %reshape.30.links, s32[16]{0:T(128)} %fusion.10.owner, f32[192,8,384]{2,1,0:T(8,128)} %coils.4.c_ref, bf16[37120,128]{1,0:T(8,128)(2,1)} %all-gather.2.cloned.1.call-done.w_hbm), custom_call_target="tpu_custom_call" | custom-call | flops 2415919104 | bytes 20971520 | tf_op jit(solution)/shard_map/spread/pallas_call | solution.py:300
  537.8 21.6 %all-to-all-done.3 = bf16[16,12,2,8,384]{4,3,2,1,0:T(8,128)(2,1)S(1)} async-done(((bf16[16,12,2,8,384]{4,3,2,1,0:T(8,128)(2,1)}), bf16[16,12,2,8,384]{4,3,2,1,0:T(8,128)(2,1)S(1)}, u32[]{:S(2)}, u32[]{:S(2)}) %all-to-all-start.3) | async-done | bytes 2359328 | tf_op jit(solution)/shard_map/all_to_all | solution.py:477
  559.4 0.0 copy-start.2
  559.4 4.9 all-to-all-start.4
  564.3 0.0 copy-done.2
  564.3 15.8 %coils.5.c_ref = f32[192,8,384]{2,1,0:T(8,128)} custom-call(bf16[192,2,8,384]{3,2,1,0:T(8,128)(2,1)} %bitcast.41, f32[192,16,384]{2,1,0:T(8,128)} %warp.1.refs_1_, f32[384,256]{1,0:T(8,128)} %pad_maximum_fusion.2.refs_2_, bf16[384,512]{1,0:T(8,128)(2,1)} %constant.87.clone.refs_3_, bf16[384,384]{1,0:T(8,128)(2,1)} %constant.88.clone.refs_4_, ...), custom_call_target="tpu_custom_call" | custom-call | flops 7247757312 | bytes 17039360 | tf_op jit(solution)/shard_map/coils/pallas_call | solution.py:424
  580.2 15.6 %spread.3 = bf16[192,8,384]{2,1,0:T(8,128)(2,1)} custom-call(s32[1152]{0:T(1024)} %reshape.30.links, s32[16]{0:T(128)} %fusion.10.owner, f32[192,8,384]{2,1,0:T(8,128)} %coils.5.c_ref, bf16[37120,128]{1,0:T(8,128)(2,1)} %all-gather.2.cloned.1.call-done.w_hbm), custom_call_target="tpu_custom_call" | custom-call | flops 2415919104 | bytes 20971520 | tf_op jit(solution)/shard_map/spread/pallas_call | solution.py:300
  595.8 0.0 all-to-all-done.4.refs_0_
  595.8 0.0 copy-start.1
  595.8 33.8 %all_to_all.30.refs_1_ = bf16[16,12,8,384]{3,2,1,0:T(8,128)(2,1)} all-to-all(bf16[16,12,8,384]{3,2,1,0:T(8,128)(2,1)} %bitcast.39), channel_id=1, replica_groups=mesh['grp'=2,'slab'=16] {'slab'}, dimensions={0} | all-to-all | bytes 2359296 | tf_op jit(solution)/shard_map/all_to_all | solution.py:477
  629.6 0.0 copy-done.1
  629.6 6.4 update.1
  (6 shorter events, 0.1 us)
Async XLA Ops:
  11.2 83.9 %all-to-all-start = ((bf16[16,12,16,384]{3,2,1,0:T(8,128)(2,1)}), bf16[16,12,16,384]{3,2,1,0:T(8,128)(2,1)S(1)}, u32[]{:S(2)}, u32[]{:S(2)}) async-start(bf16[16,12,16,384]{3,2,1,0:T(8,128)(2,1)} %image_columns.1), calls=%async_computation | async-start | bytes 4718592 | tf_op jit(solution)/shard_map/all_to_all | solution.py:477
  20.0 4.8 copy-start.5
  24.9 69.2 %collective-permute-start = (bf16[2320,128]{1,0:T(8,128)(2,1)S(1)}, bf16[2320,128]{1,0:T(8,128)(2,1)S(1)}, u32[]{:S(2)}, u32[]{:S(2)}) collective-permute-start(bf16[2320,128]{1,0:T(8,128)(2,1)S(1)} %pad_maximum_fusion.1), channel_id=1, source_target_pairs={{0,8},{1,9},{2,10},{3,11},{4,12},{5,13},{6,14},{7,15},{8,0},{9,1},... | collective-permute-start | bytes 1781768 | tf_op jit(solution)/shard_map/ppermute | solution.py:487
  95.1 1.4 copy-start
  96.6 314.7 %all-to-all-start.1 = ((bf16[16,12,6,16,384]{4,3,2,1,0:T(8,128)(2,1)}), bf16[16,12,6,16,384]{4,3,2,1,0:T(8,128)(2,1)}, u32[]{:S(2)}, u32[]{:S(2)}) async-start(bf16[16,12,6,16,384]{4,3,2,1,0:T(8,128)(2,1)} %maps_columns.1), calls=%async_computation.1 | async-start | bytes 28311552 | tf_op jit(solution)/shard_map/all_to_all | solution.py:477
  105.3 147.6 %all-gather.2.cloned.1.call-start = ((), (), s32[]{:S(2)}) async-start(), calls=%async_computation.6 | async-start | bytes 10690560 | tf_op jit(solution)/shard_map/all_gather | solution.py:495
  411.2 5.1 copy-start.4
  411.2 87.7 %all-to-all-start.2 = ((bf16[16,12,2,8,384]{4,3,2,1,0:T(8,128)(2,1)}), bf16[16,12,2,8,384]{4,3,2,1,0:T(8,128)(2,1)S(1)}, u32[]{:S(2)}, u32[]{:S(2)}) async-start(bf16[16,12,2,8,384]{4,3,2,1,0:T(8,128)(2,1)} %get-tuple-element.14), calls=%async_computation.2 | async-start | bytes 4718592 | tf_op jit(solution)/shard_map/all_to_all | solution.py:477
  498.9 1.4 copy-start.3
  500.4 59.1 %all-to-all-start.3 = ((bf16[16,12,2,8,384]{4,3,2,1,0:T(8,128)(2,1)}), bf16[16,12,2,8,384]{4,3,2,1,0:T(8,128)(2,1)S(1)}, u32[]{:S(2)}, u32[]{:S(2)}) async-start(bf16[16,12,2,8,384]{4,3,2,1,0:T(8,128)(2,1)} %get-tuple-element.16), calls=%async_computation.3 | async-start | bytes 4718592 | tf_op jit(solution)/shard_map/all_to_all | solution.py:477
  559.4 4.9 copy-start.2
  559.4 36.4 %all-to-all-start.4 = ((bf16[16,12,8,384]{3,2,1,0:T(8,128)(2,1)}), bf16[16,12,8,384]{3,2,1,0:T(8,128)(2,1)S(1)}, u32[]{:S(2)}, u32[]{:S(2)}) async-start(bf16[16,12,8,384]{3,2,1,0:T(8,128)(2,1)} %bitcast.38), calls=%async_computation.4 | async-start | bytes 2359296 | tf_op jit(solution)/shard_map/all_to_all | solution.py:477
  595.8 33.8 %copy-start.1 = (bf16[16,12,8,384]{3,2,1,0:T(8,128)(2,1)}, bf16[16,12,8,384]{3,2,1,0:T(8,128)(2,1)S(1)}, u32[]{:S(2)}) copy-start(bf16[16,12,8,384]{3,2,1,0:T(8,128)(2,1)S(1)} %all-to-all-done.4.refs_0_) | copy-start | bytes 3538948
Sparse Core Ops, SparseCore 0:
  107.7 145.1 all-gather.1

commit v6 on v5

--- a/solution.py
+++ b/solution.py
@@ -531,7 +531,7 @@
     columns = exchange(image_columns(image, count))
     warped = warp(columns.reshape(nx, deep, LANES), packed, links, owner)
     halves = deep % 16 == 0
-    early = total - total // 4 if halves else total - 1
+    early = total - 3 * total // 8 if halves else total - 1
     late = total - early
     maps = maps_columns(coil_maps, count, 0, early)
     arrived = exchange(after(maps, columns, pair))

time: 648 us -> 625 us (0.965)
  waiting for transfers between devices: 319 us -> 296 us
    all_to_all x5, waiting for transfers between devices: 163 us -> 123 us  [exchange(): lax.all_to_all(parts, 'slab', split_axis=0, concat_axis=0, tiled=True)]
    all_gather x1, waiting for transfers between devices: 131 us -> 142 us  [gather_half(): lax.all_gather(pair, 'slab', axis=0, tiled=True, axis_index_groups=groups)]
    pallas_call x1, Pallas kernels: 15.4 us -> 22.5 us  [last_maps_columns(): pl.pallas_call(functools.partial(last_maps_kernel, count, deep), out_shap...]
    pallas_call x1, Pallas kernels: 43.4 us -> 36.4 us  [maps_columns(): pl.pallas_call(functools.partial(maps_kernel, count, deep), out_shape=jax...]
    ppermute x1, waiting for transfers between devices: 23.7 us -> 30.6 us  [swap_halves(): other = lax.ppermute(value, 'slab', [(i, i ^ half) for i in range(count)])]
  transfers between devices with their start and end apart: 7 -> 7, of which waited for: 4 -> 5; matrix products, arithmetic and copies ran while one was open for 2% -> 2% of each run, Pallas kernels for 34% -> 35%
where the time goes in v6:
time: 625 us; the launch traced here: 620 us
  waiting for transfers between devices  296 us (47%)
  Pallas kernels  228 us (36%)
  blocking collectives  33.8 us (5%)
  starting transfers between devices  31.2 us (5%)
  between operations  13.5 us (2%)
  local copies, waits for them, and re-layouts  12.7 us (2%)
    all_gather x1, waiting for transfers between devices, gather_half(): lax.all_gather(pair, 'slab', axis=0, tiled=True, axis_index_groups=groups)  142 us
    all_to_all x5, waiting for transfers between devices, exchange(): lax.all_to_all(parts, 'slab', split_axis=0, concat_axis=0, tiled=True)  123 us
    pallas_call x3, Pallas kernels, coils(): pl.pallas_call(functools.partial(coil_kernel, nx, deep, pad, fresh), out_...  112 us
    pallas_call x1, Pallas kernels, maps_columns(): pl.pallas_call(functools.partial(maps_kernel, count, deep), out_shape=jax...  36.4 us
    all_to_all x1, blocking collectives, exchange(): lax.all_to_all(parts, 'slab', split_axis=0, concat_axis=0, tiled=True)  33.8 us
    pallas_call x2, Pallas kernels, spread(): pl.pallas_call(functools.partial(spread_kernel, nx, deep, pad), out_shape...  31.3 us
    ppermute x1, waiting for transfers between devices, swap_halves(): other = lax.ppermute(value, 'slab', [(i, i ^ half) for i in range(count)])  30.6 us
    all_to_all x5, starting transfers between devices, exchange(): lax.all_to_all(parts, 'slab', split_axis=0, concat_axis=0, tiled=True)  29.1 us
  transfers between devices with their start and end apart: 7, of which 5 were waited for; matrix products, arithmetic and copies ran while one was open for 2% of the time, Pallas kernels for 35%

profile of v6, /device:TPU:13, one launch (start us, length us, event | category | flops | bytes accessed | tf_op | source)
XLA Modules:
  0.0 620.0 jit_solution(8185300386726991066)
XLA Ops:
  6.5 4.7 image_columns.1
  11.2 6.6 %all-to-all-start = ((bf16[16,12,16,384]{3,2,1,0:T(8,128)(2,1)}), bf16[16,12,16,384]{3,2,1,0:T(8,128)(2,1)S(1)}, u32[]{:S(2)}, u32[]{:S(2)}) async-start(bf16[16,12,16,384]{3,2,1,0:T(8,128)(2,1)} %image_columns.1), calls=%async_computation | async-start | bytes 4718592 | tf_op jit(solution)/shard_map/all_to_all | solution.py:477
  17.8 2.2 reshape_squeeze.3
  20.0 0.0 copy-start.4
  20.0 2.3 copy.13
  22.2 2.6 reshape.28
  24.8 0.0 copy-done.4
  24.9 2.2 collective-permute-start
  27.0 36.4 %maps_columns.1 = bf16[16,12,5,16,384]{4,3,2,1,0:T(8,128)(2,1)} custom-call(bf16[8,2,12,192,256]{4,3,2,1,0:T(8,128)(2,1)} %x_ref.4), custom_call_target="tpu_custom_call" | custom-call | bytes 23592960 | tf_op jit(solution)/shard_map/maps_columns/pallas_call | solution.py:110
  63.4 30.6 %collective-permute-done = bf16[2320,128]{1,0:T(8,128)(2,1)S(1)} collective-permute-done((bf16[2320,128]{1,0:T(8,128)(2,1)S(1)}, bf16[2320,128]{1,0:T(8,128)(2,1)S(1)}, u32[]{:S(2)}, u32[]{:S(2)}) %collective-permute-start) | collective-permute-done | bytes 593952 | tf_op jit(solution)/shard_map/ppermute | solution.py:487
  94.1 1.1 pad_maximum_fusion
  95.2 0.0 all-to-all-done
  95.2 0.0 copy-start
  95.2 1.4 copy-done
  96.7 8.6 %all-to-all-start.1 = ((bf16[16,12,5,16,384]{4,3,2,1,0:T(8,128)(2,1)}), bf16[16,12,5,16,384]{4,3,2,1,0:T(8,128)(2,1)}, u32[]{:S(2)}, u32[]{:S(2)}) async-start(bf16[16,12,5,16,384]{4,3,2,1,0:T(8,128)(2,1)} %maps_columns.1), calls=%async_computation.1 | async-start | bytes 23592960 | tf_op jit(solution)/shard_map/all_to_all | solution.py:477
  105.3 0.0 all-gather.2.cloned.1.call-start
  105.3 0.7 all-gather.2.cloned.1.call-update
  106.0 22.5 %last_maps_columns.1 = (bf16[16,12,3,8,384]{4,3,2,1,0:T(8,128)(2,1)}, bf16[16,12,3,8,384]{4,3,2,1,0:T(8,128)(2,1)}) custom-call(bf16[8,2,12,192,256]{4,3,2,1,0:T(8,128)(2,1)} %x_ref.4), custom_call_target="tpu_custom_call" | custom-call | bytes 14155776 | tf_op jit(solution)/shard_map/last_maps_columns/pallas_call | solution.py:129
  128.5 0.6 fusion.10.owner
  129.1 142.4 %all-gather.2.cloned.1.call-done.w_hbm = bf16[37120,128]{1,0:T(8,128)(2,1)} async-done(((bf16[4640,128]{1,0:T(8,128)(2,1)}), bf16[37120,128]{1,0:T(8,128)(2,1)}) %all-gather.2.cloned.1.call-update) | async-done | bytes 9502736 | tf_op jit(solution)/shard_map/all_gather | solution.py:495
  271.5 0.8 slice_convert_fusion
  272.3 0.7 reshape.30.links
  273.0 15.1 %warp.1.refs_1_ = f32[192,16,384]{2,1,0:T(8,128)} custom-call(s32[1152]{0:T(1024)} %reshape.30.links, s32[16]{0:T(128)} %fusion.10.owner, bf16[192,16,384]{2,1,0:T(8,128)(2,1)} %bitcast.37, bf16[37120,128]{1,0:T(8,128)(2,1)} %all-gather.2.cloned.1.call-done.w_hbm), custom_call_target="tpu_custom_call" | custom-call | flops 2415919104 | bytes 20971520 | tf_op jit(solution)/shard_map/warp/pallas_call | solution.py:215
  288.1 73.8 %all-to-all-done.1 = bf16[16,12,5,16,384]{4,3,2,1,0:T(8,128)(2,1)} async-done(((bf16[16,12,5,16,384]{4,3,2,1,0:T(8,128)(2,1)}), bf16[16,12,5,16,384]{4,3,2,1,0:T(8,128)(2,1)}, u32[]{:S(2)}, u32[]{:S(2)}) %all-to-all-start.1) | async-done | bytes 11796512 | tf_op jit(solution)/shard_map/all_to_all | solution.py:477
  361.9 4.1 all-to-all-start.2
  366.0 0.9 convert_bitcast_fusion
  366.9 0.8 pad_maximum_fusion.2.refs_2_
  367.7 69.1 %coils.3.refs_7_ = f32[192,16,384]{2,1,0:T(8,128)} custom-call(bf16[192,5,16,384]{3,2,1,0:T(8,128)(2,1)} %bitcast.8.refs_0_, f32[192,16,384]{2,1,0:T(8,128)} %warp.1.refs_1_, f32[384,256]{1,0:T(8,128)} %pad_maximum_fusion.2.refs_2_, bf16[384,512]{1,0:T(8,128)(2,1)} %constant.87.clone.refs_3_, bf16[384,384]{1,0:T(8,128)(2,1)} %constant.88.clone.refs_4_, ...), custom_call_target="tpu_custom_call" | custom-call | flops 36238786560 | bytes 26476544 | tf_op jit(solution)/shard_map/coils/pallas_call | solution.py:424
  436.8 7.4 %all-to-all-done.2 = bf16[16,12,3,8,384]{4,3,2,1,0:T(8,128)(2,1)S(1)} async-done(((bf16[16,12,3,8,384]{4,3,2,1,0:T(8,128)(2,1)}), bf16[16,12,3,8,384]{4,3,2,1,0:T(8,128)(2,1)S(1)}, u32[]{:S(2)}, u32[]{:S(2)}) %all-to-all-start.2) | async-done | bytes 3538976 | tf_op jit(solution)/shard_map/all_to_all | solution.py:477
  444.3 0.0 copy-start.3
  444.3 1.7 copy-done.3
  446.0 4.9 all-to-all-start.3
  450.9 21.4 %coils.4.c_ref = f32[192,8,384]{2,1,0:T(8,128)} custom-call(bf16[192,3,8,384]{3,2,1,0:T(8,128)(2,1)} %bitcast.42, f32[192,16,384]{2,1,0:T(8,128)} %warp.1.refs_1_, f32[384,256]{1,0:T(8,128)} %pad_maximum_fusion.2.refs_2_, bf16[384,512]{1,0:T(8,128)(2,1)} %constant.87.clone.refs_3_, bf16[384,384]{1,0:T(8,128)(2,1)} %constant.88.clone.refs_4_, ...), custom_call_target="tpu_custom_call" | custom-call | flops 10871635968 | bytes 18219008 | tf_op jit(solution)/shard_map/coils/pallas_call | solution.py:424
  472.3 15.6 %spread.2 = bf16[192,8,384]{2,1,0:T(8,128)(2,1)} custom-call(s32[1152]{0:T(1024)} %reshape.30.links, s32[16]{0:T(128)} %fusion.10.owner, f32[192,8,384]{2,1,0:T(8,128)} %coils.4.c_ref, bf16[37120,128]{1,0:T(8,128)(2,1)} %all-gather.2.cloned.1.call-done.w_hbm), custom_call_target="tpu_custom_call" | custom-call | flops 2415919104 | bytes 20971520 | tf_op jit(solution)/shard_map/spread/pallas_call | solution.py:300
  488.0 41.3 %all-to-all-done.3 = bf16[16,12,3,8,384]{4,3,2,1,0:T(8,128)(2,1)S(1)} async-done(((bf16[16,12,3,8,384]{4,3,2,1,0:T(8,128)(2,1)}), bf16[16,12,3,8,384]{4,3,2,1,0:T(8,128)(2,1)S(1)}, u32[]{:S(2)}, u32[]{:S(2)}) %all-to-all-start.3) | async-done | bytes 3538976 | tf_op jit(solution)/shard_map/all_to_all | solution.py:477
  529.3 0.0 copy-start.2
  529.3 1.7 copy-done.2
  531.0 4.9 all-to-all-start.4
  535.9 21.4 %coils.5.c_ref = f32[192,8,384]{2,1,0:T(8,128)} custom-call(bf16[192,3,8,384]{3,2,1,0:T(8,128)(2,1)} %bitcast.41, f32[192,16,384]{2,1,0:T(8,128)} %warp.1.refs_1_, f32[384,256]{1,0:T(8,128)} %pad_maximum_fusion.2.refs_2_, bf16[384,512]{1,0:T(8,128)(2,1)} %constant.87.clone.refs_3_, bf16[384,384]{1,0:T(8,128)(2,1)} %constant.88.clone.refs_4_, ...), custom_call_target="tpu_custom_call" | custom-call | flops 10871635968 | bytes 18219008 | tf_op jit(solution)/shard_map/coils/pallas_call | solution.py:424
  557.3 15.6 %spread.3 = bf16[192,8,384]{2,1,0:T(8,128)(2,1)} custom-call(s32[1152]{0:T(1024)} %reshape.30.links, s32[16]{0:T(128)} %fusion.10.owner, f32[192,8,384]{2,1,0:T(8,128)} %coils.5.c_ref, bf16[37120,128]{1,0:T(8,128)(2,1)} %all-gather.2.cloned.1.call-done.w_hbm), custom_call_target="tpu_custom_call" | custom-call | flops 2415919104 | bytes 20971520 | tf_op jit(solution)/shard_map/spread/pallas_call | solution.py:300
  573.0 0.0 all-to-all-done.4.refs_0_
  573.0 0.0 copy-start.1
  573.0 33.8 %all_to_all.30.refs_1_ = bf16[16,12,8,384]{3,2,1,0:T(8,128)(2,1)} all-to-all(bf16[16,12,8,384]{3,2,1,0:T(8,128)(2,1)} %bitcast.39), channel_id=1, replica_groups=mesh['grp'=2,'slab'=16] {'slab'}, dimensions={0} | all-to-all | bytes 2359296 | tf_op jit(solution)/shard_map/all_to_all | solution.py:477
  606.8 0.0 copy-done.1
  606.8 6.4 %update.1 = f32[2,12,192,256]{3,2,1,0:T(8,128)} custom-call(bf16[16,12,8,384]{3,2,1,0:T(8,128)(2,1)} %copy-done.1, bf16[16,12,8,384]{3,2,1,0:T(8,128)(2,1)} %all_to_all.30.refs_1_, f32[2,12,192,256]{3,2,1,0:T(8,128)} %refs_2_.1, bf16[2,12,192,256]{3,2,1,0:T(8,128)(2,1)} %refs_3_.4), custom_call_target="tpu_custom_call" | custom-call | bytes 14155776 | tf_op jit(solution)/shard_map/update/pallas_call | solution.py:463
  (5 shorter events, 0.1 us)
Async XLA Ops:
  11.2 84.0 %all-to-all-start = ((bf16[16,12,16,384]{3,2,1,0:T(8,128)(2,1)}), bf16[16,12,16,384]{3,2,1,0:T(8,128)(2,1)S(1)}, u32[]{:S(2)}, u32[]{:S(2)}) async-start(bf16[16,12,16,384]{3,2,1,0:T(8,128)(2,1)} %image_columns.1), calls=%async_computation | async-start | bytes 4718592 | tf_op jit(solution)/shard_map/all_to_all | solution.py:477
  20.0 4.8 copy-start.4
  24.9 69.2 %collective-permute-start = (bf16[2320,128]{1,0:T(8,128)(2,1)S(1)}, bf16[2320,128]{1,0:T(8,128)(2,1)S(1)}, u32[]{:S(2)}, u32[]{:S(2)}) collective-permute-start(bf16[2320,128]{1,0:T(8,128)(2,1)S(1)} %pad_maximum_fusion.1), channel_id=1, source_target_pairs={{0,8},{1,9},{2,10},{3,11},{4,12},{5,13},{6,14},{7,15},{8,0},{9,1},... | collective-permute-start | bytes 1781768 | tf_op jit(solution)/shard_map/ppermute | solution.py:487
  95.2 1.4 copy-start
  96.7 265.2 %all-to-all-start.1 = ((bf16[16,12,5,16,384]{4,3,2,1,0:T(8,128)(2,1)}), bf16[16,12,5,16,384]{4,3,2,1,0:T(8,128)(2,1)}, u32[]{:S(2)}, u32[]{:S(2)}) async-start(bf16[16,12,5,16,384]{4,3,2,1,0:T(8,128)(2,1)} %maps_columns.1), calls=%async_computation.1 | async-start | bytes 23592960 | tf_op jit(solution)/shard_map/all_to_all | solution.py:477
  105.3 166.3 %all-gather.2.cloned.1.call-start = ((), (), s32[]{:S(2)}) async-start(), calls=%async_computation.6 | async-start | bytes 10690560 | tf_op jit(solution)/shard_map/all_gather | solution.py:495
  361.9 82.4 %all-to-all-start.2 = ((bf16[16,12,3,8,384]{4,3,2,1,0:T(8,128)(2,1)}), bf16[16,12,3,8,384]{4,3,2,1,0:T(8,128)(2,1)S(1)}, u32[]{:S(2)}, u32[]{:S(2)}) async-start(bf16[16,12,3,8,384]{4,3,2,1,0:T(8,128)(2,1)} %get-tuple-element.14), calls=%async_computation.2 | async-start | bytes 7077888 | tf_op jit(solution)/shard_map/all_to_all | solution.py:477
  444.3 1.8 copy-start.3
  446.0 83.2 %all-to-all-start.3 = ((bf16[16,12,3,8,384]{4,3,2,1,0:T(8,128)(2,1)}), bf16[16,12,3,8,384]{4,3,2,1,0:T(8,128)(2,1)S(1)}, u32[]{:S(2)}, u32[]{:S(2)}) async-start(bf16[16,12,3,8,384]{4,3,2,1,0:T(8,128)(2,1)} %get-tuple-element.16), calls=%async_computation.3 | async-start | bytes 7077888 | tf_op jit(solution)/shard_map/all_to_all | solution.py:477
  529.3 1.8 copy-start.2
  531.0 42.0 %all-to-all-start.4 = ((bf16[16,12,8,384]{3,2,1,0:T(8,128)(2,1)}), bf16[16,12,8,384]{3,2,1,0:T(8,128)(2,1)S(1)}, u32[]{:S(2)}, u32[]{:S(2)}) async-start(bf16[16,12,8,384]{3,2,1,0:T(8,128)(2,1)} %bitcast.38), calls=%async_computation.4 | async-start | bytes 2359296 | tf_op jit(solution)/shard_map/all_to_all | solution.py:477
  573.0 33.8 %copy-start.1 = (bf16[16,12,8,384]{3,2,1,0:T(8,128)(2,1)}, bf16[16,12,8,384]{3,2,1,0:T(8,128)(2,1)S(1)}, u32[]{:S(2)}) copy-start(bf16[16,12,8,384]{3,2,1,0:T(8,128)(2,1)S(1)} %all-to-all-done.4.refs_0_) | copy-start | bytes 3538948
Sparse Core Ops, SparseCore 0:
  107.7 163.7 all-gather.1

commit v7 on v6

--- a/solution.py
+++ b/solution.py
@@ -61,21 +61,25 @@
     return stacked.T
 
 
-def spread_rows(outs, rows, scratch, count, deep):
-    if len(outs) == 1 and deep % 16 == 0:
-        outs[0][...] = rows.reshape(count, deep, LANES)
-        return
-    part = deep // len(outs)
-    scratch[...] = rows.astype(F32)
-    for h, out in enumerate(outs):
-        for d in range(count):
-            out[d] = scratch[pl.ds(d * deep + h * part, part), :].astype(BF)
+def part_rows(scratch, count, deep, parts, d, h):
+    part = deep // parts
+    return scratch[pl.ds((h * count + d) * part, part), :]
+
+
+def spread_rows(out, scratch, count, deep, parts):
+    for d in range(count):
+        rows = [part_rows(scratch, count, deep, parts, d, h) for h in range(parts)]
+        out[d] = jnp.concatenate(rows, axis=0).astype(BF)
+
+
+def parts_of(deep):
+    return 2 if deep % 16 == 0 else 1
 
 
 def image_kernel(count, deep, x_ref, o_ref, scratch):
     for x in range(x_ref.shape[1]):
-        rows = to_rows(x_ref[:, x].astype(BF))
-        spread_rows([o_ref.at[:, x]], rows, scratch, count, deep)
+        scratch[x] = to_rows(x_ref[:, x].astype(BF)).astype(F32)
+        spread_rows(o_ref.at[:, x], scratch.at[x], count, deep, parts_of(deep))
 
 
 def image_columns(image, count):
@@ -88,7 +92,7 @@
         grid=(planes // group,),
         in_specs=[pl.BlockSpec((2, group, ny, nz), lambda x: (0, x, 0, 0))],
         out_specs=pl.BlockSpec((count, group, deep, LANES), lambda x: (0, x, 0, 0)),
-        scratch_shapes=[pltpu.VMEM((nz, LANES), F32)],
+        scratch_shapes=[pltpu.VMEM((group, nz, LANES), F32)],
         compiler_params=params(),
         cost_estimate=pl.CostEstimate(flops=0, bytes_accessed=image.size * 6, transcendentals=0),
         name="image_columns",
@@ -96,12 +100,23 @@
 
 
 def maps_kernel(count, deep, x_ref, o_ref, scratch):
-    spread_rows([o_ref.at[:, 0, 0]], to_rows(x_ref[0, :, 0]), scratch, count, deep)
-
-
-def last_maps_kernel(count, deep, x_ref, first_ref, second_ref, scratch):
-    outs = [first_ref.at[:, 0, 0], second_ref.at[:, 0, 0]]
-    spread_rows(outs, to_rows(x_ref[0, :, 0]), scratch, count, deep)
+    scratch[...] = to_rows(x_ref[0, :, 0]).astype(F32)
+    spread_rows(o_ref.at[:, 0, 0], scratch, count, deep, parts_of(deep))
+
+
+def last_maps_kernel(count, deep, coils, x_ref, first_ref, second_ref, scratch):
+    scratch[...] = to_rows(x_ref[0, :, 0]).astype(F32)
+    for c in range(coils):
+
+        @pl.when(pl.program_id(1) == c)
+        def _():
+            for d in range(count):
+                half = part_rows(scratch, count, deep, 2, d, 1).astype(BF)
+                first_ref[d, 0, c] = part_rows(scratch, count, deep, 2, d, 0).astype(BF)
+                if c == 0:
+                    first_ref[d, 0, coils] = half
+                else:
+                    second_ref[d, 0, c - 1] = half
 
 
 def maps_columns(coil_maps, count, first, coils):
@@ -125,13 +140,16 @@
 def last_maps_columns(coil_maps, count, first, coils):
     _, _, planes, ny, nz = coil_maps.shape
     deep = nz // count
-    part = deep // 2
-    return pl.pallas_call(
-        functools.partial(last_maps_kernel, count, deep),
-        out_shape=[jax.ShapeDtypeStruct((count, planes, coils, part, LANES), BF)] * 2,
+    sizes = (coils + 1, coils - 1)
+    return pl.pallas_call(
+        functools.partial(last_maps_kernel, count, deep, coils),
+        out_shape=[jax.ShapeDtypeStruct((count, planes, n, deep // 2, LANES), BF) for n in sizes],
         grid=(planes, coils),
         in_specs=[pl.BlockSpec((1, 2, 1, ny, nz), lambda x, c: (first + c, 0, x, 0, 0))],
-        out_specs=[pl.BlockSpec((count, 1, 1, part, LANES), lambda x, c: (0, x, c, 0, 0))] * 2,
+        out_specs=[
+            pl.BlockSpec((count, 1, n, deep // 2, LANES), lambda x, c: (0, x, 0, 0, 0))
+            for n in sizes
+        ],
         scratch_shapes=[pltpu.VMEM((nz, LANES), F32)],
         compiler_params=params(),
         cost_estimate=pl.CostEstimate(
@@ -404,14 +422,14 @@
     lax.fori_loop(0, nx // group, combine, 0, unroll=4)
 
 
-def coils(maps, warped, mask, tabs, before, part):
-    nx, count, deep, _ = maps.shape
+def coils(maps, first, count, warped, mask, tabs, before, part):
+    nx, _, deep, _ = maps.shape
     pad = max(8, deep)
     fresh = before is None
     whole = lambda shape: pl.BlockSpec(
         shape, lambda c: (0,) * len(shape), pipeline_mode=pl.Buffered(1)
     )
-    in_specs = [pl.BlockSpec((nx, 1, deep, LANES), lambda c: (0, c, 0, 0))]
+    in_specs = [pl.BlockSpec((nx, 1, deep, LANES), lambda c: (0, first + c, 0, 0))]
     args = [maps, warped, mask, *tabs] + ([] if fresh else [before])
     def columns(array):
         at = part if array.shape[1] > deep else 0
@@ -438,14 +456,12 @@
     )(*args)
 
 
-def update_kernel(count, parts, *refs):
-    backs = refs[:parts]
-    i_ref, a_ref, o_ref, scratch = refs[parts:]
-    part = backs[0].shape[2]
+def update_kernel(count, b_ref, i_ref, a_ref, *refs):
+    o_ref, scratch = refs[-2:]
+    part = b_ref.shape[2]
     for x in range(o_ref.shape[1]):
-        for h, back in enumerate(backs):
-            for d in range(count):
-                scratch[x, pl.ds((d * parts + h) * part, part), :] = back[d, x].astype(F32)
+        for d in range(count):
+            scratch[x, pl.ds(d * part, part), :] = b_ref[d, x].astype(F32)
         grad = scratch[x].astype(BF).T.astype(F32)
         real = jnp.concatenate([grad[0:128], grad[256:320]], axis=0)
         imag = jnp.concatenate([grad[128:256], grad[320:384]], axis=0)
@@ -453,24 +469,32 @@
             o_ref[p, x] = i_ref[p, x] - 0.5 * (value - a_ref[p, x].astype(F32))
 
 
-def update(backs, image, adjoint):
-    parts = len(backs)
-    count, planes, part, _ = backs[0].shape
-    _, _, ny, nz = image.shape
+def update(back, image, adjoint, part, before):
+    count, planes, deep, _ = back.shape
+    _, _, ny, _ = image.shape
+    lanes = count * deep
     group = 3 if planes % 3 == 0 else 1
-    block = pl.BlockSpec((2, group, ny, nz), lambda x: (0, x, 0, 0))
-    back = pl.BlockSpec((count, group, part, LANES), lambda x: (0, x, 0, 0))
-    return pl.pallas_call(
-        functools.partial(update_kernel, count, parts),
+    block = pl.BlockSpec((2, group, ny, lanes), lambda x: (0, x, 0, part))
+    more = [] if before is None else [before]
+    return pl.pallas_call(
+        functools.partial(update_kernel, count),
         out_shape=jax.ShapeDtypeStruct(image.shape, F32),
         grid=(planes // group,),
-        in_specs=[back] * parts + [block, block],
+        in_specs=[
+            pl.BlockSpec((count, group, deep, LANES), lambda x: (0, x, 0, 0)),
+            block,
+            block,
+        ]
+        + [pl.BlockSpec(memory_space=pl.ANY)] * len(more),
         out_specs=block,
-        scratch_shapes=[pltpu.VMEM((group, nz, LANES), F32)],
-        compiler_params=params(),
-        cost_estimate=pl.CostEstimate(flops=0, bytes_accessed=image.size * 12, transcendentals=0),
+        scratch_shapes=[pltpu.VMEM((group, lanes, LANES), F32)],
+        input_output_aliases={3: 0} if more else {},
+        compiler_params=params(),
+        cost_estimate=pl.CostEstimate(
+            flops=0, bytes_accessed=2 * planes * ny * lanes * 12, transcendentals=0
+        ),
         name="update",
-    )(*backs, image, adjoint)
+    )(back, image, adjoint, *more)
 
 
 def exchange(parts):
@@ -520,9 +544,9 @@
     digits = digits[:, :4, :targets].astype(jnp.int32)
     links = (digits[:, :2] * BLK + digits[:, 2:]).reshape(-1)
 
-    def run(received, before, part):
-        size = received.shape[2]
-        return coils(received.reshape(nx, size, -1, LANES), warped, mask, tabs, before, part)
+    def run(received, first, size, before, part):
+        maps = received.reshape(nx, received.shape[2], -1, LANES)
+        return coils(maps, first, size, warped, mask, tabs, before, part)
 
     def back(combined, *needs):
         grad = spread(combined, packed, links, owner)
@@ -530,7 +554,7 @@
 
     columns = exchange(image_columns(image, count))
     warped = warp(columns.reshape(nx, deep, LANES), packed, links, owner)
-    halves = deep % 16 == 0
+    halves = parts_of(deep) == 2
     early = total - 3 * total // 8 if halves else total - 1
     late = total - early
     maps = maps_columns(coil_maps, count, 0, early)
@@ -538,16 +562,20 @@
     if not halves:
         maps = maps_columns(coil_maps, count, early, late)
         last = exchange(after(maps, arrived, warped))
-        combined = run(last, run(arrived, None, 0), 0)
-        return update([back(combined)], image, adjoint_data)
+        combined = run(last, 0, late, run(arrived, 0, early, None, 0), 0)
+        return update(back(combined), image, adjoint_data, 0, None)
 
     first, second = last_maps_columns(coil_maps, count, early, late)
     first = exchange(after(first, arrived, warped))
-    combined = run(arrived, None, 0)
+    combined = run(arrived, 0, early, None, 0)
     second = exchange(after(second, first, combined))
-    back_first = back(run(first, combined, 0), second)
-    back_second = back(run(second, combined, 1), back_first)
-    return update([back_first, back_second], image, adjoint_data)
+    half_first = run(first, 0, late, combined, 0)
+    half_second = run(first, late, 1, combined, 1)
+    back_first = back(half_first, second, half_second)
+    half_second = run(second, 0, late - 1, half_second, 1)
+    back_second = back(half_second, back_first)
+    result = update(back_first, image, adjoint_data, 0, None)
+    return update(back_second, image, adjoint_data, 1, result)
 
 
 def solution(mesh):

time: 625 us -> 613 us (0.981)
  blocking collectives: 33.8 us -> 0 us
  waiting for transfers between devices: 296 us -> 308 us
  Pallas kernels: 228 us -> 237 us
  starting transfers between devices: 31.2 us -> 37.8 us
    all_to_all x1 -> x0, blocking collectives: 33.8 us -> none  [exchange(): lax.all_to_all(parts, 'slab', split_axis=0, concat_axis=0, tiled=True)]
    all_to_all x5 -> x6, waiting for transfers between devices: 123 us -> 136 us  [exchange(): lax.all_to_all(parts, 'slab', split_axis=0, concat_axis=0, tiled=True)]
    all_to_all x5 -> x6, starting transfers between devices: 29.1 us -> 35.6 us  [exchange(): lax.all_to_all(parts, 'slab', split_axis=0, concat_axis=0, tiled=True)]
    pallas_call x3 -> x4, Pallas kernels: 112 us -> 117 us  [coils(): pl.pallas_call(functools.partial(coil_kernel, nx, deep, pad, fresh), out_...]
    pallas_call x2 -> x3, Pallas kernels: 28.9 us -> 33 us  [the longest x1 24 us: last_maps_columns(): pl.pallas_call(functools.partial(last_maps_kernel, count, deep, coils), o...]
  transfers between devices with their start and end apart: 7 -> 8, of which waited for: 5 -> 6; matrix products, arithmetic and copies ran while one was open for 2% -> 2% of each run, Pallas kernels for 35% -> 37%
where the time goes in v7:
time: 613 us; the launch traced here: 610 us
  waiting for transfers between devices  308 us (50%)
  Pallas kernels  237 us (39%)
  starting transfers between devices  37.8 us (6%)
  between operations  13.6 us (2%)
  local copies, waits for them, and re-layouts  10.2 us (2%)
    all_gather x1, waiting for transfers between devices, gather_half(): lax.all_gather(pair, 'slab', axis=0, tiled=True, axis_index_groups=groups)  141 us
    all_to_all x6, waiting for transfers between devices, exchange(): lax.all_to_all(parts, 'slab', split_axis=0, concat_axis=0, tiled=True)  136 us
    pallas_call x4, Pallas kernels, coils(): pl.pallas_call(functools.partial(coil_kernel, nx, deep, pad, fresh), out_...  117 us
    pallas_call x1, Pallas kernels, maps_columns(): pl.pallas_call(functools.partial(maps_kernel, count, deep), out_shape=jax...  36.4 us
    all_to_all x6, starting transfers between devices, exchange(): lax.all_to_all(parts, 'slab', split_axis=0, concat_axis=0, tiled=True)  35.6 us
    pallas_call x2, Pallas kernels, spread(): pl.pallas_call(functools.partial(spread_kernel, nx, deep, pad), out_shape...  31.3 us
    ppermute x1, waiting for transfers between devices, swap_halves(): other = lax.ppermute(value, 'slab', [(i, i ^ half) for i in range(count)])  30.6 us
    pallas_call x1, Pallas kernels, last_maps_columns(): pl.pallas_call(functools.partial(last_maps_kernel, count, deep, coils), o...  24 us
  transfers between devices with their start and end apart: 8, of which 6 were waited for; matrix products, arithmetic and copies ran while one was open for 2% of the time, Pallas kernels for 37%

profile of v7, /device:TPU:13, one launch (start us, length us, event | category | flops | bytes accessed | tf_op | source)
XLA Modules:
  0.0 610.3 jit_solution(10830288254699466503)
XLA Ops:
  6.5 4.7 image_columns.1
  11.2 6.6 %all-to-all-start = ((bf16[16,12,16,384]{3,2,1,0:T(8,128)(2,1)}), bf16[16,12,16,384]{3,2,1,0:T(8,128)(2,1)S(1)}, u32[]{:S(2)}, u32[]{:S(2)}) async-start(bf16[16,12,16,384]{3,2,1,0:T(8,128)(2,1)} %image_columns.1), calls=%async_computation | async-start | bytes 4718592 | tf_op jit(solution)/shard_map/all_to_all | solution.py:501
  17.8 2.2 reshape_squeeze.3
  20.0 0.0 copy-start.5
  20.0 2.2 copy.14
  22.2 2.6 reshape.29
  24.8 0.0 copy-done.5
  24.9 2.2 collective-permute-start
  27.0 36.4 %maps_columns.1 = bf16[16,12,5,16,384]{4,3,2,1,0:T(8,128)(2,1)} custom-call(bf16[8,2,12,192,256]{4,3,2,1,0:T(8,128)(2,1)} %x_ref.4), custom_call_target="tpu_custom_call" | custom-call | bytes 23592960 | tf_op jit(solution)/shard_map/maps_columns/pallas_call | solution.py:125
  63.4 30.6 %collective-permute-done = bf16[2320,128]{1,0:T(8,128)(2,1)S(1)} collective-permute-done((bf16[2320,128]{1,0:T(8,128)(2,1)S(1)}, bf16[2320,128]{1,0:T(8,128)(2,1)S(1)}, u32[]{:S(2)}, u32[]{:S(2)}) %collective-permute-start) | collective-permute-done | bytes 593952 | tf_op jit(solution)/shard_map/ppermute | solution.py:511
  94.1 1.1 pad_maximum_fusion
  95.2 0.0 all-to-all-done
  95.2 0.0 copy-start
  95.2 1.4 copy-done
  96.6 8.6 %all-to-all-start.1 = ((bf16[16,12,5,16,384]{4,3,2,1,0:T(8,128)(2,1)}), bf16[16,12,5,16,384]{4,3,2,1,0:T(8,128)(2,1)}, u32[]{:S(2)}, u32[]{:S(2)}) async-start(bf16[16,12,5,16,384]{4,3,2,1,0:T(8,128)(2,1)} %maps_columns.1), calls=%async_computation.1 | async-start | bytes 23592960 | tf_op jit(solution)/shard_map/all_to_all | solution.py:501
  105.2 0.0 all-gather.2.cloned.1.call-start
  105.2 0.7 all-gather.2.cloned.1.call-update
  105.9 24.0 %last_maps_columns.1 = (bf16[16,12,4,8,384]{4,3,2,1,0:T(8,128)(2,1)}, bf16[16,12,2,8,384]{4,3,2,1,0:T(8,128)(2,1)}) custom-call(bf16[8,2,12,192,256]{4,3,2,1,0:T(8,128)(2,1)} %x_ref.4), custom_call_target="tpu_custom_call" | custom-call | bytes 14155776 | tf_op jit(solution)/shard_map/last_maps_columns/pallas_call | solution.py:144
  130.0 0.6 fusion.10.owner
  130.6 140.9 %all-gather.2.cloned.1.call-done.w_hbm = bf16[37120,128]{1,0:T(8,128)(2,1)} async-done(((bf16[4640,128]{1,0:T(8,128)(2,1)}), bf16[37120,128]{1,0:T(8,128)(2,1)}) %all-gather.2.cloned.1.call-update) | async-done | bytes 9502736 | tf_op jit(solution)/shard_map/all_gather | solution.py:519
  271.4 0.8 slice_convert_fusion
  272.2 0.7 reshape.31.links
  272.9 15.1 %warp.1.refs_1_ = f32[192,16,384]{2,1,0:T(8,128)} custom-call(s32[1152]{0:T(1024)} %reshape.31.links, s32[16]{0:T(128)} %fusion.10.owner, bf16[192,16,384]{2,1,0:T(8,128)(2,1)} %bitcast.37, bf16[37120,128]{1,0:T(8,128)(2,1)} %all-gather.2.cloned.1.call-done.w_hbm), custom_call_target="tpu_custom_call" | custom-call | flops 2415919104 | bytes 20971520 | tf_op jit(solution)/shard_map/warp/pallas_call | solution.py:233
  288.0 73.8 %all-to-all-done.1 = bf16[16,12,5,16,384]{4,3,2,1,0:T(8,128)(2,1)} async-done(((bf16[16,12,5,16,384]{4,3,2,1,0:T(8,128)(2,1)}), bf16[16,12,5,16,384]{4,3,2,1,0:T(8,128)(2,1)}, u32[]{:S(2)}, u32[]{:S(2)}) %all-to-all-start.1) | async-done | bytes 11796512 | tf_op jit(solution)/shard_map/all_to_all | solution.py:501
  361.8 0.0 copy-start.4
  361.8 4.6 all-to-all-start.2
  366.4 0.0 copy-done.4
  366.5 0.8 pad_maximum_fusion.2.refs_2_
  367.2 69.2 %coils.4.refs_7_ = f32[192,16,384]{2,1,0:T(8,128)} custom-call(bf16[192,5,16,384]{3,2,1,0:T(8,128)(2,1)} %bitcast.6.refs_0_, f32[192,16,384]{2,1,0:T(8,128)} %warp.1.refs_1_, f32[384,256]{1,0:T(8,128)} %pad_maximum_fusion.2.refs_2_, bf16[384,512]{1,0:T(8,128)(2,1)} %constant.87.clone.refs_3_, bf16[384,384]{1,0:T(8,128)(2,1)} %constant.88.clone.refs_4_, ...), custom_call_target="tpu_custom_call" | custom-call | flops 36238786560 | bytes 26476544 | tf_op jit(solution)/shard_map/coils/pallas_call | solution.py:442
  436.4 33.3 %all-to-all-done.2 = bf16[16,12,4,8,384]{4,3,2,1,0:T(8,128)(2,1)} async-done(((bf16[16,12,4,8,384]{4,3,2,1,0:T(8,128)(2,1)}), bf16[16,12,4,8,384]{4,3,2,1,0:T(8,128)(2,1)}, u32[]{:S(2)}, u32[]{:S(2)}) %all-to-all-start.2) | async-done | bytes 4718624 | tf_op jit(solution)/shard_map/all_to_all | solution.py:501
  469.7 4.9 all-to-all-start.3
  474.6 21.3 %coils.7.c_ref = f32[192,8,384]{2,1,0:T(8,128)} custom-call(bf16[192,4,8,384]{3,2,1,0:T(8,128)(2,1)} %bitcast.9.refs_0_, f32[192,16,384]{2,1,0:T(8,128)} %warp.1.refs_1_, f32[384,256]{1,0:T(8,128)} %pad_maximum_fusion.2.refs_2_, bf16[384,512]{1,0:T(8,128)(2,1)} %constant.87.clone.refs_3_, bf16[384,384]{1,0:T(8,128)(2,1)} %constant.88.clone.refs_4_, ...), custom_call_target="tpu_custom_call" | custom-call | flops 10871635968 | bytes 18219008 | tf_op jit(solution)/shard_map/coils/pallas_call | solution.py:442
  495.9 15.7 %spread.3 = bf16[192,8,384]{2,1,0:T(8,128)(2,1)} custom-call(s32[1152]{0:T(1024)} %reshape.31.links, s32[16]{0:T(128)} %fusion.10.owner, f32[192,8,384]{2,1,0:T(8,128)} %coils.7.c_ref, bf16[37120,128]{1,0:T(8,128)(2,1)} %all-gather.2.cloned.1.call-done.w_hbm), custom_call_target="tpu_custom_call" | custom-call | flops 2415919104 | bytes 20971520 | tf_op jit(solution)/shard_map/spread/pallas_call | solution.py:318
  511.6 10.2 %coils.5.refs_7_ = f32[192,8,384]{2,1,0:T(8,128)} custom-call(bf16[192,4,8,384]{3,2,1,0:T(8,128)(2,1)} %bitcast.9.refs_0_, f32[192,16,384]{2,1,0:T(8,128)} %warp.1.refs_1_, f32[384,256]{1,0:T(8,128)} %pad_maximum_fusion.2.refs_2_, bf16[384,512]{1,0:T(8,128)(2,1)} %constant.87.clone.refs_3_, bf16[384,384]{1,0:T(8,128)(2,1)} %constant.88.clone.refs_4_, ...), custom_call_target="tpu_custom_call" | custom-call | flops 3623878656 | bytes 15859712 | tf_op jit(solution)/shard_map/coils/pallas_call | solution.py:442
  521.8 5.8 all-to-all-done.3
  527.7 0.0 copy-start.3
  527.7 4.9 all-to-all-start.4
  532.6 0.0 copy-done.3
  532.6 15.8 %coils.6.c_ref = f32[192,8,384]{2,1,0:T(8,128)} custom-call(bf16[192,2,8,384]{3,2,1,0:T(8,128)(2,1)} %bitcast.40, f32[192,16,384]{2,1,0:T(8,128)} %warp.1.refs_1_, f32[384,256]{1,0:T(8,128)} %pad_maximum_fusion.2.refs_2_, bf16[384,512]{1,0:T(8,128)(2,1)} %constant.87.clone.refs_3_, bf16[384,384]{1,0:T(8,128)(2,1)} %constant.88.clone.refs_4_, ...), custom_call_target="tpu_custom_call" | custom-call | flops 7247757312 | bytes 17039360 | tf_op jit(solution)/shard_map/coils/pallas_call | solution.py:442
  548.4 15.7 %spread.2 = bf16[192,8,384]{2,1,0:T(8,128)(2,1)} custom-call(s32[1152]{0:T(1024)} %reshape.31.links, s32[16]{0:T(128)} %fusion.10.owner, f32[192,8,384]{2,1,0:T(8,128)} %coils.6.c_ref, bf16[37120,128]{1,0:T(8,128)(2,1)} %all-gather.2.cloned.1.call-done.w_hbm), custom_call_target="tpu_custom_call" | custom-call | flops 2415919104 | bytes 20971520 | tf_op jit(solution)/shard_map/spread/pallas_call | solution.py:318
  564.1 0.0 all-to-all-done.4.b_ref
  564.1 0.0 copy-start.1
  564.1 6.0 all-to-all-start.5
  570.1 0.0 copy-done.1
  570.1 4.5 update.2.refs_0_
  574.6 23.2 %all-to-all-done.5.b_ref = bf16[16,12,8,384]{3,2,1,0:T(8,128)(2,1)S(1)} async-done(((bf16[16,12,8,384]{3,2,1,0:T(8,128)(2,1)}), bf16[16,12,8,384]{3,2,1,0:T(8,128)(2,1)S(1)}, u32[]{:S(2)}, u32[]{:S(2)}) %all-to-all-start.5) | async-done | bytes 1179680 | tf_op jit(solution)/shard_map/all_to_all | solution.py:501
  597.9 1.0 copy-done.2
  598.9 4.5 update.3
  (7 shorter events, 0.1 us)
Async XLA Ops:
  11.2 84.0 %all-to-all-start = ((bf16[16,12,16,384]{3,2,1,0:T(8,128)(2,1)}), bf16[16,12,16,384]{3,2,1,0:T(8,128)(2,1)S(1)}, u32[]{:S(2)}, u32[]{:S(2)}) async-start(bf16[16,12,16,384]{3,2,1,0:T(8,128)(2,1)} %image_columns.1), calls=%async_computation | async-start | bytes 4718592 | tf_op jit(solution)/shard_map/all_to_all | solution.py:501
  20.0 4.8 copy-start.5
  24.9 69.2 %collective-permute-start = (bf16[2320,128]{1,0:T(8,128)(2,1)S(1)}, bf16[2320,128]{1,0:T(8,128)(2,1)S(1)}, u32[]{:S(2)}, u32[]{:S(2)}) collective-permute-start(bf16[2320,128]{1,0:T(8,128)(2,1)S(1)} %pad_maximum_fusion.1), channel_id=1, source_target_pairs={{0,8},{1,9},{2,10},{3,11},{4,12},{5,13},{6,14},{7,15},{8,0},{9,1},... | collective-permute-start | bytes 1781768 | tf_op jit(solution)/shard_map/ppermute | solution.py:511
  95.2 1.4 copy-start
  96.6 265.2 %all-to-all-start.1 = ((bf16[16,12,5,16,384]{4,3,2,1,0:T(8,128)(2,1)}), bf16[16,12,5,16,384]{4,3,2,1,0:T(8,128)(2,1)}, u32[]{:S(2)}, u32[]{:S(2)}) async-start(bf16[16,12,5,16,384]{4,3,2,1,0:T(8,128)(2,1)} %maps_columns.1), calls=%async_computation.1 | async-start | bytes 23592960 | tf_op jit(solution)/shard_map/all_to_all | solution.py:501
  105.2 166.3 %all-gather.2.cloned.1.call-start = ((), (), s32[]{:S(2)}) async-start(), calls=%async_computation.6 | async-start | bytes 10690560 | tf_op jit(solution)/shard_map/all_gather | solution.py:519
  361.8 4.6 copy-start.4
  361.8 107.9 %all-to-all-start.2 = ((bf16[16,12,4,8,384]{4,3,2,1,0:T(8,128)(2,1)}), bf16[16,12,4,8,384]{4,3,2,1,0:T(8,128)(2,1)}, u32[]{:S(2)}, u32[]{:S(2)}) async-start(bf16[16,12,4,8,384]{4,3,2,1,0:T(8,128)(2,1)} %get-tuple-element.15), calls=%async_computation.2 | async-start | bytes 9437184 | tf_op jit(solution)/shard_map/all_to_all | solution.py:501
  469.7 57.9 %all-to-all-start.3 = ((bf16[16,12,2,8,384]{4,3,2,1,0:T(8,128)(2,1)}), bf16[16,12,2,8,384]{4,3,2,1,0:T(8,128)(2,1)S(1)}, u32[]{:S(2)}, u32[]{:S(2)}) async-start(bf16[16,12,2,8,384]{4,3,2,1,0:T(8,128)(2,1)} %get-tuple-element.16), calls=%async_computation.3 | async-start | bytes 4718592 | tf_op jit(solution)/shard_map/all_to_all | solution.py:501
  527.7 4.9 copy-start.3
  527.7 36.4 %all-to-all-start.4 = ((bf16[16,12,8,384]{3,2,1,0:T(8,128)(2,1)}), bf16[16,12,8,384]{3,2,1,0:T(8,128)(2,1)S(1)}, u32[]{:S(2)}, u32[]{:S(2)}) async-start(bf16[16,12,8,384]{3,2,1,0:T(8,128)(2,1)} %bitcast.10), calls=%async_computation.4 | async-start | bytes 2359296 | tf_op jit(solution)/shard_map/all_to_all | solution.py:501
  564.1 6.0 copy-start.1
  564.1 33.8 %all-to-all-start.5 = ((bf16[16,12,8,384]{3,2,1,0:T(8,128)(2,1)}), bf16[16,12,8,384]{3,2,1,0:T(8,128)(2,1)S(1)}, u32[]{:S(2)}, u32[]{:S(2)}) async-start(bf16[16,12,8,384]{3,2,1,0:T(8,128)(2,1)} %bitcast.38), calls=%async_computation.5 | async-start | bytes 2359296 | tf_op jit(solution)/shard_map/all_to_all | solution.py:501
  597.9 1.0 copy-start.2
Sparse Core Ops, SparseCore 0:
  107.7 163.7 all-gather.1

commit v8 on v7

--- a/solution.py
+++ b/solution.py
@@ -13,7 +13,7 @@
 LANES = 384
 TAIL = 16
 HALF = 256
-VMEM_LIMIT = 56 * 1024 * 1024
+VMEM_LIMIT = 48 * 1024 * 1024
 BF = jnp.bfloat16
 F32 = jnp.float32
 
@@ -52,6 +52,10 @@
 
 def params():
     return pltpu.CompilerParams(vmem_limit_bytes=VMEM_LIMIT)
+
+
+def in_vmem(array):
+    return pltpu.with_memory_space_constraint(array, pltpu.VMEM)
 
 
 def to_rows(parts):
@@ -236,7 +240,7 @@
         grid_spec=pltpu.PrefetchScalarGridSpec(
             num_scalar_prefetch=2,
             grid=(1,),
-            in_specs=[whole, pl.BlockSpec(memory_space=pl.ANY)],
+            in_specs=[pl.BlockSpec(memory_space=pltpu.VMEM), pl.BlockSpec(memory_space=pl.ANY)],
             out_specs=whole,
             scratch_shapes=[
                 pltpu.VMEM((blocks * BLK, 2 * BLK), BF),
@@ -249,11 +253,10 @@
             flops=2 * blocks * 256 * 256 * 32, bytes_accessed=20 << 20, transcendentals=0
         ),
         name="warp",
-    )(links, owner, columns, weights)
-
-
-def spread_kernel(nx, deep, pad, links, owner, c_ref, w_hbm, o_ref, held, total, sems):
-    fetch_all(w_hbm, held, sems)
+    )(links, owner, in_vmem(columns), weights)
+
+
+def spread(nx, deep, pad, links, owner, c_ref, w_hbm, o_ref, held, total, sems):
     count = sems.shape[0]
     planes = nx // count
 
@@ -310,38 +313,21 @@
     lax.fori_loop(0, nx, gather, 0, unroll=8)
 
 
-def spread(combined, weights, links, owner):
-    nx, deep, _ = combined.shape
-    blocks = 3 * nx
-    pad = max(8, deep)
-    whole = pl.BlockSpec((nx, deep, LANES), lambda i, l, p: (0, 0, 0))
-    return pl.pallas_call(
-        functools.partial(spread_kernel, nx, deep, pad),
-        out_shape=jax.ShapeDtypeStruct((nx, deep, LANES), BF),
-        grid_spec=pltpu.PrefetchScalarGridSpec(
-            num_scalar_prefetch=2,
-            grid=(1,),
-            in_specs=[whole, pl.BlockSpec(memory_space=pl.ANY)],
-            out_specs=whole,
-            scratch_shapes=[
-                pltpu.VMEM((blocks * BLK, 2 * BLK), BF),
-                pltpu.VMEM((blocks, 2 * pad, 128), F32),
-                pltpu.SemaphoreType.DMA((owner.shape[0],)),
-            ],
-        ),
-        compiler_params=params(),
-        cost_estimate=pl.CostEstimate(
-            flops=2 * blocks * 256 * 256 * 32, bytes_accessed=20 << 20, transcendentals=0
-        ),
-        name="spread",
-    )(links, owner, combined, weights)
-
-
-def coil_kernel(nx, deep, pad, fresh, *refs):
-    if fresh:
-        s_ref, w_ref, mask, iy, fx, bx, oy, o_ref, rows = refs
+def coil_kernel(nx, deep, pad, fresh, ends, landed, *refs):
+    if ends:
+        links, owner, *refs = refs
+    s_ref, w_ref, mask, iy, fx, bx, oy, *refs = refs
+    if not fresh:
+        before, *refs = refs
+    if ends:
+        w_hbm, grad_ref, rows, o_ref, held, total, sems = refs
+
+        @pl.when(pl.program_id(0) == 0)
+        def _():
+            fetch_all(w_hbm, held, sems)
     else:
-        s_ref, w_ref, mask, iy, fx, bx, oy, before, o_ref, rows = refs
+        o_ref, rows = refs
+    s_ref = s_ref.at[:, pl.program_id(0) if landed else 0]
     group = 8 if nx % 8 == 0 else 1
     cube = rows.reshape(3, nx, pad, 128)
     low = low_half((group, deep, 128))
@@ -351,7 +337,7 @@
 
     def expand(i, carry):
         at = pl.ds(i * group, group)
-        s0, s1, s2 = thirds(s_ref.at[:, 0], at)
+        s0, s1, s2 = thirds(s_ref, at)
         w0, w1, w2 = thirds(w_ref, at)
         turned = pltpu.roll(s2, BLK, 2)
         other = pltpu.roll(w2, BLK, 2)
@@ -401,7 +387,7 @@
 
     def combine(i, carry):
         at = pl.ds(i * group, group)
-        s0, s1, s2 = thirds(s_ref.at[:, 0], at)
+        s0, s1, s2 = thirds(s_ref, at)
         r0, r1, r2 = (cube[v, at, pl.ds(0, deep), :] for v in range(3))
         turned = pltpu.roll(s2, BLK, 2)
         other = pltpu.roll(r2, BLK, 2)
@@ -420,32 +406,59 @@
         return carry
 
     lax.fori_loop(0, nx // group, combine, 0, unroll=4)
-
-
-def coils(maps, first, count, warped, mask, tabs, before, part):
+    if ends:
+
+        @pl.when(pl.program_id(0) == pl.num_programs(0) - 1)
+        def _():
+            spread(nx, deep, pad, links, owner, o_ref, w_hbm, grad_ref, held, total, sems)
+
+
+def coils(maps, first, count, warped, mask, tabs, before, part, warping=None, landed=False):
     nx, _, deep, _ = maps.shape
     pad = max(8, deep)
-    fresh = before is None
-    whole = lambda shape: pl.BlockSpec(
-        shape, lambda c: (0,) * len(shape), pipeline_mode=pl.Buffered(1)
-    )
-    in_specs = [pl.BlockSpec((nx, 1, deep, LANES), lambda c: (0, first + c, 0, 0))]
-    args = [maps, warped, mask, *tabs] + ([] if fresh else [before])
+    fresh, ends = before is None, warping is not None
+
+    def whole(shape):
+        return pl.BlockSpec(shape, lambda c, *_: (0,) * len(shape), pipeline_mode=pl.Buffered(1))
+
     def columns(array):
         at = part if array.shape[1] > deep else 0
         return pl.BlockSpec(
-            (nx, deep, LANES), lambda c: (0, at, 0), pipeline_mode=pl.Buffered(1)
+            (nx, deep, LANES), lambda c, *_: (0, at, 0), pipeline_mode=pl.Buffered(1)
         )
 
+    if landed:
+        maps = in_vmem(maps)
+        in_specs = [pl.BlockSpec(memory_space=pltpu.VMEM)]
+    else:
+        in_specs = [pl.BlockSpec((nx, 1, deep, LANES), lambda c, *_: (0, first + c, 0, 0))]
+    args = [maps, warped, mask, *tabs]
     in_specs += [columns(warped)] + [whole(a.shape) for a in (mask, *tabs)]
-    in_specs += [] if fresh else [columns(before)]
+    if not fresh:
+        args += [before]
+        in_specs += [columns(before)]
+    scratch = [pltpu.VMEM((3, nx * pad, 128), F32)]
+    prefetched = []
+    if ends:
+        weights, *prefetched = warping
+        args += [weights]
+        in_specs += [pl.BlockSpec(memory_space=pl.ANY)]
+        scratch += [
+            pltpu.VMEM((nx, deep, LANES), F32),
+            pltpu.VMEM((3 * nx * BLK, 2 * BLK), BF),
+            pltpu.VMEM((3 * nx, 2 * pad, 128), F32),
+            pltpu.SemaphoreType.DMA((prefetched[1].shape[0],)),
+        ]
     return pl.pallas_call(
-        functools.partial(coil_kernel, nx, deep, pad, fresh),
-        out_shape=jax.ShapeDtypeStruct((nx, deep, LANES), F32),
-        grid=(count,),
-        in_specs=in_specs,
-        out_specs=pl.BlockSpec((nx, deep, LANES), lambda c: (0, 0, 0)),
-        scratch_shapes=[pltpu.VMEM((3, nx * pad, 128), F32)],
+        functools.partial(coil_kernel, nx, deep, pad, fresh, ends, landed),
+        out_shape=jax.ShapeDtypeStruct((nx, deep, LANES), BF if ends else F32),
+        grid_spec=pltpu.PrefetchScalarGridSpec(
+            num_scalar_prefetch=len(prefetched),
+            grid=(count,),
+            in_specs=in_specs,
+            out_specs=pl.BlockSpec((nx, deep, LANES), lambda c, *_: (0, 0, 0)),
+            scratch_shapes=scratch,
+        ),
         compiler_params=params(),
         cost_estimate=pl.CostEstimate(
             flops=count * deep * 4 * 8 * nx * nx * 192 * 2,
@@ -453,15 +466,17 @@
             transcendentals=0,
         ),
         name="coils",
-    )(*args)
+    )(*prefetched, *args)
 
 
 def update_kernel(count, b_ref, i_ref, a_ref, *refs):
     o_ref, scratch = refs[-2:]
     part = b_ref.shape[2]
-    for x in range(o_ref.shape[1]):
+    group = o_ref.shape[1]
+    for x in range(group):
+        plane = pl.program_id(0) * group + x
         for d in range(count):
-            scratch[x, pl.ds(d * part, part), :] = b_ref[d, x].astype(F32)
+            scratch[x, pl.ds(d * part, part), :] = b_ref[d, plane].astype(F32)
         grad = scratch[x].astype(BF).T.astype(F32)
         real = jnp.concatenate([grad[0:128], grad[256:320]], axis=0)
         imag = jnp.concatenate([grad[128:256], grad[320:384]], axis=0)
@@ -481,7 +496,7 @@
         out_shape=jax.ShapeDtypeStruct(image.shape, F32),
         grid=(planes // group,),
         in_specs=[
-            pl.BlockSpec((count, group, deep, LANES), lambda x: (0, x, 0, 0)),
+            pl.BlockSpec(memory_space=pltpu.VMEM),
             block,
             block,
         ]
@@ -494,7 +509,7 @@
             flops=0, bytes_accessed=2 * planes * ny * lanes * 12, transcendentals=0
         ),
         name="update",
-    )(back, image, adjoint, *more)
+    )(in_vmem(back), image, adjoint, *more)
 
 
 def exchange(parts):
@@ -508,8 +523,7 @@
 def swap_halves(value):
     count = lax.axis_size("slab")
     half = count // 2
-    other = lax.ppermute(value, "slab", [(i, i ^ half) for i in range(count)])
-    return jnp.concatenate([value, other], axis=0)
+    return lax.ppermute(value, "slab", [(i, i ^ half) for i in range(count)])
 
 
 def gather_half(pair):
@@ -538,42 +552,44 @@
     chosen = sources[0].T
     digits = jnp.concatenate([chosen // BLK, chosen % BLK], axis=0).astype(BF)
     digits = jnp.pad(digits, ((0, TAIL - 4), (0, 2 * BLK - targets)))
-    pair = swap_halves(jnp.concatenate([matrices, digits], axis=0))
-    packed, owner = gather_half(pair)
+    own = jnp.concatenate([matrices, digits], axis=0)
+    crossed = swap_halves(own)
+    packed, owner = gather_half(jnp.concatenate([own, crossed], axis=0))
     digits = packed.reshape(count, targets * BLK + TAIL, 2 * BLK)[:, targets * BLK :]
     digits = digits[:, :4, :targets].astype(jnp.int32)
     links = (digits[:, :2] * BLK + digits[:, 2:]).reshape(-1)
 
-    def run(received, first, size, before, part):
+    def run(received, first, size, before, part, **more):
         maps = received.reshape(nx, received.shape[2], -1, LANES)
-        return coils(maps, first, size, warped, mask, tabs, before, part)
-
-    def back(combined, *needs):
-        grad = spread(combined, packed, links, owner)
+        return coils(maps, first, size, warped, mask, tabs, before, part, **more)
+
+    def back(grad, *needs):
         return exchange(after(grad, *needs).reshape(count, planes, -1, LANES))
 
     columns = exchange(image_columns(image, count))
     warped = warp(columns.reshape(nx, deep, LANES), packed, links, owner)
+    warping = (packed, links, owner)
     halves = parts_of(deep) == 2
     early = total - 3 * total // 8 if halves else total - 1
     late = total - early
     maps = maps_columns(coil_maps, count, 0, early)
-    arrived = exchange(after(maps, columns, pair))
+    arrived = exchange(after(maps, columns, crossed))
     if not halves:
         maps = maps_columns(coil_maps, count, early, late)
         last = exchange(after(maps, arrived, warped))
-        combined = run(last, 0, late, run(arrived, 0, early, None, 0), 0)
-        return update(back(combined), image, adjoint_data, 0, None)
+        combined = run(arrived, 0, early, None, 0)
+        grad = run(last, 0, late, combined, 0, warping=warping)
+        return update(back(grad), image, adjoint_data, 0, None)
 
     first, second = last_maps_columns(coil_maps, count, early, late)
     first = exchange(after(first, arrived, warped))
     combined = run(arrived, 0, early, None, 0)
     second = exchange(after(second, first, combined))
-    half_first = run(first, 0, late, combined, 0)
-    half_second = run(first, late, 1, combined, 1)
-    back_first = back(half_first, second, half_second)
-    half_second = run(second, 0, late - 1, half_second, 1)
-    back_second = back(half_second, back_first)
+    grad = run(first, 0, late, combined, 0, warping=warping)
+    half = run(first, late, 1, combined, 1)
+    back_first = back(grad, second, half)
+    grad = run(second, 0, late - 1, half, 1, warping=warping, landed=True)
+    back_second = back(grad, back_first)
     result = update(back_first, image, adjoint_data, 0, None)
     return update(back_second, image, adjoint_data, 1, result)
 

time: 613 us -> 611 us (level)
  Pallas kernels: 237 us -> 221 us
  local copies, waits for them, and re-layouts: 10.2 us -> 19.2 us
    pallas_call x6 -> x4, Pallas kernels: 148 us -> 137 us  [coils(): pl.pallas_call(functools.partial(coil_kernel, nx, deep, pad, fresh, ends,...]
    unnamed x12 -> x38, local copies, waits for them, and re-layouts: 2.48 us -> 12.1 us
    all_to_all x6, waiting for transfers between devices: 136 us -> 143 us  [exchange(): lax.all_to_all(parts, 'slab', split_axis=0, concat_axis=0, tiled=True)]
  transfers between devices with their start and end apart: 8 -> 8, of which waited for: 6 -> 6; matrix products, arithmetic and copies ran while one was open for 2% -> 1% of each run, Pallas kernels for 37% -> 35%
where the time goes in v8:
time: 611 us; the launch traced here: 608 us
  waiting for transfers between devices  314 us (51%)
  Pallas kernels  221 us (36%)
  starting transfers between devices  37.9 us (6%)
  local copies, waits for them, and re-layouts  19.2 us (3%)
  between operations  13.7 us (2%)
    all_to_all x6, waiting for transfers between devices, exchange(): lax.all_to_all(parts, 'slab', split_axis=0, concat_axis=0, tiled=True)  143 us
    all_gather x1, waiting for transfers between devices, gather_half(): lax.all_gather(pair, 'slab', axis=0, tiled=True, axis_index_groups=groups)  141 us
    pallas_call x4, Pallas kernels, coils(): pl.pallas_call(functools.partial(coil_kernel, nx, deep, pad, fresh, ends,...  137 us
    pallas_call x1, Pallas kernels, maps_columns(): pl.pallas_call(functools.partial(maps_kernel, count, deep), out_shape=jax...  36.2 us
    all_to_all x6, starting transfers between devices, exchange(): lax.all_to_all(parts, 'slab', split_axis=0, concat_axis=0, tiled=True)  35.8 us
    ppermute x1, waiting for transfers between devices, swap_halves(): return lax.ppermute(value, 'slab', [(i, i ^ half) for i in range(count)])  30.8 us
    pallas_call x1, Pallas kernels, last_maps_columns(): pl.pallas_call(functools.partial(last_maps_kernel, count, deep, coils), o...  23.1 us
    pallas_call x1, Pallas kernels, warp(): pl.pallas_call(functools.partial(warp_kernel, nx, deep, pad), out_shape=j...  13.3 us
  transfers between devices with their start and end apart: 8, of which 6 were waited for; matrix products, arithmetic and copies ran while one was open for 1% of the time, Pallas kernels for 35%

profile of v8, /device:TPU:13, one launch (start us, length us, event | category | flops | bytes accessed | tf_op | source)
XLA Modules:
  0.0 608.5 jit_solution(2208794623702733397)
XLA Ops:
  6.5 3.5 image_columns.1
  10.1 0.0 copy-start.1
  10.1 1.4 copy-done.1
  11.5 6.6 %all-to-all-start = ((bf16[16,12,16,384]{3,2,1,0:T(8,128)(2,1)}), bf16[16,12,16,384]{3,2,1,0:T(8,128)(2,1)S(1)}, u32[]{:S(2)}, u32[]{:S(2)}) async-start(bf16[16,12,16,384]{3,2,1,0:T(8,128)(2,1)} %copy-done.1), calls=%async_computation | async-start | bytes 4718592 | tf_op jit(solution)/shard_map/all_to_all | solution.py:516
  18.0 2.2 reshape_squeeze.3
  20.2 0.0 copy-start.18
  20.2 2.2 copy.14
  22.5 2.6 reshape.29
  25.1 2.2 collective-permute-start
  27.3 36.2 %maps_columns.1 = bf16[16,12,5,16,384]{4,3,2,1,0:T(8,128)(2,1)} custom-call(bf16[8,2,12,192,256]{4,3,2,1,0:T(8,128)(2,1)} %x_ref.4), custom_call_target="tpu_custom_call" | custom-call | bytes 23592960 | tf_op jit(solution)/shard_map/maps_columns/pallas_call | solution.py:129
  63.5 30.8 %collective-permute-done = bf16[2320,128]{1,0:T(8,128)(2,1)S(1)} collective-permute-done((bf16[2320,128]{1,0:T(8,128)(2,1)S(1)}, bf16[2320,128]{1,0:T(8,128)(2,1)S(1)}, u32[]{:S(2)}, u32[]{:S(2)}) %collective-permute-start) | collective-permute-done | bytes 593952 | tf_op jit(solution)/shard_map/ppermute | solution.py:526
  94.3 0.0 all-to-all-done
  94.3 8.6 %all-to-all-start.1 = ((bf16[16,12,5,16,384]{4,3,2,1,0:T(8,128)(2,1)}), bf16[16,12,5,16,384]{4,3,2,1,0:T(8,128)(2,1)}, u32[]{:S(2)}, u32[]{:S(2)}) async-start(bf16[16,12,5,16,384]{4,3,2,1,0:T(8,128)(2,1)} %maps_columns.1), calls=%async_computation.1 | async-start | bytes 23592960 | tf_op jit(solution)/shard_map/all_to_all | solution.py:516
  102.9 0.0 all-gather.2.cloned.1.call-start
  103.0 1.1 pad_maximum_fusion
  104.1 0.0 all-gather.2.cloned.1.call-update
  104.1 23.1 %last_maps_columns.1 = (bf16[16,12,4,8,384]{4,3,2,1,0:T(8,128)(2,1)}, bf16[16,12,2,8,384]{4,3,2,1,0:T(8,128)(2,1)S(1)}) custom-call(bf16[8,2,12,192,256]{4,3,2,1,0:T(8,128)(2,1)} %x_ref.4), custom_call_target="tpu_custom_call" | custom-call | bytes 14155776 | tf_op jit(solution)/shard_map/last_maps_columns/pallas_call | solution.py:148
  127.2 1.4 copy-done.3
  128.6 140.6 %all-gather.2.cloned.1.call-done.w_hbm.refs_10_ = bf16[37120,128]{1,0:T(8,128)(2,1)} async-done(((bf16[4640,128]{1,0:T(8,128)(2,1)}), bf16[37120,128]{1,0:T(8,128)(2,1)}) %all-gather.2.cloned.1.call-update) | async-done | bytes 9502736 | tf_op jit(solution)/shard_map/all_gather | solution.py:533
  269.2 0.8 slice_convert_fusion
  270.0 0.1 reshape.31.links.refs_0_
  270.1 13.3 %warp.1.refs_1_.refs_3_ = f32[192,16,384]{2,1,0:T(8,128)} custom-call(s32[1152]{0:T(1024)S(1)} %reshape.31.links.refs_0_, s32[16]{0:T(128)S(1)} %fusion.10.owner.refs_1_, bf16[192,16,384]{2,1,0:T(8,128)(2,1)S(1)} %bitcast.36, bf16[37120,128]{1,0:T(8,128)(2,1)} %all-gather.2.cloned.1.call-done.w_hbm.refs_10_), custom_call_target="tpu_custom_call" | custom-call | flops 2415919104 | bytes 20971520 | tf_op jit(solution)/shard_map/warp/pallas_call | solution.py:237
  283.4 76.2 %all-to-all-done.1 = bf16[16,12,5,16,384]{4,3,2,1,0:T(8,128)(2,1)} async-done(((bf16[16,12,5,16,384]{4,3,2,1,0:T(8,128)(2,1)}), bf16[16,12,5,16,384]{4,3,2,1,0:T(8,128)(2,1)}, u32[]{:S(2)}, u32[]{:S(2)}) %all-to-all-start.1) | async-done | bytes 11796512 | tf_op jit(solution)/shard_map/all_to_all | solution.py:516
  359.6 0.0 copy-start.14
  359.6 4.6 all-to-all-start.2
  364.3 68.8 %coils.4.refs_7_.refs_9_ = f32[192,16,384]{2,1,0:T(8,128)} custom-call(bf16[192,5,16,384]{3,2,1,0:T(8,128)(2,1)} %bitcast.6.refs_0_, f32[192,16,384]{2,1,0:T(8,128)} %warp.1.refs_1_.refs_3_, f32[384,256]{1,0:T(8,128)S(1)} %pad_maximum_fusion.2.refs_2_.refs_4_, bf16[384,512]{1,0:T(8,128)(2,1)S(1)} %copy-done.7, bf16[384,384]{1,0:T(8,128)(2,1)S(1)} %copy-done.11, ...), custom_call_target="tpu_custom_call" | custom-call | flops 36238786560 | bytes 26476544 | tf_op jit(solution)/shard_map/coils/pallas_call | solution.py:452
  433.1 34.3 %all-to-all-done.2 = bf16[16,12,4,8,384]{4,3,2,1,0:T(8,128)(2,1)} async-done(((bf16[16,12,4,8,384]{4,3,2,1,0:T(8,128)(2,1)}), bf16[16,12,4,8,384]{4,3,2,1,0:T(8,128)(2,1)}, u32[]{:S(2)}, u32[]{:S(2)}) %all-to-all-start.2) | async-done | bytes 4718624 | tf_op jit(solution)/shard_map/all_to_all | solution.py:516
  467.5 4.9 all-to-all-start.3
  472.4 1.0 copy-done.12
  473.3 1.0 copy-done.15
  474.3 8.2 %coils.5.refs_9_ = f32[192,8,384]{2,1,0:T(8,128)S(1)} custom-call(bf16[192,4,8,384]{3,2,1,0:T(8,128)(2,1)} %bitcast.9.refs_0_.refs_2_, f32[192,16,384]{2,1,0:T(8,128)} %warp.1.refs_1_.refs_3_, f32[384,256]{1,0:T(8,128)S(1)} %pad_maximum_fusion.2.refs_2_.refs_4_, bf16[384,512]{1,0:T(8,128)(2,1)S(1)} %copy-done.7, bf16[384,384]{1,0:T(8,128)(2,1)S(1)} %copy-done.12, ...), custom_call_target="tpu_custom_call" | custom-call | flops 3623878656 | bytes 15859712 | tf_op jit(solution)/shard_map/coils/pallas_call | solution.py:452
  482.6 0.0 copy-start.2
  482.6 1.4 copy-done.2
  484.0 32.9 %coils.7 = bf16[192,8,384]{2,1,0:T(8,128)(2,1)} custom-call(s32[1152]{0:T(1024)S(1)} %reshape.31.links.refs_0_, s32[16]{0:T(128)S(1)} %fusion.10.owner.refs_1_, bf16[192,4,8,384]{3,2,1,0:T(8,128)(2,1)} %bitcast.9.refs_0_.refs_2_, f32[192,16,384]{2,1,0:T(8,128)} %warp.1.refs_1_.refs_3_, f32[384,256]{1,0:T(8,128)S(1)} %pad_maximum_fusion.2.refs_2_.refs_4_, ...), custom_call_target="tpu_custom_call" | custom-call | flops 10871635968 | bytes 18219008 | tf_op jit(solution)/shard_map/coils/pallas_call | solution.py:452
  516.9 8.6 %all-to-all-done.3 = bf16[16,12,2,8,384]{4,3,2,1,0:T(8,128)(2,1)} async-done(((bf16[16,12,2,8,384]{4,3,2,1,0:T(8,128)(2,1)}), bf16[16,12,2,8,384]{4,3,2,1,0:T(8,128)(2,1)}, u32[]{:S(2)}, u32[]{:S(2)}) %all-to-all-start.3) | async-done | bytes 2359328 | tf_op jit(solution)/shard_map/all_to_all | solution.py:516
  525.5 4.9 all-to-all-start.4
  530.4 1.0 copy-done.5
  531.4 1.0 copy-done.8
  532.4 1.0 copy-done.10
  533.4 1.0 copy-done.13
  534.4 1.0 copy-done.16
  535.3 26.7 %coils.6 = bf16[192,8,384]{2,1,0:T(8,128)(2,1)S(1)} custom-call(s32[1152]{0:T(1024)S(1)} %reshape.31.links.refs_0_, s32[16]{0:T(128)S(1)} %fusion.10.owner.refs_1_, bf16[192,2,8,384]{3,2,1,0:T(8,128)(2,1)} %bitcast.8.refs_2_, f32[192,16,384]{2,1,0:T(8,128)} %warp.1.refs_1_.refs_3_, f32[384,256]{1,0:T(8,128)S(1)} %copy-done.5, ...), custom_call_target="tpu_custom_call" | custom-call | flops 7247757312 | bytes 17039360 | tf_op jit(solution)/shard_map/coils/pallas_call | solution.py:452
  562.0 1.0 copy-done.6
  563.0 0.0 all-to-all-done.4.b_ref
  563.0 6.2 %all-to-all-start.5 = ((bf16[16,12,8,384]{3,2,1,0:T(8,128)(2,1)}), bf16[16,12,8,384]{3,2,1,0:T(8,128)(2,1)}, u32[]{:S(2)}, u32[]{:S(2)}) async-start(bf16[16,12,8,384]{3,2,1,0:T(8,128)(2,1)} %bitcast.37), calls=%async_computation.5 | async-start | bytes 2359296 | tf_op jit(solution)/shard_map/all_to_all | solution.py:516
  569.2 4.2 update.2.refs_0_
  573.4 23.7 %all-to-all-done.5.b_ref = bf16[16,12,8,384]{3,2,1,0:T(8,128)(2,1)} async-done(((bf16[16,12,8,384]{3,2,1,0:T(8,128)(2,1)}), bf16[16,12,8,384]{3,2,1,0:T(8,128)(2,1)}, u32[]{:S(2)}, u32[]{:S(2)}) %all-to-all-start.5) | async-done | bytes 1179680 | tf_op jit(solution)/shard_map/all_to_all | solution.py:516
  597.1 4.5 update.3
  (31 shorter events, 0.2 us)
Async XLA Ops:
  10.1 1.4 copy-start.1
  11.5 82.9 %all-to-all-start = ((bf16[16,12,16,384]{3,2,1,0:T(8,128)(2,1)}), bf16[16,12,16,384]{3,2,1,0:T(8,128)(2,1)S(1)}, u32[]{:S(2)}, u32[]{:S(2)}) async-start(bf16[16,12,16,384]{3,2,1,0:T(8,128)(2,1)} %copy-done.1), calls=%async_computation | async-start | bytes 4718592 | tf_op jit(solution)/shard_map/all_to_all | solution.py:516
  20.2 4.8 copy-start.18
  25.1 69.2 %collective-permute-start = (bf16[2320,128]{1,0:T(8,128)(2,1)S(1)}, bf16[2320,128]{1,0:T(8,128)(2,1)S(1)}, u32[]{:S(2)}, u32[]{:S(2)}) collective-permute-start(bf16[2320,128]{1,0:T(8,128)(2,1)S(1)} %pad_maximum_fusion.1), channel_id=1, source_target_pairs={{0,8},{1,9},{2,10},{3,11},{4,12},{5,13},{6,14},{7,15},{8,0},{9,1},... | collective-permute-start | bytes 1781768 | tf_op jit(solution)/shard_map/ppermute | solution.py:526
  94.3 265.2 %all-to-all-start.1 = ((bf16[16,12,5,16,384]{4,3,2,1,0:T(8,128)(2,1)}), bf16[16,12,5,16,384]{4,3,2,1,0:T(8,128)(2,1)}, u32[]{:S(2)}, u32[]{:S(2)}) async-start(bf16[16,12,5,16,384]{4,3,2,1,0:T(8,128)(2,1)} %maps_columns.1), calls=%async_computation.1 | async-start | bytes 23592960 | tf_op jit(solution)/shard_map/all_to_all | solution.py:516
  102.9 166.3 %all-gather.2.cloned.1.call-start = ((), (), s32[]{:S(2)}) async-start(), calls=%async_computation.6 | async-start | bytes 10690560 | tf_op jit(solution)/shard_map/all_gather | solution.py:533
  127.2 1.4 copy-start.3
  359.5 4.6 copy-start.17
  359.5 4.7 copy-start.7
  359.5 4.7 copy-start.9
  359.5 4.8 copy-start.11
  359.6 4.8 copy-start.14
  359.6 107.9 %all-to-all-start.2 = ((bf16[16,12,4,8,384]{4,3,2,1,0:T(8,128)(2,1)}), bf16[16,12,4,8,384]{4,3,2,1,0:T(8,128)(2,1)}, u32[]{:S(2)}, u32[]{:S(2)}) async-start(bf16[16,12,4,8,384]{4,3,2,1,0:T(8,128)(2,1)} %get-tuple-element.15), calls=%async_computation.2 | async-start | bytes 9437184 | tf_op jit(solution)/shard_map/all_to_all | solution.py:516
  364.3 118.3 %copy-start.4 = (f32[384,256]{1,0:T(8,128)}, f32[384,256]{1,0:T(8,128)S(1)}, u32[]{:S(2)}) copy-start(f32[384,256]{1,0:T(8,128)S(1)} %pad_maximum_fusion.2.refs_2_.refs_4_) | copy-start | bytes 1179652
  467.5 58.1 %all-to-all-start.3 = ((bf16[16,12,2,8,384]{4,3,2,1,0:T(8,128)(2,1)}), bf16[16,12,2,8,384]{4,3,2,1,0:T(8,128)(2,1)}, u32[]{:S(2)}, u32[]{:S(2)}) async-start(bf16[16,12,2,8,384]{4,3,2,1,0:T(8,128)(2,1)} %copy-done.3), calls=%async_computation.3 | async-start | bytes 4718592 | tf_op jit(solution)/shard_map/all_to_all | solution.py:516
  472.4 1.0 copy-start.12
  473.3 1.0 copy-start.15
  482.6 1.4 copy-start.2
  525.5 37.5 %all-to-all-start.4 = ((bf16[16,12,8,384]{3,2,1,0:T(8,128)(2,1)}), bf16[16,12,8,384]{3,2,1,0:T(8,128)(2,1)S(1)}, u32[]{:S(2)}, u32[]{:S(2)}) async-start(bf16[16,12,8,384]{3,2,1,0:T(8,128)(2,1)} %bitcast.10), calls=%async_computation.4 | async-start | bytes 2359296 | tf_op jit(solution)/shard_map/all_to_all | solution.py:516
  530.4 1.0 copy-start.5
  531.4 1.0 copy-start.8
  532.4 1.0 copy-start.10
  533.4 1.0 copy-start.13
  534.4 1.0 copy-start.16
  562.0 1.0 copy-start.6
  563.0 6.2 %copy-start = (bf16[2,12,192,256]{3,2,1,0:T(8,128)(2,1)S(1)}, bf16[2,12,192,256]{3,2,1,0:T(8,128)(2,1)}, u32[]{:S(2)}) copy-start(bf16[2,12,192,256]{3,2,1,0:T(8,128)(2,1)} %a_ref.3) | copy-start | bytes 7077892
  563.0 34.0 %all-to-all-start.5 = ((bf16[16,12,8,384]{3,2,1,0:T(8,128)(2,1)}), bf16[16,12,8,384]{3,2,1,0:T(8,128)(2,1)}, u32[]{:S(2)}, u32[]{:S(2)}) async-start(bf16[16,12,8,384]{3,2,1,0:T(8,128)(2,1)} %bitcast.37), calls=%async_computation.5 | async-start | bytes 2359296 | tf_op jit(solution)/shard_map/all_to_all | solution.py:516
Sparse Core Ops, SparseCore 0:
  105.4 163.7 all-gather.1

commit v9 on v8

--- a/solution.py
+++ b/solution.py
@@ -13,7 +13,7 @@
 LANES = 384
 TAIL = 16
 HALF = 256
-VMEM_LIMIT = 48 * 1024 * 1024
+VMEM_LIMIT = 56 * 1024 * 1024
 BF = jnp.bfloat16
 F32 = jnp.float32
 

time: 611 us -> 605 us (level)
  local copies, waits for them, and re-layouts: 19.2 us -> 7.74 us
  Pallas kernels: 221 us -> 228 us
    unnamed x38 -> x4, local copies, waits for them, and re-layouts: 12.1 us -> 0.01 us
  transfers between devices with their start and end apart: 8 -> 8, of which waited for: 6 -> 7; matrix products, arithmetic and copies ran while one was open for 1% -> 2% of each run, Pallas kernels for 35% -> 36%
where the time goes in v9:
time: 605 us; the launch traced here: 603 us
  waiting for transfers between devices  313 us (52%)
  Pallas kernels  228 us (38%)
  starting transfers between devices  37.8 us (6%)
  between operations  13.5 us (2%)
  local copies, waits for them, and re-layouts  7.74 us (1%)
    all_to_all x6, waiting for transfers between devices, exchange(): lax.all_to_all(parts, 'slab', split_axis=0, concat_axis=0, tiled=True)  141 us
    pallas_call x4, Pallas kernels, coils(): pl.pallas_call(functools.partial(coil_kernel, nx, deep, pad, fresh, ends,...  141 us
    all_gather x1, waiting for transfers between devices, gather_half(): lax.all_gather(pair, 'slab', axis=0, tiled=True, axis_index_groups=groups)  140 us
    pallas_call x1, Pallas kernels, maps_columns(): pl.pallas_call(functools.partial(maps_kernel, count, deep), out_shape=jax...  36.3 us
    all_to_all x6, starting transfers between devices, exchange(): lax.all_to_all(parts, 'slab', split_axis=0, concat_axis=0, tiled=True)  35.6 us
    ppermute x1, waiting for transfers between devices, swap_halves(): return lax.ppermute(value, 'slab', [(i, i ^ half) for i in range(count)])  30.7 us
    pallas_call x1, Pallas kernels, last_maps_columns(): pl.pallas_call(functools.partial(last_maps_kernel, count, deep, coils), o...  24.1 us
    pallas_call x1, Pallas kernels, warp(): pl.pallas_call(functools.partial(warp_kernel, nx, deep, pad), out_shape=j...  13.4 us
  transfers between devices with their start and end apart: 8, of which 7 were waited for; matrix products, arithmetic and copies ran while one was open for 2% of the time, Pallas kernels for 36%

profile of v9, /device:TPU:13, one launch (start us, length us, event | category | flops | bytes accessed | tf_op | source)
XLA Modules:
  0.0 602.7 jit_solution(10348825683449758696)
XLA Ops:
  6.5 4.7 image_columns.1
  11.2 6.6 %all-to-all-start = ((bf16[16,12,16,384]{3,2,1,0:T(8,128)(2,1)}), bf16[16,12,16,384]{3,2,1,0:T(8,128)(2,1)S(1)}, u32[]{:S(2)}, u32[]{:S(2)}) async-start(bf16[16,12,16,384]{3,2,1,0:T(8,128)(2,1)} %image_columns.1), calls=%async_computation | async-start | bytes 4718592 | tf_op jit(solution)/shard_map/all_to_all | solution.py:516
  17.8 2.2 reshape_squeeze.3
  20.0 0.0 copy-start.1
  20.0 2.3 copy.14
  22.2 2.6 reshape.29
  24.8 0.0 copy-done.1
  24.9 2.2 collective-permute-start
  27.1 36.3 %maps_columns.1 = bf16[16,12,5,16,384]{4,3,2,1,0:T(8,128)(2,1)} custom-call(bf16[8,2,12,192,256]{4,3,2,1,0:T(8,128)(2,1)} %x_ref.4), custom_call_target="tpu_custom_call" | custom-call | bytes 23592960 | tf_op jit(solution)/shard_map/maps_columns/pallas_call | solution.py:129
  63.3 30.7 %collective-permute-done = bf16[2320,128]{1,0:T(8,128)(2,1)S(1)} collective-permute-done((bf16[2320,128]{1,0:T(8,128)(2,1)S(1)}, bf16[2320,128]{1,0:T(8,128)(2,1)S(1)}, u32[]{:S(2)}, u32[]{:S(2)}) %collective-permute-start) | collective-permute-done | bytes 593952 | tf_op jit(solution)/shard_map/ppermute | solution.py:526
  94.1 0.0 all-to-all-done
  94.1 8.6 %all-to-all-start.1 = ((bf16[16,12,5,16,384]{4,3,2,1,0:T(8,128)(2,1)}), bf16[16,12,5,16,384]{4,3,2,1,0:T(8,128)(2,1)}, u32[]{:S(2)}, u32[]{:S(2)}) async-start(bf16[16,12,5,16,384]{4,3,2,1,0:T(8,128)(2,1)} %maps_columns.1), calls=%async_computation.1 | async-start | bytes 23592960 | tf_op jit(solution)/shard_map/all_to_all | solution.py:516
  102.7 0.0 all-gather.2.cloned.1.call-start
  102.7 1.1 pad_maximum_fusion
  103.9 0.0 all-gather.2.cloned.1.call-update
  103.9 24.1 %last_maps_columns.1 = (bf16[16,12,4,8,384]{4,3,2,1,0:T(8,128)(2,1)}, bf16[16,12,2,8,384]{4,3,2,1,0:T(8,128)(2,1)}) custom-call(bf16[8,2,12,192,256]{4,3,2,1,0:T(8,128)(2,1)} %x_ref.4), custom_call_target="tpu_custom_call" | custom-call | bytes 14155776 | tf_op jit(solution)/shard_map/last_maps_columns/pallas_call | solution.py:148
  128.0 0.5 fusion.10.owner.refs_1_
  128.5 140.4 %all-gather.2.cloned.1.call-done.w_hbm.refs_10_ = bf16[37120,128]{1,0:T(8,128)(2,1)} async-done(((bf16[4640,128]{1,0:T(8,128)(2,1)}), bf16[37120,128]{1,0:T(8,128)(2,1)}) %all-gather.2.cloned.1.call-update) | async-done | bytes 9502736 | tf_op jit(solution)/shard_map/all_gather | solution.py:533
  268.9 0.8 slice_convert_fusion
  269.7 0.7 reshape.31.links.refs_0_
  270.4 13.4 %warp.1.refs_1_.refs_3_ = f32[192,16,384]{2,1,0:T(8,128)} custom-call(s32[1152]{0:T(1024)} %reshape.31.links.refs_0_, s32[16]{0:T(128)} %fusion.10.owner.refs_1_, bf16[192,16,384]{2,1,0:T(8,128)(2,1)S(1)} %bitcast.36, bf16[37120,128]{1,0:T(8,128)(2,1)} %all-gather.2.cloned.1.call-done.w_hbm.refs_10_), custom_call_target="tpu_custom_call" | custom-call | flops 2415919104 | bytes 20971520 | tf_op jit(solution)/shard_map/warp/pallas_call | solution.py:237
  283.8 75.5 %all-to-all-done.1 = bf16[16,12,5,16,384]{4,3,2,1,0:T(8,128)(2,1)} async-done(((bf16[16,12,5,16,384]{4,3,2,1,0:T(8,128)(2,1)}), bf16[16,12,5,16,384]{4,3,2,1,0:T(8,128)(2,1)}, u32[]{:S(2)}, u32[]{:S(2)}) %all-to-all-start.1) | async-done | bytes 11796512 | tf_op jit(solution)/shard_map/all_to_all | solution.py:516
  359.3 0.0 copy-start
  359.3 4.6 all-to-all-start.2
  363.9 0.0 copy-done
  364.0 0.8 pad_maximum_fusion.2.refs_2_.refs_4_
  364.7 69.4 %coils.4.refs_7_.refs_9_ = f32[192,16,384]{2,1,0:T(8,128)} custom-call(bf16[192,5,16,384]{3,2,1,0:T(8,128)(2,1)} %bitcast.6.refs_0_, f32[192,16,384]{2,1,0:T(8,128)} %warp.1.refs_1_.refs_3_, f32[384,256]{1,0:T(8,128)} %pad_maximum_fusion.2.refs_2_.refs_4_, bf16[384,512]{1,0:T(8,128)(2,1)} %constant.87.clone.refs_3_.refs_5_, ...), custom_call_target="tpu_custom_call" | custom-call | flops 36238786560 | bytes 26476544 | tf_op jit(solution)/shard_map/coils/pallas_call | solution.py:452
  434.1 33.1 %all-to-all-done.2 = bf16[16,12,4,8,384]{4,3,2,1,0:T(8,128)(2,1)} async-done(((bf16[16,12,4,8,384]{4,3,2,1,0:T(8,128)(2,1)}), bf16[16,12,4,8,384]{4,3,2,1,0:T(8,128)(2,1)}, u32[]{:S(2)}, u32[]{:S(2)}) %all-to-all-start.2) | async-done | bytes 4718624 | tf_op jit(solution)/shard_map/all_to_all | solution.py:516
  467.2 4.9 all-to-all-start.3
  472.1 10.2 %coils.5.refs_9_ = f32[192,8,384]{2,1,0:T(8,128)} custom-call(bf16[192,4,8,384]{3,2,1,0:T(8,128)(2,1)} %bitcast.9.refs_0_.refs_2_, f32[192,16,384]{2,1,0:T(8,128)} %warp.1.refs_1_.refs_3_, f32[384,256]{1,0:T(8,128)} %pad_maximum_fusion.2.refs_2_.refs_4_, bf16[384,512]{1,0:T(8,128)(2,1)} %constant.87.clone.refs_3_.refs_5_, ...), custom_call_target="tpu_custom_call" | custom-call | flops 3623878656 | bytes 15859712 | tf_op jit(solution)/shard_map/coils/pallas_call | solution.py:452
  482.3 33.5 %coils.7 = bf16[192,8,384]{2,1,0:T(8,128)(2,1)} custom-call(s32[1152]{0:T(1024)} %reshape.31.links.refs_0_, s32[16]{0:T(128)} %fusion.10.owner.refs_1_, bf16[192,4,8,384]{3,2,1,0:T(8,128)(2,1)} %bitcast.9.refs_0_.refs_2_, f32[192,16,384]{2,1,0:T(8,128)} %warp.1.refs_1_.refs_3_, f32[384,256]{1,0:T(8,128)} %pad_maximum_fusion.2.refs_2_.refs_4_, ...), custom_call_target="tpu_custom_call" | custom-call | flops 10871635968 | bytes 18219008 | tf_op jit(solution)/shard_map/coils/pallas_call | solution.py:452
  515.8 9.3 %all-to-all-done.3 = bf16[16,12,2,8,384]{4,3,2,1,0:T(8,128)(2,1)S(1)} async-done(((bf16[16,12,2,8,384]{4,3,2,1,0:T(8,128)(2,1)}), bf16[16,12,2,8,384]{4,3,2,1,0:T(8,128)(2,1)S(1)}, u32[]{:S(2)}, u32[]{:S(2)}) %all-to-all-start.3) | async-done | bytes 2359328 | tf_op jit(solution)/shard_map/all_to_all | solution.py:516
  525.1 4.9 all-to-all-start.4
  530.0 27.7 %coils.6 = bf16[192,8,384]{2,1,0:T(8,128)(2,1)} custom-call(s32[1152]{0:T(1024)} %reshape.31.links.refs_0_, s32[16]{0:T(128)} %fusion.10.owner.refs_1_, bf16[192,2,8,384]{3,2,1,0:T(8,128)(2,1)S(1)} %bitcast.37, f32[192,16,384]{2,1,0:T(8,128)} %warp.1.refs_1_.refs_3_, f32[384,256]{1,0:T(8,128)} %pad_maximum_fusion.2.refs_2_.refs_4_, ...), custom_call_target="tpu_custom_call" | custom-call | flops 7247757312 | bytes 17039360 | tf_op jit(solution)/shard_map/coils/pallas_call | solution.py:452
  557.7 0.1 all-to-all-done.4.b_ref
  557.8 6.0 all-to-all-start.5
  563.8 4.3 update.2.refs_0_
  568.1 23.4 %all-to-all-done.5.b_ref = bf16[16,12,8,384]{3,2,1,0:T(8,128)(2,1)S(1)} async-done(((bf16[16,12,8,384]{3,2,1,0:T(8,128)(2,1)}), bf16[16,12,8,384]{3,2,1,0:T(8,128)(2,1)S(1)}, u32[]{:S(2)}, u32[]{:S(2)}) %all-to-all-start.5) | async-done | bytes 1179680 | tf_op jit(solution)/shard_map/all_to_all | solution.py:516
  591.5 4.3 update.3
  (6 shorter events, 0.1 us)
Async XLA Ops:
  11.2 82.9 %all-to-all-start = ((bf16[16,12,16,384]{3,2,1,0:T(8,128)(2,1)}), bf16[16,12,16,384]{3,2,1,0:T(8,128)(2,1)S(1)}, u32[]{:S(2)}, u32[]{:S(2)}) async-start(bf16[16,12,16,384]{3,2,1,0:T(8,128)(2,1)} %image_columns.1), calls=%async_computation | async-start | bytes 4718592 | tf_op jit(solution)/shard_map/all_to_all | solution.py:516
  20.0 4.8 copy-start.1
  24.9 69.1 %collective-permute-start = (bf16[2320,128]{1,0:T(8,128)(2,1)S(1)}, bf16[2320,128]{1,0:T(8,128)(2,1)S(1)}, u32[]{:S(2)}, u32[]{:S(2)}) collective-permute-start(bf16[2320,128]{1,0:T(8,128)(2,1)S(1)} %pad_maximum_fusion.1), channel_id=1, source_target_pairs={{0,8},{1,9},{2,10},{3,11},{4,12},{5,13},{6,14},{7,15},{8,0},{9,1},... | collective-permute-start | bytes 1781768 | tf_op jit(solution)/shard_map/ppermute | solution.py:526
  94.1 265.2 %all-to-all-start.1 = ((bf16[16,12,5,16,384]{4,3,2,1,0:T(8,128)(2,1)}), bf16[16,12,5,16,384]{4,3,2,1,0:T(8,128)(2,1)}, u32[]{:S(2)}, u32[]{:S(2)}) async-start(bf16[16,12,5,16,384]{4,3,2,1,0:T(8,128)(2,1)} %maps_columns.1), calls=%async_computation.1 | async-start | bytes 23592960 | tf_op jit(solution)/shard_map/all_to_all | solution.py:516
  102.7 166.3 %all-gather.2.cloned.1.call-start = ((), (), s32[]{:S(2)}) async-start(), calls=%async_computation.6 | async-start | bytes 10690560 | tf_op jit(solution)/shard_map/all_gather | solution.py:533
  359.3 4.6 copy-start
  359.3 107.9 %all-to-all-start.2 = ((bf16[16,12,4,8,384]{4,3,2,1,0:T(8,128)(2,1)}), bf16[16,12,4,8,384]{4,3,2,1,0:T(8,128)(2,1)}, u32[]{:S(2)}, u32[]{:S(2)}) async-start(bf16[16,12,4,8,384]{4,3,2,1,0:T(8,128)(2,1)} %get-tuple-element.15), calls=%async_computation.2 | async-start | bytes 9437184 | tf_op jit(solution)/shard_map/all_to_all | solution.py:516
  467.2 57.9 %all-to-all-start.3 = ((bf16[16,12,2,8,384]{4,3,2,1,0:T(8,128)(2,1)}), bf16[16,12,2,8,384]{4,3,2,1,0:T(8,128)(2,1)S(1)}, u32[]{:S(2)}, u32[]{:S(2)}) async-start(bf16[16,12,2,8,384]{4,3,2,1,0:T(8,128)(2,1)} %get-tuple-element.16), calls=%async_computation.3 | async-start | bytes 4718592 | tf_op jit(solution)/shard_map/all_to_all | solution.py:516
  525.1 32.7 %all-to-all-start.4 = ((bf16[16,12,8,384]{3,2,1,0:T(8,128)(2,1)}), bf16[16,12,8,384]{3,2,1,0:T(8,128)(2,1)S(1)}, u32[]{:S(2)}, u32[]{:S(2)}) async-start(bf16[16,12,8,384]{3,2,1,0:T(8,128)(2,1)} %bitcast.40), calls=%async_computation.4 | async-start | bytes 2359296 | tf_op jit(solution)/shard_map/all_to_all | solution.py:516
  557.8 33.7 %all-to-all-start.5 = ((bf16[16,12,8,384]{3,2,1,0:T(8,128)(2,1)}), bf16[16,12,8,384]{3,2,1,0:T(8,128)(2,1)S(1)}, u32[]{:S(2)}, u32[]{:S(2)}) async-start(bf16[16,12,8,384]{3,2,1,0:T(8,128)(2,1)} %bitcast.41), calls=%async_computation.5 | async-start | bytes 2359296 | tf_op jit(solution)/shard_map/all_to_all | solution.py:516
Sparse Core Ops, SparseCore 0:
  105.1 163.7 all-gather.1

commit v10 on v9

--- a/solution.py
+++ b/solution.py
@@ -89,7 +89,7 @@
 def image_columns(image, count):
     _, planes, ny, nz = image.shape
     deep = nz // count
-    group = 3 if planes % 3 == 0 else 1
+    group = math.gcd(planes, 6)
     return pl.pallas_call(
         functools.partial(image_kernel, count, deep),
         out_shape=jax.ShapeDtypeStruct((count, planes, deep, LANES), BF),
@@ -313,12 +313,13 @@
     lax.fori_loop(0, nx, gather, 0, unroll=8)
 
 
-def coil_kernel(nx, deep, pad, fresh, ends, landed, *refs):
+def coil_kernel(nx, deep, pad, skip, ends, landed, *refs):
+    fresh = skip is None
     if ends:
         links, owner, *refs = refs
     s_ref, w_ref, mask, iy, fx, bx, oy, *refs = refs
     if not fresh:
-        before, *refs = refs
+        before, *refs, sem = refs
     if ends:
         w_hbm, grad_ref, rows, o_ref, held, total, sems = refs
 
@@ -327,6 +328,10 @@
             fetch_all(w_hbm, held, sems)
     else:
         o_ref, rows = refs
+    first = pl.program_id(0) == 0
+    if not fresh:
+        earlier = pltpu.make_async_copy(before.at[:, pl.ds(skip, deep), :], o_ref, sem)
+        pl.when(first)(earlier.start)
     s_ref = s_ref.at[:, pl.program_id(0) if landed else 0]
     group = 8 if nx % 8 == 0 else 1
     cube = rows.reshape(3, nx, pad, 128)
@@ -383,7 +388,8 @@
 
     lax.fori_loop(0, deep // batch, column, 0)
 
-    first = pl.program_id(0) == 0
+    if not fresh:
+        pl.when(first)(earlier.wait)
 
     def combine(i, carry):
         at = pl.ds(i * group, group)
@@ -401,8 +407,9 @@
         for v in range(3):
             lanes = slice(v * 128, (v + 1) * 128)
             old = o_ref[at, :, lanes]
-            start = jnp.zeros_like(old) if fresh else before[at, :, lanes]
-            o_ref[at, :, lanes] = jnp.where(first, start, old) + terms[v]
+            if fresh:
+                old = jnp.where(first, jnp.zeros_like(old), old)
+            o_ref[at, :, lanes] = old + terms[v]
         return carry
 
     lax.fori_loop(0, nx // group, combine, 0, unroll=4)
@@ -434,9 +441,11 @@
         in_specs = [pl.BlockSpec((nx, 1, deep, LANES), lambda c, *_: (0, first + c, 0, 0))]
     args = [maps, warped, mask, *tabs]
     in_specs += [columns(warped)] + [whole(a.shape) for a in (mask, *tabs)]
+    skip = None
     if not fresh:
         args += [before]
-        in_specs += [columns(before)]
+        in_specs += [pl.BlockSpec(memory_space=pl.ANY)]
+        skip = part * deep if before.shape[1] > deep else 0
     scratch = [pltpu.VMEM((3, nx * pad, 128), F32)]
     prefetched = []
     if ends:
@@ -449,8 +458,10 @@
             pltpu.VMEM((3 * nx, 2 * pad, 128), F32),
             pltpu.SemaphoreType.DMA((prefetched[1].shape[0],)),
         ]
+    if not fresh:
+        scratch += [pltpu.SemaphoreType.DMA]
     return pl.pallas_call(
-        functools.partial(coil_kernel, nx, deep, pad, fresh, ends, landed),
+        functools.partial(coil_kernel, nx, deep, pad, skip, ends, landed),
         out_shape=jax.ShapeDtypeStruct((nx, deep, LANES), BF if ends else F32),
         grid_spec=pltpu.PrefetchScalarGridSpec(
             num_scalar_prefetch=len(prefetched),
@@ -488,7 +499,7 @@
     count, planes, deep, _ = back.shape
     _, _, ny, _ = image.shape
     lanes = count * deep
-    group = 3 if planes % 3 == 0 else 1
+    group = math.gcd(planes, 6)
     block = pl.BlockSpec((2, group, ny, lanes), lambda x: (0, x, 0, part))
     more = [] if before is None else [before]
     return pl.pallas_call(

time: 605 us -> 602 us (level)
  no operation moved by 1% of the time
where the time goes in v10:
time: 602 us; the launch traced here: 600 us
  waiting for transfers between devices  316 us (52%)
  Pallas kernels  222 us (37%)
  starting transfers between devices  36.9 us (6%)
  between operations  13.5 us (2%)
  local copies, waits for them, and re-layouts  7.74 us (1%)
    all_to_all x6, waiting for transfers between devices, exchange(): lax.all_to_all(parts, 'slab', split_axis=0, concat_axis=0, tiled=True)  145 us
    all_gather x1, waiting for transfers between devices, gather_half(): lax.all_gather(pair, 'slab', axis=0, tiled=True, axis_index_groups=groups)  140 us
    pallas_call x4, Pallas kernels, coils(): pl.pallas_call(functools.partial(coil_kernel, nx, deep, pad, skip, ends,...  138 us
    pallas_call x1, Pallas kernels, maps_columns(): pl.pallas_call(functools.partial(maps_kernel, count, deep), out_shape=jax...  36.3 us
    all_to_all x6, starting transfers between devices, exchange(): lax.all_to_all(parts, 'slab', split_axis=0, concat_axis=0, tiled=True)  34.7 us
    ppermute x1, waiting for transfers between devices, swap_halves(): return lax.ppermute(value, 'slab', [(i, i ^ half) for i in range(count)])  30.7 us
    pallas_call x1, Pallas kernels, last_maps_columns(): pl.pallas_call(functools.partial(last_maps_kernel, count, deep, coils), o...  24.1 us
    pallas_call x1, Pallas kernels, warp(): pl.pallas_call(functools.partial(warp_kernel, nx, deep, pad), out_shape=j...  13.4 us
  transfers between devices with their start and end apart: 8, of which 7 were waited for; matrix products, arithmetic and copies ran while one was open for 2% of the time, Pallas kernels for 36%

profile of v10, /device:TPU:13, one launch (start us, length us, event | category | flops | bytes accessed | tf_op | source)
XLA Modules:
  0.0 599.8 jit_solution(16762171404817813193)
XLA Ops:
  6.5 3.7 image_columns.1
  10.3 6.6 %all-to-all-start = ((bf16[16,12,16,384]{3,2,1,0:T(8,128)(2,1)}), bf16[16,12,16,384]{3,2,1,0:T(8,128)(2,1)S(1)}, u32[]{:S(2)}, u32[]{:S(2)}) async-start(bf16[16,12,16,384]{3,2,1,0:T(8,128)(2,1)} %image_columns.1), calls=%async_computation | async-start | bytes 4718592 | tf_op jit(solution)/shard_map/all_to_all | solution.py:527
  16.8 2.2 reshape_squeeze.3
  19.0 0.0 copy-start.1
  19.1 2.3 copy.14
  21.3 2.6 reshape.29
  23.9 0.0 copy-done.1
  24.0 2.2 collective-permute-start
  26.1 36.3 %maps_columns.1 = bf16[16,12,5,16,384]{4,3,2,1,0:T(8,128)(2,1)} custom-call(bf16[8,2,12,192,256]{4,3,2,1,0:T(8,128)(2,1)} %x_ref.4), custom_call_target="tpu_custom_call" | custom-call | bytes 23592960 | tf_op jit(solution)/shard_map/maps_columns/pallas_call | solution.py:129
  62.4 30.7 %collective-permute-done = bf16[2320,128]{1,0:T(8,128)(2,1)S(1)} collective-permute-done((bf16[2320,128]{1,0:T(8,128)(2,1)S(1)}, bf16[2320,128]{1,0:T(8,128)(2,1)S(1)}, u32[]{:S(2)}, u32[]{:S(2)}) %collective-permute-start) | collective-permute-done | bytes 593952 | tf_op jit(solution)/shard_map/ppermute | solution.py:537
  93.1 0.0 all-to-all-done
  93.1 8.6 %all-to-all-start.1 = ((bf16[16,12,5,16,384]{4,3,2,1,0:T(8,128)(2,1)}), bf16[16,12,5,16,384]{4,3,2,1,0:T(8,128)(2,1)}, u32[]{:S(2)}, u32[]{:S(2)}) async-start(bf16[16,12,5,16,384]{4,3,2,1,0:T(8,128)(2,1)} %maps_columns.1), calls=%async_computation.1 | async-start | bytes 23592960 | tf_op jit(solution)/shard_map/all_to_all | solution.py:527
  101.8 0.0 all-gather.2.cloned.1.call-start
  101.8 1.1 pad_maximum_fusion
  102.9 0.0 all-gather.2.cloned.1.call-update
  103.0 24.1 %last_maps_columns.1 = (bf16[16,12,4,8,384]{4,3,2,1,0:T(8,128)(2,1)}, bf16[16,12,2,8,384]{4,3,2,1,0:T(8,128)(2,1)}) custom-call(bf16[8,2,12,192,256]{4,3,2,1,0:T(8,128)(2,1)} %x_ref.4), custom_call_target="tpu_custom_call" | custom-call | bytes 14155776 | tf_op jit(solution)/shard_map/last_maps_columns/pallas_call | solution.py:148
  127.0 0.5 fusion.10.owner.refs_1_
  127.6 140.4 %all-gather.2.cloned.1.call-done.w_hbm.refs_10_ = bf16[37120,128]{1,0:T(8,128)(2,1)} async-done(((bf16[4640,128]{1,0:T(8,128)(2,1)}), bf16[37120,128]{1,0:T(8,128)(2,1)}) %all-gather.2.cloned.1.call-update) | async-done | bytes 9502736 | tf_op jit(solution)/shard_map/all_gather | solution.py:544
  268.0 0.8 slice_convert_fusion
  268.8 0.7 reshape.31.links.refs_0_
  269.5 13.4 %warp.1.refs_1_.refs_3_ = f32[192,16,384]{2,1,0:T(8,128)} custom-call(s32[1152]{0:T(1024)} %reshape.31.links.refs_0_, s32[16]{0:T(128)} %fusion.10.owner.refs_1_, bf16[192,16,384]{2,1,0:T(8,128)(2,1)S(1)} %bitcast.36, bf16[37120,128]{1,0:T(8,128)(2,1)} %all-gather.2.cloned.1.call-done.w_hbm.refs_10_), custom_call_target="tpu_custom_call" | custom-call | flops 2415919104 | bytes 20971520 | tf_op jit(solution)/shard_map/warp/pallas_call | solution.py:237
  282.9 75.4 %all-to-all-done.1 = bf16[16,12,5,16,384]{4,3,2,1,0:T(8,128)(2,1)} async-done(((bf16[16,12,5,16,384]{4,3,2,1,0:T(8,128)(2,1)}), bf16[16,12,5,16,384]{4,3,2,1,0:T(8,128)(2,1)}, u32[]{:S(2)}, u32[]{:S(2)}) %all-to-all-start.1) | async-done | bytes 11796512 | tf_op jit(solution)/shard_map/all_to_all | solution.py:527
  358.4 0.0 copy-start
  358.4 4.6 all-to-all-start.2
  363.0 0.0 copy-done
  363.0 0.8 pad_maximum_fusion.2.refs_2_.refs_4_
  363.8 69.4 %coils.4.refs_7_.refs_9_ = f32[192,16,384]{2,1,0:T(8,128)} custom-call(bf16[192,5,16,384]{3,2,1,0:T(8,128)(2,1)} %bitcast.6.refs_0_, f32[192,16,384]{2,1,0:T(8,128)} %warp.1.refs_1_.refs_3_, f32[384,256]{1,0:T(8,128)} %pad_maximum_fusion.2.refs_2_.refs_4_, bf16[384,512]{1,0:T(8,128)(2,1)} %constant.87.clone.refs_3_.refs_5_, ...), custom_call_target="tpu_custom_call" | custom-call | flops 36238786560 | bytes 26476544 | tf_op jit(solution)/shard_map/coils/pallas_call | solution.py:463
  433.2 33.1 %all-to-all-done.2 = bf16[16,12,4,8,384]{4,3,2,1,0:T(8,128)(2,1)} async-done(((bf16[16,12,4,8,384]{4,3,2,1,0:T(8,128)(2,1)}), bf16[16,12,4,8,384]{4,3,2,1,0:T(8,128)(2,1)}, u32[]{:S(2)}, u32[]{:S(2)}) %all-to-all-start.2) | async-done | bytes 4718624 | tf_op jit(solution)/shard_map/all_to_all | solution.py:527
  466.3 4.9 all-to-all-start.3
  471.2 9.4 %coils.5.refs_9_ = f32[192,8,384]{2,1,0:T(8,128)} custom-call(bf16[192,4,8,384]{3,2,1,0:T(8,128)(2,1)} %bitcast.9.refs_0_.refs_2_, f32[192,16,384]{2,1,0:T(8,128)} %warp.1.refs_1_.refs_3_, f32[384,256]{1,0:T(8,128)} %pad_maximum_fusion.2.refs_2_.refs_4_, bf16[384,512]{1,0:T(8,128)(2,1)} %constant.87.clone.refs_3_.refs_5_, ...), custom_call_target="tpu_custom_call" | custom-call | flops 3623878656 | bytes 15859712 | tf_op jit(solution)/shard_map/coils/pallas_call | solution.py:463
  480.6 32.8 %coils.7 = bf16[192,8,384]{2,1,0:T(8,128)(2,1)} custom-call(s32[1152]{0:T(1024)} %reshape.31.links.refs_0_, s32[16]{0:T(128)} %fusion.10.owner.refs_1_, bf16[192,4,8,384]{3,2,1,0:T(8,128)(2,1)} %bitcast.9.refs_0_.refs_2_, f32[192,16,384]{2,1,0:T(8,128)} %warp.1.refs_1_.refs_3_, f32[384,256]{1,0:T(8,128)} %pad_maximum_fusion.2.refs_2_.refs_4_, ...), custom_call_target="tpu_custom_call" | custom-call | flops 10871635968 | bytes 18219008 | tf_op jit(solution)/shard_map/coils/pallas_call | solution.py:463
  513.4 10.8 %all-to-all-done.3 = bf16[16,12,2,8,384]{4,3,2,1,0:T(8,128)(2,1)S(1)} async-done(((bf16[16,12,2,8,384]{4,3,2,1,0:T(8,128)(2,1)}), bf16[16,12,2,8,384]{4,3,2,1,0:T(8,128)(2,1)S(1)}, u32[]{:S(2)}, u32[]{:S(2)}) %all-to-all-start.3) | async-done | bytes 2359328 | tf_op jit(solution)/shard_map/all_to_all | solution.py:527
  524.2 4.9 all-to-all-start.4
  529.1 26.8 %coils.6 = bf16[192,8,384]{2,1,0:T(8,128)(2,1)} custom-call(s32[1152]{0:T(1024)} %reshape.31.links.refs_0_, s32[16]{0:T(128)} %fusion.10.owner.refs_1_, bf16[192,2,8,384]{3,2,1,0:T(8,128)(2,1)S(1)} %bitcast.37, f32[192,16,384]{2,1,0:T(8,128)} %warp.1.refs_1_.refs_3_, f32[384,256]{1,0:T(8,128)} %pad_maximum_fusion.2.refs_2_.refs_4_, ...), custom_call_target="tpu_custom_call" | custom-call | flops 7247757312 | bytes 17039360 | tf_op jit(solution)/shard_map/coils/pallas_call | solution.py:463
  555.9 1.0 all-to-all-done.4.b_ref
  556.9 5.1 all-to-all-start.5
  562.0 3.3 update.2.refs_0_
  565.2 24.5 %all-to-all-done.5.b_ref = bf16[16,12,8,384]{3,2,1,0:T(8,128)(2,1)S(1)} async-done(((bf16[16,12,8,384]{3,2,1,0:T(8,128)(2,1)}), bf16[16,12,8,384]{3,2,1,0:T(8,128)(2,1)S(1)}, u32[]{:S(2)}, u32[]{:S(2)}) %all-to-all-start.5) | async-done | bytes 1179680 | tf_op jit(solution)/shard_map/all_to_all | solution.py:527
  589.7 3.3 update.3
  (6 shorter events, 0.1 us)
Async XLA Ops:
  10.3 82.9 %all-to-all-start = ((bf16[16,12,16,384]{3,2,1,0:T(8,128)(2,1)}), bf16[16,12,16,384]{3,2,1,0:T(8,128)(2,1)S(1)}, u32[]{:S(2)}, u32[]{:S(2)}) async-start(bf16[16,12,16,384]{3,2,1,0:T(8,128)(2,1)} %image_columns.1), calls=%async_computation | async-start | bytes 4718592 | tf_op jit(solution)/shard_map/all_to_all | solution.py:527
  19.0 4.8 copy-start.1
  24.0 69.1 %collective-permute-start = (bf16[2320,128]{1,0:T(8,128)(2,1)S(1)}, bf16[2320,128]{1,0:T(8,128)(2,1)S(1)}, u32[]{:S(2)}, u32[]{:S(2)}) collective-permute-start(bf16[2320,128]{1,0:T(8,128)(2,1)S(1)} %pad_maximum_fusion.1), channel_id=1, source_target_pairs={{0,8},{1,9},{2,10},{3,11},{4,12},{5,13},{6,14},{7,15},{8,0},{9,1},... | collective-permute-start | bytes 1781768 | tf_op jit(solution)/shard_map/ppermute | solution.py:537
  93.1 265.2 %all-to-all-start.1 = ((bf16[16,12,5,16,384]{4,3,2,1,0:T(8,128)(2,1)}), bf16[16,12,5,16,384]{4,3,2,1,0:T(8,128)(2,1)}, u32[]{:S(2)}, u32[]{:S(2)}) async-start(bf16[16,12,5,16,384]{4,3,2,1,0:T(8,128)(2,1)} %maps_columns.1), calls=%async_computation.1 | async-start | bytes 23592960 | tf_op jit(solution)/shard_map/all_to_all | solution.py:527
  101.8 166.3 %all-gather.2.cloned.1.call-start = ((), (), s32[]{:S(2)}) async-start(), calls=%async_computation.6 | async-start | bytes 10690560 | tf_op jit(solution)/shard_map/all_gather | solution.py:544
  358.4 4.6 copy-start
  358.4 107.9 %all-to-all-start.2 = ((bf16[16,12,4,8,384]{4,3,2,1,0:T(8,128)(2,1)}), bf16[16,12,4,8,384]{4,3,2,1,0:T(8,128)(2,1)}, u32[]{:S(2)}, u32[]{:S(2)}) async-start(bf16[16,12,4,8,384]{4,3,2,1,0:T(8,128)(2,1)} %get-tuple-element.15), calls=%async_computation.2 | async-start | bytes 9437184 | tf_op jit(solution)/shard_map/all_to_all | solution.py:527
  466.3 57.9 %all-to-all-start.3 = ((bf16[16,12,2,8,384]{4,3,2,1,0:T(8,128)(2,1)}), bf16[16,12,2,8,384]{4,3,2,1,0:T(8,128)(2,1)S(1)}, u32[]{:S(2)}, u32[]{:S(2)}) async-start(bf16[16,12,2,8,384]{4,3,2,1,0:T(8,128)(2,1)} %get-tuple-element.16), calls=%async_computation.3 | async-start | bytes 4718592 | tf_op jit(solution)/shard_map/all_to_all | solution.py:527
  524.2 32.7 %all-to-all-start.4 = ((bf16[16,12,8,384]{3,2,1,0:T(8,128)(2,1)}), bf16[16,12,8,384]{3,2,1,0:T(8,128)(2,1)S(1)}, u32[]{:S(2)}, u32[]{:S(2)}) async-start(bf16[16,12,8,384]{3,2,1,0:T(8,128)(2,1)} %bitcast.40), calls=%async_computation.4 | async-start | bytes 2359296 | tf_op jit(solution)/shard_map/all_to_all | solution.py:527
  556.9 32.8 %all-to-all-start.5 = ((bf16[16,12,8,384]{3,2,1,0:T(8,128)(2,1)}), bf16[16,12,8,384]{3,2,1,0:T(8,128)(2,1)S(1)}, u32[]{:S(2)}, u32[]{:S(2)}) async-start(bf16[16,12,8,384]{3,2,1,0:T(8,128)(2,1)} %bitcast.41), calls=%async_computation.5 | async-start | bytes 2359296 | tf_op jit(solution)/shard_map/all_to_all | solution.py:527
Sparse Core Ops, SparseCore 0:
  104.2 163.7 all-gather.1

commit v11 on v10

--- a/solution.py
+++ b/solution.py
@@ -531,20 +531,15 @@
     return lax.optimization_barrier((value, *others))[0]
 
 
-def swap_halves(value):
+def gather_all(value):
     count = lax.axis_size("slab")
     half = count // 2
-    return lax.ppermute(value, "slab", [(i, i ^ half) for i in range(count)])
-
-
-def gather_half(pair):
-    count = lax.axis_size("slab")
-    half = count // 2
-    groups = [list(range(half)), list(range(half, count))]
-    gathered = lax.all_gather(pair, "slab", axis=0, tiled=True, axis_index_groups=groups)
-    mine = lax.axis_index("slab") // half
+    pairs = [[i, i + half] for i in range(half)]
+    halves = [list(range(half)), list(range(half, count))]
+    for groups in (pairs, halves):
+        value = lax.all_gather(value, "slab", axis=0, tiled=True, axis_index_groups=groups)
     place = jnp.arange(count, dtype=jnp.int32)
-    return gathered, place // 2 + half * ((place % 2) ^ mine)
+    return value, place // 2 + half * (place % 2)
 
 
 def per_device(image, adjoint_data, coil_maps, masks, sources, weights):
@@ -564,8 +559,7 @@
     digits = jnp.concatenate([chosen // BLK, chosen % BLK], axis=0).astype(BF)
     digits = jnp.pad(digits, ((0, TAIL - 4), (0, 2 * BLK - targets)))
     own = jnp.concatenate([matrices, digits], axis=0)
-    crossed = swap_halves(own)
-    packed, owner = gather_half(jnp.concatenate([own, crossed], axis=0))
+    packed, owner = gather_all(own)
     digits = packed.reshape(count, targets * BLK + TAIL, 2 * BLK)[:, targets * BLK :]
     digits = digits[:, :4, :targets].astype(jnp.int32)
     links = (digits[:, :2] * BLK + digits[:, 2:]).reshape(-1)
@@ -584,7 +578,7 @@
     early = total - 3 * total // 8 if halves else total - 1
     late = total - early
     maps = maps_columns(coil_maps, count, 0, early)
-    arrived = exchange(after(maps, columns, crossed))
+    arrived = exchange(after(maps, columns))
     if not halves:
         maps = maps_columns(coil_maps, count, early, late)
         last = exchange(after(maps, arrived, warped))
@@ -593,7 +587,7 @@
         return update(back(grad), image, adjoint_data, 0, None)
 
     first, second = last_maps_columns(coil_maps, count, early, late)
-    first = exchange(after(first, arrived, warped))
+    first = exchange(after(first, arrived))
     combined = run(arrived, 0, early, None, 0)
     second = exchange(after(second, first, combined))
     grad = run(first, 0, late, combined, 0, warping=warping)

time: 602 us -> 601 us (level)
    all_to_all x6, waiting for transfers between devices: 145 us -> 210 us  [exchange(): lax.all_to_all(parts, 'slab', split_axis=0, concat_axis=0, tiled=True)]
    ppermute x1 -> x0, waiting for transfers between devices: 30.7 us -> none  [swap_halves(): return lax.ppermute(value, 'slab', [(i, i ^ half) for i in range(count)])]
    all_gather x1 -> x2, waiting for transfers between devices: 140 us -> 110 us  [gather_all(): lax.all_gather(value, 'slab', axis=0, tiled=True, axis_index_groups=groups)]
where the time goes in v11:
time: 601 us; the launch traced here: 599 us
  waiting for transfers between devices  320 us (53%)
  Pallas kernels  222 us (37%)
  starting transfers between devices  32.6 us (5%)
  between operations  13.5 us (2%)
  local copies, waits for them, and re-layouts  6.9 us (1%)
    all_to_all x6, waiting for transfers between devices, exchange(): lax.all_to_all(parts, 'slab', split_axis=0, concat_axis=0, tiled=True)  210 us
    pallas_call x4, Pallas kernels, coils(): pl.pallas_call(functools.partial(coil_kernel, nx, deep, pad, skip, ends,...  138 us
    all_gather x2, waiting for transfers between devices, gather_all(): lax.all_gather(value, 'slab', axis=0, tiled=True, axis_index_groups=groups)  110 us
    pallas_call x1, Pallas kernels, maps_columns(): pl.pallas_call(functools.partial(maps_kernel, count, deep), out_shape=jax...  36.5 us
    all_to_all x6, starting transfers between devices, exchange(): lax.all_to_all(parts, 'slab', split_axis=0, concat_axis=0, tiled=True)  32.5 us
    pallas_call x1, Pallas kernels, last_maps_columns(): pl.pallas_call(functools.partial(last_maps_kernel, count, deep, coils), o...  24.1 us
    pallas_call x1, Pallas kernels, warp(): pl.pallas_call(functools.partial(warp_kernel, nx, deep, pad), out_shape=j...  13.4 us
  transfers between devices with their start and end apart: 8, of which 7 were waited for; matrix products, arithmetic and copies ran while one was open for 2% of the time, Pallas kernels for 36%

profile of v11, /device:TPU:13, one launch (start us, length us, event | category | flops | bytes accessed | tf_op | source)
XLA Modules:
  0.0 599.1 jit_solution(8776779116263446094)
XLA Ops:
  6.5 3.7 image_columns.1
  10.3 6.6 %all-to-all-start = ((bf16[16,12,16,384]{3,2,1,0:T(8,128)(2,1)}), bf16[16,12,16,384]{3,2,1,0:T(8,128)(2,1)S(1)}, u32[]{:S(2)}, u32[]{:S(2)}) async-start(bf16[16,12,16,384]{3,2,1,0:T(8,128)(2,1)} %image_columns.1), calls=%async_computation | async-start | bytes 4718592 | tf_op jit(solution)/shard_map/all_to_all | solution.py:527
  16.8 36.5 %maps_columns.1 = bf16[16,12,5,16,384]{4,3,2,1,0:T(8,128)(2,1)} custom-call(bf16[8,2,12,192,256]{4,3,2,1,0:T(8,128)(2,1)} %x_ref.4), custom_call_target="tpu_custom_call" | custom-call | bytes 23592960 | tf_op jit(solution)/shard_map/maps_columns/pallas_call | solution.py:129
  53.3 0.0 copy-start
  53.3 16.6 %all-to-all-done = bf16[16,12,16,384]{3,2,1,0:T(8,128)(2,1)S(1)} async-done(((bf16[16,12,16,384]{3,2,1,0:T(8,128)(2,1)}), bf16[16,12,16,384]{3,2,1,0:T(8,128)(2,1)S(1)}, u32[]{:S(2)}, u32[]{:S(2)}) %all-to-all-start) | async-done | bytes 2359328 | tf_op jit(solution)/shard_map/all_to_all | solution.py:527
  69.9 4.9 all-to-all-start.1
  74.8 0.0 all-gather.3.cloned.1.call-start
  74.8 0.0 copy-done
  74.8 2.3 reshape_squeeze.3
  77.1 0.0 copy-start.2
  77.1 2.5 copy.14
  79.6 1.4 reshape.29
  81.0 0.0 copy-done.2
  81.0 1.9 pad_maximum_fusion
  83.0 0.0 all-gather.3.cloned.1.call-update
  83.0 0.0 all-gather.5.cloned.1.call-start
  83.0 110.0 %all-gather.3.cloned.1.call-done = bf16[4640,128]{1,0:T(8,128)(2,1)} async-done(((bf16[2320,128]{1,0:T(8,128)(2,1)}), bf16[4640,128]{1,0:T(8,128)(2,1)}) %all-gather.3.cloned.1.call-update) | async-done | bytes 1187856 | tf_op jit(solution)/shard_map/all_gather | solution.py:540
  193.0 0.0 all-gather.5.cloned.1.call-update
  193.0 24.1 %last_maps_columns.1 = (bf16[16,12,4,8,384]{4,3,2,1,0:T(8,128)(2,1)}, bf16[16,12,2,8,384]{4,3,2,1,0:T(8,128)(2,1)}) custom-call(bf16[8,2,12,192,256]{4,3,2,1,0:T(8,128)(2,1)} %x_ref.4), custom_call_target="tpu_custom_call" | custom-call | bytes 14155776 | tf_op jit(solution)/shard_map/last_maps_columns/pallas_call | solution.py:148
  217.2 138.4 %all-to-all-done.1 = bf16[16,12,5,16,384]{4,3,2,1,0:T(8,128)(2,1)} async-done(((bf16[16,12,5,16,384]{4,3,2,1,0:T(8,128)(2,1)}), bf16[16,12,5,16,384]{4,3,2,1,0:T(8,128)(2,1)}, u32[]{:S(2)}, u32[]{:S(2)}) %all-to-all-start.1) | async-done | bytes 11796512 | tf_op jit(solution)/shard_map/all_to_all | solution.py:527
  355.6 0.0 copy-start.1
  355.6 6.2 %all-to-all-start.2 = ((bf16[16,12,4,8,384]{4,3,2,1,0:T(8,128)(2,1)}), bf16[16,12,4,8,384]{4,3,2,1,0:T(8,128)(2,1)}, u32[]{:S(2)}, u32[]{:S(2)}) async-start(bf16[16,12,4,8,384]{4,3,2,1,0:T(8,128)(2,1)} %get-tuple-element.15), calls=%async_computation.2 | async-start | bytes 9437184 | tf_op jit(solution)/shard_map/all_to_all | solution.py:527
  361.8 0.0 copy-done.1
  361.9 0.5 fusion.9.owner.refs_1_
  362.4 0.8 pad_maximum_fusion.1.refs_2_.refs_4_
  363.2 0.0 all-gather.5.cloned.1.call-done.w_hbm.refs_10_
  363.2 0.8 slice_convert_fusion
  364.0 0.7 reshape.31.links.refs_0_
  364.7 13.4 %warp.1.refs_1_.refs_3_ = f32[192,16,384]{2,1,0:T(8,128)} custom-call(s32[1152]{0:T(1024)} %reshape.31.links.refs_0_, s32[16]{0:T(128)} %fusion.9.owner.refs_1_, bf16[192,16,384]{2,1,0:T(8,128)(2,1)S(1)} %bitcast.36, bf16[37120,128]{1,0:T(8,128)(2,1)} %all-gather.5.cloned.1.call-done.w_hbm.refs_10_), custom_call_target="tpu_custom_call" | custom-call | flops 2415919104 | bytes 20971520 | tf_op jit(solution)/shard_map/warp/pallas_call | solution.py:237
  378.0 69.2 %coils.4.refs_7_.refs_9_ = f32[192,16,384]{2,1,0:T(8,128)} custom-call(bf16[192,5,16,384]{3,2,1,0:T(8,128)(2,1)} %bitcast.5.refs_0_, f32[192,16,384]{2,1,0:T(8,128)} %warp.1.refs_1_.refs_3_, f32[384,256]{1,0:T(8,128)} %pad_maximum_fusion.1.refs_2_.refs_4_, bf16[384,512]{1,0:T(8,128)(2,1)} %constant.70.clone.refs_3_.refs_5_, ...), custom_call_target="tpu_custom_call" | custom-call | flops 36238786560 | bytes 26476544 | tf_op jit(solution)/shard_map/coils/pallas_call | solution.py:463
  447.2 18.3 %all-to-all-done.2 = bf16[16,12,4,8,384]{4,3,2,1,0:T(8,128)(2,1)} async-done(((bf16[16,12,4,8,384]{4,3,2,1,0:T(8,128)(2,1)}), bf16[16,12,4,8,384]{4,3,2,1,0:T(8,128)(2,1)}, u32[]{:S(2)}, u32[]{:S(2)}) %all-to-all-start.2) | async-done | bytes 4718624 | tf_op jit(solution)/shard_map/all_to_all | solution.py:527
  465.5 4.9 all-to-all-start.3
  470.4 9.4 %coils.5.refs_9_ = f32[192,8,384]{2,1,0:T(8,128)} custom-call(bf16[192,4,8,384]{3,2,1,0:T(8,128)(2,1)} %bitcast.9.refs_0_.refs_2_, f32[192,16,384]{2,1,0:T(8,128)} %warp.1.refs_1_.refs_3_, f32[384,256]{1,0:T(8,128)} %pad_maximum_fusion.1.refs_2_.refs_4_, bf16[384,512]{1,0:T(8,128)(2,1)} %constant.70.clone.refs_3_.refs_5_, ...), custom_call_target="tpu_custom_call" | custom-call | flops 3623878656 | bytes 15859712 | tf_op jit(solution)/shard_map/coils/pallas_call | solution.py:463
  479.8 32.7 %coils.7 = bf16[192,8,384]{2,1,0:T(8,128)(2,1)} custom-call(s32[1152]{0:T(1024)} %reshape.31.links.refs_0_, s32[16]{0:T(128)} %fusion.9.owner.refs_1_, bf16[192,4,8,384]{3,2,1,0:T(8,128)(2,1)} %bitcast.9.refs_0_.refs_2_, f32[192,16,384]{2,1,0:T(8,128)} %warp.1.refs_1_.refs_3_, f32[384,256]{1,0:T(8,128)} %pad_maximum_fusion.1.refs_2_.refs_4_, ...), custom_call_target="tpu_custom_call" | custom-call | flops 10871635968 | bytes 18219008 | tf_op jit(solution)/shard_map/coils/pallas_call | solution.py:463
  512.5 11.0 %all-to-all-done.3 = bf16[16,12,2,8,384]{4,3,2,1,0:T(8,128)(2,1)S(1)} async-done(((bf16[16,12,2,8,384]{4,3,2,1,0:T(8,128)(2,1)}), bf16[16,12,2,8,384]{4,3,2,1,0:T(8,128)(2,1)S(1)}, u32[]{:S(2)}, u32[]{:S(2)}) %all-to-all-start.3) | async-done | bytes 2359328 | tf_op jit(solution)/shard_map/all_to_all | solution.py:527
  523.5 4.9 all-to-all-start.4
  528.4 26.8 %coils.6 = bf16[192,8,384]{2,1,0:T(8,128)(2,1)} custom-call(s32[1152]{0:T(1024)} %reshape.31.links.refs_0_, s32[16]{0:T(128)} %fusion.9.owner.refs_1_, bf16[192,2,8,384]{3,2,1,0:T(8,128)(2,1)S(1)} %bitcast.37, f32[192,16,384]{2,1,0:T(8,128)} %warp.1.refs_1_.refs_3_, f32[384,256]{1,0:T(8,128)} %pad_maximum_fusion.1.refs_2_.refs_4_, ...), custom_call_target="tpu_custom_call" | custom-call | flops 7247757312 | bytes 17039360 | tf_op jit(solution)/shard_map/coils/pallas_call | solution.py:463
  555.2 1.0 all-to-all-done.4.b_ref
  556.1 5.1 all-to-all-start.5
  561.2 3.3 update.2.refs_0_
  564.5 24.5 %all-to-all-done.5.b_ref = bf16[16,12,8,384]{3,2,1,0:T(8,128)(2,1)S(1)} async-done(((bf16[16,12,8,384]{3,2,1,0:T(8,128)(2,1)}), bf16[16,12,8,384]{3,2,1,0:T(8,128)(2,1)S(1)}, u32[]{:S(2)}, u32[]{:S(2)}) %all-to-all-start.5) | async-done | bytes 1179680 | tf_op jit(solution)/shard_map/all_to_all | solution.py:527
  589.0 3.3 update.3
  (5 shorter events, 0.1 us)
Async XLA Ops:
  10.3 59.6 %all-to-all-start = ((bf16[16,12,16,384]{3,2,1,0:T(8,128)(2,1)}), bf16[16,12,16,384]{3,2,1,0:T(8,128)(2,1)S(1)}, u32[]{:S(2)}, u32[]{:S(2)}) async-start(bf16[16,12,16,384]{3,2,1,0:T(8,128)(2,1)} %image_columns.1), calls=%async_computation | async-start | bytes 4718592 | tf_op jit(solution)/shard_map/all_to_all | solution.py:527
  53.3 21.5 %copy-start = (bf16[1,36,8192]{2,1,0:T(8,128)(2,1)S(1)}, bf16[1,36,8192]{2,1,0:T(8,128)(2,1)}, u32[]{:S(2)}) copy-start(bf16[1,36,8192]{2,1,0:T(8,128)(2,1)} %param.15) | copy-start | bytes 1769476
  69.9 285.7 %all-to-all-start.1 = ((bf16[16,12,5,16,384]{4,3,2,1,0:T(8,128)(2,1)}), bf16[16,12,5,16,384]{4,3,2,1,0:T(8,128)(2,1)}, u32[]{:S(2)}, u32[]{:S(2)}) async-start(bf16[16,12,5,16,384]{4,3,2,1,0:T(8,128)(2,1)} %maps_columns.1), calls=%async_computation.1 | async-start | bytes 23592960 | tf_op jit(solution)/shard_map/all_to_all | solution.py:527
  74.8 118.2 %all-gather.3.cloned.1.call-start = ((), (), s32[]{:S(2)}) async-start(), calls=%async_computation.6 | async-start | bytes 1781760 | tf_op jit(solution)/shard_map/all_gather | solution.py:540
  77.1 3.9 copy-start.2
  83.0 280.2 %all-gather.5.cloned.1.call-start = ((), (), s32[]{:S(2)}) async-start(), calls=%async_computation.7 | async-start | bytes 10690560 | tf_op jit(solution)/shard_map/all_gather | solution.py:540
  355.6 6.2 %copy-start.1 = (s32[1,192,192]{2,1,0:T(8,128)S(1)}, s32[1,192,192]{2,1,0:T(8,128)}, u32[]{:S(2)}) copy-start(s32[1,192,192]{2,1,0:T(8,128)} %param.13) | copy-start | bytes 442372
  355.6 109.9 %all-to-all-start.2 = ((bf16[16,12,4,8,384]{4,3,2,1,0:T(8,128)(2,1)}), bf16[16,12,4,8,384]{4,3,2,1,0:T(8,128)(2,1)}, u32[]{:S(2)}, u32[]{:S(2)}) async-start(bf16[16,12,4,8,384]{4,3,2,1,0:T(8,128)(2,1)} %get-tuple-element.15), calls=%async_computation.2 | async-start | bytes 9437184 | tf_op jit(solution)/shard_map/all_to_all | solution.py:527
  465.5 57.9 %all-to-all-start.3 = ((bf16[16,12,2,8,384]{4,3,2,1,0:T(8,128)(2,1)}), bf16[16,12,2,8,384]{4,3,2,1,0:T(8,128)(2,1)S(1)}, u32[]{:S(2)}, u32[]{:S(2)}) async-start(bf16[16,12,2,8,384]{4,3,2,1,0:T(8,128)(2,1)} %get-tuple-element.16), calls=%async_computation.3 | async-start | bytes 4718592 | tf_op jit(solution)/shard_map/all_to_all | solution.py:527
  523.5 32.7 %all-to-all-start.4 = ((bf16[16,12,8,384]{3,2,1,0:T(8,128)(2,1)}), bf16[16,12,8,384]{3,2,1,0:T(8,128)(2,1)S(1)}, u32[]{:S(2)}, u32[]{:S(2)}) async-start(bf16[16,12,8,384]{3,2,1,0:T(8,128)(2,1)} %bitcast.40), calls=%async_computation.4 | async-start | bytes 2359296 | tf_op jit(solution)/shard_map/all_to_all | solution.py:527
  556.1 32.8 %all-to-all-start.5 = ((bf16[16,12,8,384]{3,2,1,0:T(8,128)(2,1)}), bf16[16,12,8,384]{3,2,1,0:T(8,128)(2,1)S(1)}, u32[]{:S(2)}, u32[]{:S(2)}) async-start(bf16[16,12,8,384]{3,2,1,0:T(8,128)(2,1)} %bitcast.41), calls=%async_computation.5 | async-start | bytes 2359296 | tf_op jit(solution)/shard_map/all_to_all | solution.py:527
Sparse Core Ops, SparseCore 0:
  83.1 109.8 all-gather.2
  194.7 103.8 all-gather.4

commit v12 on v10

--- a/solution.py
+++ b/solution.py
@@ -353,7 +353,7 @@
         cube[2, at, pl.ds(0, deep), :] = real * w2 + imag * jnp.where(low, -other, other)
         return carry
 
-    lax.fori_loop(0, nx // group, expand, 0, unroll=4)
+    lax.fori_loop(0, nx // group, expand, 0, unroll=8)
 
     batch = 4 if deep % 4 == 0 else 1
 
@@ -412,7 +412,7 @@
             o_ref[at, :, lanes] = old + terms[v]
         return carry
 
-    lax.fori_loop(0, nx // group, combine, 0, unroll=4)
+    lax.fori_loop(0, nx // group, combine, 0, unroll=8)
     if ends:
 
         @pl.when(pl.program_id(0) == pl.num_programs(0) - 1)

time: 602 us -> 602 us (level)
  transfers between devices with their start and end apart: 8 -> 8, of which waited for: 7 -> 7; matrix products, arithmetic and copies ran while one was open for 2% -> 2% of each run, Pallas kernels for 36% -> 35%
where the time goes in v12:
time: 602 us; the launch traced here: 600 us
  waiting for transfers between devices  319 us (53%)
  Pallas kernels  220 us (37%)
  starting transfers between devices  36.6 us (6%)
  between operations  13.5 us (2%)
  local copies, waits for them, and re-layouts  7.74 us (1%)
    all_to_all x6, waiting for transfers between devices, exchange(): lax.all_to_all(parts, 'slab', split_axis=0, concat_axis=0, tiled=True)  147 us
    all_gather x1, waiting for transfers between devices, gather_half(): lax.all_gather(pair, 'slab', axis=0, tiled=True, axis_index_groups=groups)  140 us
    pallas_call x4, Pallas kernels, coils(): pl.pallas_call(functools.partial(coil_kernel, nx, deep, pad, skip, ends,...  136 us
    pallas_call x1, Pallas kernels, maps_columns(): pl.pallas_call(functools.partial(maps_kernel, count, deep), out_shape=jax...  36.3 us
    all_to_all x6, starting transfers between devices, exchange(): lax.all_to_all(parts, 'slab', split_axis=0, concat_axis=0, tiled=True)  34.5 us
    ppermute x1, waiting for transfers between devices, swap_halves(): return lax.ppermute(value, 'slab', [(i, i ^ half) for i in range(count)])  30.7 us
    pallas_call x1, Pallas kernels, last_maps_columns(): pl.pallas_call(functools.partial(last_maps_kernel, count, deep, coils), o...  24.1 us
    pallas_call x1, Pallas kernels, warp(): pl.pallas_call(functools.partial(warp_kernel, nx, deep, pad), out_shape=j...  13.4 us
  transfers between devices with their start and end apart: 8, of which 7 were waited for; matrix products, arithmetic and copies ran while one was open for 2% of the time, Pallas kernels for 35%

profile of v12, /device:TPU:13, one launch (start us, length us, event | category | flops | bytes accessed | tf_op | source)
XLA Modules:
  0.0 599.6 jit_solution(3688688630159156903)
XLA Ops:
  6.5 3.7 image_columns.1
  10.3 6.6 %all-to-all-start = ((bf16[16,12,16,384]{3,2,1,0:T(8,128)(2,1)}), bf16[16,12,16,384]{3,2,1,0:T(8,128)(2,1)S(1)}, u32[]{:S(2)}, u32[]{:S(2)}) async-start(bf16[16,12,16,384]{3,2,1,0:T(8,128)(2,1)} %image_columns.1), calls=%async_computation | async-start | bytes 4718592 | tf_op jit(solution)/shard_map/all_to_all | solution.py:527
  16.8 2.2 reshape_squeeze.3
  19.0 0.0 copy-start.1
  19.1 2.3 copy.14
  21.3 2.6 reshape.29
  23.9 0.0 copy-done.1
  24.0 2.2 collective-permute-start
  26.1 36.3 %maps_columns.1 = bf16[16,12,5,16,384]{4,3,2,1,0:T(8,128)(2,1)} custom-call(bf16[8,2,12,192,256]{4,3,2,1,0:T(8,128)(2,1)} %x_ref.4), custom_call_target="tpu_custom_call" | custom-call | bytes 23592960 | tf_op jit(solution)/shard_map/maps_columns/pallas_call | solution.py:129
  62.4 30.7 %collective-permute-done = bf16[2320,128]{1,0:T(8,128)(2,1)S(1)} collective-permute-done((bf16[2320,128]{1,0:T(8,128)(2,1)S(1)}, bf16[2320,128]{1,0:T(8,128)(2,1)S(1)}, u32[]{:S(2)}, u32[]{:S(2)}) %collective-permute-start) | collective-permute-done | bytes 593952 | tf_op jit(solution)/shard_map/ppermute | solution.py:537
  93.1 0.0 all-to-all-done
  93.1 8.6 %all-to-all-start.1 = ((bf16[16,12,5,16,384]{4,3,2,1,0:T(8,128)(2,1)}), bf16[16,12,5,16,384]{4,3,2,1,0:T(8,128)(2,1)}, u32[]{:S(2)}, u32[]{:S(2)}) async-start(bf16[16,12,5,16,384]{4,3,2,1,0:T(8,128)(2,1)} %maps_columns.1), calls=%async_computation.1 | async-start | bytes 23592960 | tf_op jit(solution)/shard_map/all_to_all | solution.py:527
  101.8 0.0 all-gather.2.cloned.1.call-start
  101.8 1.1 pad_maximum_fusion
  102.9 0.0 all-gather.2.cloned.1.call-update
  103.0 24.1 %last_maps_columns.1 = (bf16[16,12,4,8,384]{4,3,2,1,0:T(8,128)(2,1)}, bf16[16,12,2,8,384]{4,3,2,1,0:T(8,128)(2,1)}) custom-call(bf16[8,2,12,192,256]{4,3,2,1,0:T(8,128)(2,1)} %x_ref.4), custom_call_target="tpu_custom_call" | custom-call | bytes 14155776 | tf_op jit(solution)/shard_map/last_maps_columns/pallas_call | solution.py:148
  127.0 0.5 fusion.10.owner.refs_1_
  127.6 140.4 %all-gather.2.cloned.1.call-done.w_hbm.refs_10_ = bf16[37120,128]{1,0:T(8,128)(2,1)} async-done(((bf16[4640,128]{1,0:T(8,128)(2,1)}), bf16[37120,128]{1,0:T(8,128)(2,1)}) %all-gather.2.cloned.1.call-update) | async-done | bytes 9502736 | tf_op jit(solution)/shard_map/all_gather | solution.py:544
  268.0 0.8 slice_convert_fusion
  268.8 0.7 reshape.31.links.refs_0_
  269.5 13.4 %warp.1.refs_1_.refs_3_ = f32[192,16,384]{2,1,0:T(8,128)} custom-call(s32[1152]{0:T(1024)} %reshape.31.links.refs_0_, s32[16]{0:T(128)} %fusion.10.owner.refs_1_, bf16[192,16,384]{2,1,0:T(8,128)(2,1)S(1)} %bitcast.36, bf16[37120,128]{1,0:T(8,128)(2,1)} %all-gather.2.cloned.1.call-done.w_hbm.refs_10_), custom_call_target="tpu_custom_call" | custom-call | flops 2415919104 | bytes 20971520 | tf_op jit(solution)/shard_map/warp/pallas_call | solution.py:237
  282.9 75.4 %all-to-all-done.1 = bf16[16,12,5,16,384]{4,3,2,1,0:T(8,128)(2,1)} async-done(((bf16[16,12,5,16,384]{4,3,2,1,0:T(8,128)(2,1)}), bf16[16,12,5,16,384]{4,3,2,1,0:T(8,128)(2,1)}, u32[]{:S(2)}, u32[]{:S(2)}) %all-to-all-start.1) | async-done | bytes 11796512 | tf_op jit(solution)/shard_map/all_to_all | solution.py:527
  358.4 0.0 copy-start
  358.4 4.6 all-to-all-start.2
  363.0 0.0 copy-done
  363.0 0.8 pad_maximum_fusion.2.refs_2_.refs_4_
  363.8 67.9 %coils.4.refs_7_.refs_9_ = f32[192,16,384]{2,1,0:T(8,128)} custom-call(bf16[192,5,16,384]{3,2,1,0:T(8,128)(2,1)} %bitcast.6.refs_0_, f32[192,16,384]{2,1,0:T(8,128)} %warp.1.refs_1_.refs_3_, f32[384,256]{1,0:T(8,128)} %pad_maximum_fusion.2.refs_2_.refs_4_, bf16[384,512]{1,0:T(8,128)(2,1)} %constant.87.clone.refs_3_.refs_5_, ...), custom_call_target="tpu_custom_call" | custom-call | flops 36238786560 | bytes 26476544 | tf_op jit(solution)/shard_map/coils/pallas_call | solution.py:463
  431.7 34.6 %all-to-all-done.2 = bf16[16,12,4,8,384]{4,3,2,1,0:T(8,128)(2,1)} async-done(((bf16[16,12,4,8,384]{4,3,2,1,0:T(8,128)(2,1)}), bf16[16,12,4,8,384]{4,3,2,1,0:T(8,128)(2,1)}, u32[]{:S(2)}, u32[]{:S(2)}) %all-to-all-start.2) | async-done | bytes 4718624 | tf_op jit(solution)/shard_map/all_to_all | solution.py:527
  466.3 4.9 all-to-all-start.3
  471.2 9.2 %coils.5.refs_9_ = f32[192,8,384]{2,1,0:T(8,128)} custom-call(bf16[192,4,8,384]{3,2,1,0:T(8,128)(2,1)} %bitcast.9.refs_0_.refs_2_, f32[192,16,384]{2,1,0:T(8,128)} %warp.1.refs_1_.refs_3_, f32[384,256]{1,0:T(8,128)} %pad_maximum_fusion.2.refs_2_.refs_4_, bf16[384,512]{1,0:T(8,128)(2,1)} %constant.87.clone.refs_3_.refs_5_, ...), custom_call_target="tpu_custom_call" | custom-call | flops 3623878656 | bytes 15859712 | tf_op jit(solution)/shard_map/coils/pallas_call | solution.py:463
  480.4 32.2 %coils.7 = bf16[192,8,384]{2,1,0:T(8,128)(2,1)} custom-call(s32[1152]{0:T(1024)} %reshape.31.links.refs_0_, s32[16]{0:T(128)} %fusion.10.owner.refs_1_, bf16[192,4,8,384]{3,2,1,0:T(8,128)(2,1)} %bitcast.9.refs_0_.refs_2_, f32[192,16,384]{2,1,0:T(8,128)} %warp.1.refs_1_.refs_3_, f32[384,256]{1,0:T(8,128)} %pad_maximum_fusion.2.refs_2_.refs_4_, ...), custom_call_target="tpu_custom_call" | custom-call | flops 10871635968 | bytes 18219008 | tf_op jit(solution)/shard_map/coils/pallas_call | solution.py:463
  512.6 11.6 %all-to-all-done.3 = bf16[16,12,2,8,384]{4,3,2,1,0:T(8,128)(2,1)S(1)} async-done(((bf16[16,12,2,8,384]{4,3,2,1,0:T(8,128)(2,1)}), bf16[16,12,2,8,384]{4,3,2,1,0:T(8,128)(2,1)S(1)}, u32[]{:S(2)}, u32[]{:S(2)}) %all-to-all-start.3) | async-done | bytes 2359328 | tf_op jit(solution)/shard_map/all_to_all | solution.py:527
  524.2 4.9 all-to-all-start.4
  529.1 26.4 %coils.6 = bf16[192,8,384]{2,1,0:T(8,128)(2,1)} custom-call(s32[1152]{0:T(1024)} %reshape.31.links.refs_0_, s32[16]{0:T(128)} %fusion.10.owner.refs_1_, bf16[192,2,8,384]{3,2,1,0:T(8,128)(2,1)S(1)} %bitcast.37, f32[192,16,384]{2,1,0:T(8,128)} %warp.1.refs_1_.refs_3_, f32[384,256]{1,0:T(8,128)} %pad_maximum_fusion.2.refs_2_.refs_4_, ...), custom_call_target="tpu_custom_call" | custom-call | flops 7247757312 | bytes 17039360 | tf_op jit(solution)/shard_map/coils/pallas_call | solution.py:463
  555.5 1.4 all-to-all-done.4.b_ref
  556.9 4.9 all-to-all-start.5
  561.8 3.3 update.2.refs_0_
  565.0 24.5 %all-to-all-done.5.b_ref = bf16[16,12,8,384]{3,2,1,0:T(8,128)(2,1)S(1)} async-done(((bf16[16,12,8,384]{3,2,1,0:T(8,128)(2,1)}), bf16[16,12,8,384]{3,2,1,0:T(8,128)(2,1)S(1)}, u32[]{:S(2)}, u32[]{:S(2)}) %all-to-all-start.5) | async-done | bytes 1179680 | tf_op jit(solution)/shard_map/all_to_all | solution.py:527
  589.5 3.3 update.3
  (6 shorter events, 0.1 us)
Async XLA Ops:
  10.3 82.9 %all-to-all-start = ((bf16[16,12,16,384]{3,2,1,0:T(8,128)(2,1)}), bf16[16,12,16,384]{3,2,1,0:T(8,128)(2,1)S(1)}, u32[]{:S(2)}, u32[]{:S(2)}) async-start(bf16[16,12,16,384]{3,2,1,0:T(8,128)(2,1)} %image_columns.1), calls=%async_computation | async-start | bytes 4718592 | tf_op jit(solution)/shard_map/all_to_all | solution.py:527
  19.0 4.8 copy-start.1
  24.0 69.1 %collective-permute-start = (bf16[2320,128]{1,0:T(8,128)(2,1)S(1)}, bf16[2320,128]{1,0:T(8,128)(2,1)S(1)}, u32[]{:S(2)}, u32[]{:S(2)}) collective-permute-start(bf16[2320,128]{1,0:T(8,128)(2,1)S(1)} %pad_maximum_fusion.1), channel_id=1, source_target_pairs={{0,8},{1,9},{2,10},{3,11},{4,12},{5,13},{6,14},{7,15},{8,0},{9,1},... | collective-permute-start | bytes 1781768 | tf_op jit(solution)/shard_map/ppermute | solution.py:537
  93.1 265.2 %all-to-all-start.1 = ((bf16[16,12,5,16,384]{4,3,2,1,0:T(8,128)(2,1)}), bf16[16,12,5,16,384]{4,3,2,1,0:T(8,128)(2,1)}, u32[]{:S(2)}, u32[]{:S(2)}) async-start(bf16[16,12,5,16,384]{4,3,2,1,0:T(8,128)(2,1)} %maps_columns.1), calls=%async_computation.1 | async-start | bytes 23592960 | tf_op jit(solution)/shard_map/all_to_all | solution.py:527
  101.8 166.3 %all-gather.2.cloned.1.call-start = ((), (), s32[]{:S(2)}) async-start(), calls=%async_computation.6 | async-start | bytes 10690560 | tf_op jit(solution)/shard_map/all_gather | solution.py:544
  358.4 4.6 copy-start
  358.4 107.9 %all-to-all-start.2 = ((bf16[16,12,4,8,384]{4,3,2,1,0:T(8,128)(2,1)}), bf16[16,12,4,8,384]{4,3,2,1,0:T(8,128)(2,1)}, u32[]{:S(2)}, u32[]{:S(2)}) async-start(bf16[16,12,4,8,384]{4,3,2,1,0:T(8,128)(2,1)} %get-tuple-element.15), calls=%async_computation.2 | async-start | bytes 9437184 | tf_op jit(solution)/shard_map/all_to_all | solution.py:527
  466.3 57.9 %all-to-all-start.3 = ((bf16[16,12,2,8,384]{4,3,2,1,0:T(8,128)(2,1)}), bf16[16,12,2,8,384]{4,3,2,1,0:T(8,128)(2,1)S(1)}, u32[]{:S(2)}, u32[]{:S(2)}) async-start(bf16[16,12,2,8,384]{4,3,2,1,0:T(8,128)(2,1)} %get-tuple-element.16), calls=%async_computation.3 | async-start | bytes 4718592 | tf_op jit(solution)/shard_map/all_to_all | solution.py:527
  524.2 32.7 %all-to-all-start.4 = ((bf16[16,12,8,384]{3,2,1,0:T(8,128)(2,1)}), bf16[16,12,8,384]{3,2,1,0:T(8,128)(2,1)S(1)}, u32[]{:S(2)}, u32[]{:S(2)}) async-start(bf16[16,12,8,384]{3,2,1,0:T(8,128)(2,1)} %bitcast.40), calls=%async_computation.4 | async-start | bytes 2359296 | tf_op jit(solution)/shard_map/all_to_all | solution.py:527
  556.9 32.6 %all-to-all-start.5 = ((bf16[16,12,8,384]{3,2,1,0:T(8,128)(2,1)}), bf16[16,12,8,384]{3,2,1,0:T(8,128)(2,1)S(1)}, u32[]{:S(2)}, u32[]{:S(2)}) async-start(bf16[16,12,8,384]{3,2,1,0:T(8,128)(2,1)} %bitcast.41), calls=%async_computation.5 | async-start | bytes 2359296 | tf_op jit(solution)/shard_map/all_to_all | solution.py:527
Sparse Core Ops, SparseCore 0:
  104.2 163.7 all-gather.1
